TPU v7x, 256 devices: a whole 4x4x8 slice. The times are simulated.
256 devices in a mesh: ctx: 64 (over z, y, core), ch: 4 (over x).
Axes of the slice: x: 4, y: 4, z: 8, core: 2. Of those that a mesh axis runs over, the one named last changes fastest.
Arguments:
- conv_input: bfloat16 [256, 128, 8192], P('ctx', None, 'ch'), may hold values from -6 to 6
- gate_signal: bfloat16 [256, 128, 8192], P('ctx', None, 'ch'), may hold values from -6 to 6
- cotangent: bfloat16 [256, 128, 8192], P('ctx', None, 'ch'), may hold values from -6 to 6
- filters: float32 [16, 1024], replicated
- tile_owner: int32 [192], replicated, may hold values from 0 to 63, as said below
- support: int32 [192, 8], replicated, may hold values from -1 to 191, as said below
Outputs:
- gate_grad: bfloat16 [256, 128, 8192], P('ctx', None, 'ch')
- input_grad: bfloat16 [256, 128, 8192], P('ctx', None, 'ch')
- filter_grad: float32 [16, 1024], replicated
Inputs may be any that keep to these rules, and one draw needn't show every extreme that they name: tile_owner never falls from one tile to the next; every index of ctx owns from 2 to 4 tiles, some index owns 3 + 1 and some index owns 3 - 1. support[t, k] is t - k where tile t - k belongs to the document of tile t and -1 otherwise; documents are runs of whole tiles, and some document spans 8 tiles or more.
All inputs are finite; a program needn't handle non-finite values.
Results may differ from a plain program's by a relative error of at most 0.0058.
Values may be sent and summed in bfloat16 or wider, within the bound.
No kernel may reach another device: no remote copies, remote signals or barrier semaphores. Data moves between devices by JAX's collectives and lax.ppermute only.
A program may use at most 256 MiB of HBM per device.

v0:
```python
import math

import jax
import jax.numpy as jnp
from jax import lax
from jax.sharding import PartitionSpec as P

GROUP = 128
REACH = 4


def passed_along(value, axis, steps):
    count = lax.axis_size(axis)
    leading, last = (max(0, -steps), min(count, count - steps))
    return lax.ppermute(value, axis, [(source, source + steps) for source in range(leading, last)])


def filter_blocks(filters, tile_rows, maxlag):
    narrow = filters.astype(jnp.bfloat16)
    row_ids = jnp.arange(tile_rows, dtype=jnp.int32)
    lag_offsets = (
        jnp.arange(maxlag, dtype=jnp.int32)[:, None, None] * tile_rows
        + row_ids[:, None]
        - row_ids[None, :]
    )
    picked = jnp.take(narrow, jnp.clip(lag_offsets, 0, filters.shape[1] - 1), axis=1)
    return jnp.where(lag_offsets[None] >= 0, picked, jnp.zeros_like(picked))


def lag_sums(square):
    filter_count, side_length = (square.shape[0], square.shape[1])
    flipped = square[:, :, ::-1]
    padded = jnp.pad(flipped, ((0, 0), (0, 0), (0, side_length)))
    skewed = padded.reshape(filter_count, 2 * side_length * side_length)[
        :, : side_length * (2 * side_length - 1)
    ]
    return jnp.sum(skewed.reshape(filter_count, side_length, 2 * side_length - 1), axis=1)


def spread_lags(squares, lag_count):
    maxlag, filter_count, side_length = (squares.shape[0], squares.shape[1], squares.shape[2])
    accumulated = jnp.zeros((filter_count, (maxlag + 1) * side_length), jnp.float32)
    for lag_index in range(maxlag):
        start_col = lag_index * side_length
        accumulated = accumulated.at[:, start_col : start_col + 2 * side_length - 1].add(
            lag_sums(squares[lag_index])
        )
    return accumulated[:, side_length - 1 : side_length - 1 + lag_count]


def per_device(conv_input, gate_signal, cotangent, filters, tile_owner, support):
    slot_count, tile_rows, channels = conv_input.shape
    maxlag = support.shape[1]
    filter_count, lag_count = filters.shape
    group_width = GROUP
    repeats = channels // (filter_count * group_width)
    total_tiles = tile_owner.shape[0]
    devices_ctx = lax.axis_size("ctx")
    myself = lax.axis_index("ctx")
    farthest = REACH
    devices = jnp.arange(devices_ctx, dtype=jnp.int32)
    counts = jnp.sum((tile_owner[None, :] == devices[:, None]).astype(jnp.int32), axis=1)
    starts = jnp.cumsum(counts) - counts
    slot_index = jnp.arange(slot_count, dtype=jnp.int32)
    own_tiles = starts[myself] + slot_index
    own_live = slot_index < counts[myself]
    own_safe = jnp.clip(own_tiles, 0, total_tiles - 1)
    sources = support[own_safe]
    present = own_live[:, None] & (sources >= 0)
    source_safe = jnp.clip(sources, 0, total_tiles - 1)
    holder = tile_owner[source_safe]
    within = source_safe - starts[holder]
    blocks = filter_blocks(filters, tile_rows, maxlag)
    zero_tile = jnp.zeros((), jnp.bfloat16)
    gathered = [conv_input]
    for distance in range(1, farthest + 1):
        gathered.append(passed_along(conv_input, "ctx", distance))
    window = jnp.concatenate(gathered, axis=0)
    rows_at = jnp.clip((myself - holder) * slot_count + within, 0, window.shape[0] - 1)
    selected = jnp.take(window, rows_at.reshape(-1), axis=0)
    selected = selected.reshape(slot_count, maxlag, tile_rows, channels)
    selected = jnp.where(present[:, :, None, None], selected, zero_tile)
    weighted = (gate_signal.astype(jnp.float32) * cotangent.astype(jnp.float32)).astype(
        jnp.bfloat16
    )
    weighted = jnp.where(own_live[:, None, None], weighted, zero_tile)
    weighted_shaped = weighted.reshape(slot_count, tile_rows, repeats, filter_count, group_width)
    conv_out = jnp.zeros((slot_count, tile_rows, channels), jnp.float32)
    squares = []
    for lag_index in range(maxlag):
        shaped = selected[:, lag_index].reshape(
            slot_count, tile_rows, repeats, filter_count, group_width
        )
        product = jnp.einsum(
            "fij,sjrfc->sirfc", blocks[:, lag_index], shaped, preferred_element_type=jnp.float32
        )
        conv_out = conv_out + product.reshape(slot_count, tile_rows, channels)
        squares.append(
            jnp.einsum(
                "sirfc,sjrfc->fij", weighted_shaped, shaped, preferred_element_type=jnp.float32
            )
        )
    gate_grad = (cotangent.astype(jnp.float32) * conv_out).astype(jnp.bfloat16)
    norm_factor = 1.0 / math.sqrt(
        total_tiles * tile_rows * channels * lax.axis_size("ch") / filter_count
    )
    local_filters = spread_lags(jnp.stack(squares), lag_count)
    filter_grad = lax.psum(local_filters, ("ctx", "ch")) * norm_factor
    row_count = (farthest + 1) * slot_count
    partial_value = jnp.zeros((row_count, tile_rows, channels), jnp.float32)
    back_rows = jnp.clip((myself - holder) * slot_count + within, 0, row_count - 1)
    for lag_index in range(maxlag):
        adjoint_term = jnp.einsum(
            "fji,sjrfc->sirfc",
            blocks[:, lag_index],
            weighted_shaped,
            preferred_element_type=jnp.float32,
        )
        adjoint_term = jnp.where(present[:, lag_index, None, None, None, None], adjoint_term, 0.0)
        partial_value = partial_value.at[back_rows[:, lag_index]].add(
            adjoint_term.reshape(slot_count, tile_rows, channels)
        )
    adjoint = partial_value[:slot_count]
    for distance in range(1, farthest + 1):
        adjoint = adjoint + passed_along(
            partial_value[distance * slot_count : (distance + 1) * slot_count], "ctx", -distance
        )
    input_grad = adjoint.astype(jnp.bfloat16)
    return (gate_grad, input_grad, filter_grad)


def solution(mesh):
    return jax.shard_map(
        per_device,
        mesh=mesh,
        in_specs=(P("ctx", None, "ch"), P("ctx", None, "ch"), P("ctx", None, "ch"), P(), P(), P()),
        out_specs=(P("ctx", None, "ch"), P("ctx", None, "ch"), P()),
        check_vma=False,
    )
```

profile of v0, /device:TPU:1, one launch (start us, length us, event | category | flops | bytes accessed | tf_op | source)
XLA Modules:
  0.0 1288.6 jit_solution(6269767289445348876)
XLA Ops:
  32.1 454.0 %gather_fusion.4 = bf16[131072,16]{1,0:T(8,128)(2,1)} fusion(bf16[16,1024]{0,1:T(8,128)(2,1)S(1)} %copy.164, s32[131072]{0:T(1024)S(1)} %broadcast_clamp_fusion), kind=kCustom, calls=%fused_computation.4 | custom fusion | bytes 8912896 | tf_op jit(solution)/shard_map/jit(_take)/gather | solution.py:26
  486.1 29.2 %copy.166 = bf16[8,128,128,16]{2,1,3,0:T(8,128)(2,1)} copy(bf16[8,128,128,16]{3,2,1,0:T(8,128)(2,1)} %bitcast.207) | data formatting | bytes 8388608 | tf_op jit(solution)/shard_map/jit(_take)/gather | solution.py:26
  623.9 9.7 broadcast_in_dim.155
  633.6 9.0 scatter_fusion
  642.5 9.0 scatter_fusion.1
  651.6 9.0 scatter_fusion.2
  660.6 9.0 scatter_fusion.3
  669.6 8.7 scatter_fusion.4
  678.3 8.6 scatter_fusion.5
  686.9 8.3 scatter_fusion.6
  695.1 8.3 scatter_fusion.7
  703.4 12.2 fusion.52
  742.8 11.4 gather_fusion.3
  754.2 8.7 select_select_fusion
  762.9 5.9 fusion.53
  836.1 11.8 add_bitcast_fusion
  850.1 9.3 rev.24
  863.5 6.2 reshape.668
  872.1 9.3 rev.25
  885.6 6.2 reshape.670
  893.5 6.0 rev.26
  903.6 6.2 reshape.672
  913.9 5.8 rev.27
  923.8 6.2 reshape.674
  934.1 6.0 rev.28
  944.3 6.2 reshape.676
  964.5 6.2 reshape.678
  974.8 6.1 rev.30
  985.0 6.2 reshape.680
  1005.2 6.3 reshape.682
  1028.9 240.6 %all-reduce.11.cloned.1.call-done = f32[16,1024]{1,0:T(8,128)} async-done(((f32[16,1024]{1,0:T(8,128)}), f32[16,1024]{1,0:T(8,128)}) %all-reduce.11.cloned.1.call-update) | async-done | bytes 65552 | tf_op jit(solution)/shard_map/psum | solution.py:108
  1270.9 10.4 fusion.5
  (190 shorter events, 317.9 us)
Async XLA Ops:
  7.2 24.7 %copy-start.7 = (f32[16,1024]{1,0:T(8,128)S(1)}, f32[16,1024]{1,0:T(8,128)}, u32[]{:S(2)}) copy-start(f32[16,1024]{1,0:T(8,128)} %param.25) | copy-start | bytes 196612
  7.2 1262.3 %all-reduce.11.cloned.1.call-start = ((), (), s32[]{:S(2)}) async-start(), calls=%async_computation | async-start | bytes 131072 | tf_op jit(solution)/shard_map/psum | solution.py:108
  7.2 718.4 %collective-permute-start = (bf16[4,128,2048]{2,1,0:T(8,128)(2,1)}, bf16[4,128,2048]{2,1,0:T(8,128)(2,1)}, u32[]{:S(2)}, u32[]{:S(2)}) collective-permute-start(bf16[4,128,2048]{2,1,0:T(8,128)(2,1)} %param.22), channel_id=1, source_target_pairs={{0,4},{4,8},{8,12},{12,16},{16,20},{20,24},{24,28},{28,32},{32,36}... | collective-permute-start | bytes 6291464 | tf_op jit(solution)/shard_map/ppermute | solution.py:15
  11.8 718.2 %collective-permute-start.1 = (bf16[4,128,2048]{2,1,0:T(8,128)(2,1)}, bf16[4,128,2048]{2,1,0:T(8,128)(2,1)}, u32[]{:S(2)}, u32[]{:S(2)}) collective-permute-start(bf16[4,128,2048]{2,1,0:T(8,128)(2,1)} %param.22), channel_id=1, source_target_pairs={{0,8},{4,12},{8,16},{12,20},{16,24},{20,28},{24,32},{28,36},{32,40... | collective-permute-start | bytes 6291464 | tf_op jit(solution)/shard_map/ppermute | solution.py:15
  16.3 718.2 %collective-permute-start.2 = (bf16[4,128,2048]{2,1,0:T(8,128)(2,1)}, bf16[4,128,2048]{2,1,0:T(8,128)(2,1)}, u32[]{:S(2)}, u32[]{:S(2)}) collective-permute-start(bf16[4,128,2048]{2,1,0:T(8,128)(2,1)} %param.22), channel_id=1, source_target_pairs={{0,12},{4,16},{8,20},{12,24},{16,28},{20,32},{24,36},{28,40},{32,4... | collective-permute-start | bytes 6291464 | tf_op jit(solution)/shard_map/ppermute | solution.py:15
  19.9 719.7 %collective-permute-start.3 = (bf16[4,128,2048]{2,1,0:T(8,128)(2,1)}, bf16[4,128,2048]{2,1,0:T(8,128)(2,1)}, u32[]{:S(2)}, u32[]{:S(2)}) collective-permute-start(bf16[4,128,2048]{2,1,0:T(8,128)(2,1)} %param.22), channel_id=1, source_target_pairs={{0,16},{4,20},{8,24},{12,28},{16,32},{20,36},{24,40},{28,44},{32,4... | collective-permute-start | bytes 6291464 | tf_op jit(solution)/shard_map/ppermute | solution.py:15
  486.1 29.2 %copy-start.6 = (bf16[4,128,2048]{2,1,0:T(8,128)(2,1)S(1)}, bf16[4,128,2048]{2,1,0:T(8,128)(2,1)}, u32[]{:S(2)}) copy-start(bf16[4,128,2048]{2,1,0:T(8,128)(2,1)} %param.24) | copy-start | bytes 6291460
  522.1 3.4 copy-start.5
  526.1 16.7 %copy-start = (bf16[16,8,128,128]{3,2,0,1:T(8,128)(2,1)}, bf16[16,8,128,128]{3,2,0,1:T(8,128)(2,1)S(1)}, u32[]{:S(2)}) copy-start(bf16[16,8,128,128]{3,2,0,1:T(8,128)(2,1)S(1)} %select_bitcast_fusion) | copy-start | bytes 12582916
  715.7 555.3 %collective-permute-start.7 = (f32[4,128,2048]{2,1,0:T(8,128)}, f32[4,128,2048]{2,1,0:T(8,128)}, u32[]{:S(2)}, u32[]{:S(2)}) collective-permute-start(f32[4,128,2048]{2,1,0:T(8,128)} %get-tuple-element.127), channel_id=1, source_target_pairs={{16,0},{20,4},{24,8},{28,12},{32,16},{36,20},{40,24},{44,28},{48,3... | collective-permute-start | bytes 12582920 | tf_op jit(solution)/shard_map/ppermute | solution.py:15
  725.6 545.3 %collective-permute-start.6 = (f32[4,128,2048]{2,1,0:T(8,128)}, f32[4,128,2048]{2,1,0:T(8,128)}, u32[]{:S(2)}, u32[]{:S(2)}) collective-permute-start(f32[4,128,2048]{2,1,0:T(8,128)} %get-tuple-element.128), channel_id=1, source_target_pairs={{12,0},{16,4},{20,8},{24,12},{28,16},{32,20},{36,24},{40,28},{44,3... | collective-permute-start | bytes 12582920 | tf_op jit(solution)/shard_map/ppermute | solution.py:15
  730.0 540.9 %collective-permute-start.5 = (f32[4,128,2048]{2,1,0:T(8,128)}, f32[4,128,2048]{2,1,0:T(8,128)}, u32[]{:S(2)}, u32[]{:S(2)}) collective-permute-start(f32[4,128,2048]{2,1,0:T(8,128)} %get-tuple-element.129), channel_id=1, source_target_pairs={{8,0},{12,4},{16,8},{20,12},{24,16},{28,20},{32,24},{36,28},{40,32... | collective-permute-start | bytes 12582920 | tf_op jit(solution)/shard_map/ppermute | solution.py:15
  734.5 536.4 %collective-permute-start.4 = (f32[4,128,2048]{2,1,0:T(8,128)}, f32[4,128,2048]{2,1,0:T(8,128)}, u32[]{:S(2)}, u32[]{:S(2)}) collective-permute-start(f32[4,128,2048]{2,1,0:T(8,128)} %get-tuple-element.126), channel_id=1, source_target_pairs={{4,0},{8,4},{12,8},{16,12},{20,16},{24,20},{28,24},{32,28},{36,32}... | collective-permute-start | bytes 12582920 | tf_op jit(solution)/shard_map/ppermute | solution.py:15
  772.8 4.5 copy-start.2
  783.0 4.5 copy-start.3
  793.2 4.5 copy-start.4
  1005.2 15.8 %copy-start.1 = (bf16[4,128,2048]{1,2,0:T(8,128)(2,1)S(1)}, bf16[4,128,2048]{1,2,0:T(8,128)(2,1)}, u32[]{:S(2)}) copy-start(bf16[4,128,2048]{1,2,0:T(8,128)(2,1)} %copy.160) | copy-start | bytes 6291460
Sparse Core Ops, SparseCore 0:
  1021.1 248.2 all-reduce.10
where the time goes:
time: 1300 us; the launch traced here: 1290 us
  local copies, waits for them, and re-layouts  807 us (62%)
  waiting for transfers between devices  241 us (19%)
  other arithmetic  126 us (10%)
  matrix products  78 us (6%)
  starting transfers between devices  22.1 us (2%)
  between operations  15.1 us (1%)
    gather x2, local copies, waits for them, and re-layouts, filter_blocks(): jnp.take(narrow, jnp.clip(lag_offsets, 0, filters.shape[1] - 1), axis=1)  483 us
    psum x1, waiting for transfers between devices, per_device(): filter_grad = lax.psum(local_filters, ('ctx', 'ch')) * norm_factor  241 us
    scatter-add x8, other arithmetic, per_device(): partial_value.at[back_rows[:, lag_index]]  69.9 us
    rev x8, local copies, waits for them, and re-layouts, lag_sums(): flipped = square[:, :, ::-1]  54.3 us
    reshape x8, local copies, waits for them, and re-layouts, lag_sums(): skewed.reshape(filter_count, side_length, 2 * side_length - 1)  49.4 us
    reshape x8, local copies, waits for them, and re-layouts, per_device(): adjoint_term.reshape(slot_count, tile_rows, channels)  43.4 us
    dot_general x8, matrix products, per_device(): jnp.einsum('fij,sjrfc->sirfc', blocks[:, lag_index], shaped, preferred_el...  42.7 us
    slice x9, local copies, waits for them, and re-layouts, per_device(): selected[:, lag_index]  37.9 us
  transfers between devices with their start and end apart: 9, of which 1 were waited for; matrix products, arithmetic and copies ran while one was open for 78% of the time, Pallas kernels for 0%

commit v1 on v0

v1 whole, which is shorter than its diff:
```python
import functools
import math

import jax
import jax.numpy as jnp
from jax import lax
from jax.experimental import pallas as pl
from jax.experimental.pallas import tpu as pltpu
from jax.sharding import PartitionSpec as P

GROUP = 128
NEAR = 4
BF = jnp.bfloat16
F32 = jnp.float32
VMEM_LIMIT = 60 * 1024 * 1024


def params():
    return pltpu.CompilerParams(vmem_limit_bytes=VMEM_LIMIT)


def shifted(value, axis, steps):
    count = lax.axis_size(axis)
    pairs = [(a, a + steps) for a in range(max(0, -steps), min(count, count - steps))]
    return lax.ppermute(value, axis, pairs)


def swapped(value, axis, mask):
    count = lax.axis_size(axis)
    return lax.ppermute(value, axis, [(a, a ^ mask) for a in range(count)])


def chip_meta(meta):
    first, second, end, core = meta[0], meta[1], meta[2], meta[3]
    return first, second - first, end - first, core


def place(meta, index):
    _, low, _, core = chip_meta(meta)
    on_second = (index >= low).astype(jnp.int32)
    slot = jnp.clip(index - on_second * low, 0, 3)
    return on_second == core, slot


def prep_body(meta, gate, cot, x, w_out, send_out, cot_out):
    half = cot.shape[2] // 2
    w = (gate[0].astype(F32) * cot[0].astype(F32)).astype(BF)
    w_out[0] = w
    other = pl.ds(pl.multiple_of((1 - meta[3]) * half, half), half)
    send_out[0, 0] = x[0, :, other]
    send_out[1, 0] = w_out[0, :, other]
    cot_out[0] = cot[0, :, other]


def prep(meta, gate, cot, x):
    slots, rows, width = x.shape
    half = width // 2
    full = pl.BlockSpec((1, rows, width), lambda s, m: (s, 0, 0))
    return pl.pallas_call(
        prep_body,
        grid_spec=pltpu.PrefetchScalarGridSpec(
            num_scalar_prefetch=1,
            grid=(slots,),
            in_specs=[full, full, full],
            out_specs=[
                full,
                pl.BlockSpec((2, 1, rows, half), lambda s, m: (0, s, 0, 0)),
                pl.BlockSpec((1, rows, half), lambda s, m: (s, 0, 0)),
            ],
        ),
        out_shape=[
            jax.ShapeDtypeStruct(x.shape, BF),
            jax.ShapeDtypeStruct((2, slots, rows, half), BF),
            jax.ShapeDtypeStruct((slots, rows, half), BF),
        ],
        compiler_params=params(),
        name="prep",
    )(meta, gate, cot, x)


def pack_body(x_index, w_index, far, meta, xm, xt, wm, wt, *rest):
    if far:
        xh, wh, x_out, w_out = rest
    else:
        x_out, w_out = rest
    step = pl.program_id(0)
    _, _, count, _ = chip_meta(meta)
    xi = x_index(step, count)
    mine, _ = place(meta, xi)
    value = jnp.where(mine, xm[0], xt[0, 0])
    if far:
        value = jnp.where(xi < 0, xh[0], value)
    x_out[0] = value
    wi = w_index(step, count)
    mine, _ = place(meta, wi)
    value = jnp.where(mine, wm[0], wt[0, 0])
    if far:
        value = jnp.where(wi >= count, wh[0], value)
    w_out[0] = value


def pack(meta, x, w, theirs, tiles, x_index, w_index, x_halo=None, w_halo=None):
    slots, rows, width = x.shape
    half = width // 2
    far = x_halo is not None

    def own(index):
        def at(s, m):
            return (place(m, index(s, m[2] - m[0]))[1], 0, m[3])

        return pl.BlockSpec((1, rows, half), at)

    def other(which, index):
        def at(s, m):
            return (which, place(m, index(s, m[2] - m[0]))[1], 0, 0)

        return pl.BlockSpec((1, 1, rows, half), at)

    specs = [own(x_index), other(0, x_index), own(w_index), other(1, w_index)]
    args = [x, theirs, w, theirs]
    if far:
        specs += [
            pl.BlockSpec((1, rows, half), lambda s, m: (jnp.clip(x_index(s, m[2] - m[0]) + NEAR, 0, NEAR - 1), 0, 0)),
            pl.BlockSpec((1, rows, half), lambda s, m: (jnp.clip(w_index(s, m[2] - m[0]) - (m[2] - m[0]), 0, NEAR - 1), 0, 0)),
        ]
        args += [x_halo, w_halo]
    out = pl.BlockSpec((1, rows, half), lambda s, m: (s, 0, 0))
    return pl.pallas_call(
        functools.partial(pack_body, x_index, w_index, far),
        grid_spec=pltpu.PrefetchScalarGridSpec(
            num_scalar_prefetch=1, grid=(tiles,), in_specs=specs, out_specs=[out, out]
        ),
        out_shape=[jax.ShapeDtypeStruct((tiles, rows, half), BF)] * 2,
        compiler_params=params(),
        name="pack",
    )(meta, *args)


def readers_of(sup, tile, total, lags):
    found = jnp.int32(0)
    for lag in range(lags):
        at = jnp.clip(tile + lag, 0, total - 1)
        live = (tile >= 0) & (tile + lag < total) & (sup[at, lag] >= 0)
        found += live.astype(jnp.int32)
    return found


def sources_of(sup, tile, total, lags):
    at = jnp.clip(tile, 0, total - 1)
    found = jnp.int32(0)
    for lag in range(lags):
        found += (sup[at, lag] >= 0).astype(jnp.int32)
    return found


def column_mask(width, low, high):
    lane = lax.broadcasted_iota(jnp.int32, (16, width), 1)
    return jnp.where((lane >= low) & (lane < high), 1.0, 0.0).astype(BF)


def masked(value, mask):
    rows, width = value.shape
    return (value.reshape(rows // 16, 16, width) * mask[None]).reshape(rows, width)


def dot(a, b):
    return jnp.dot(a, b, preferred_element_type=F32)


def dot_nt(a, b):
    return lax.dot_general(a, b, (((1,), (1,)), ((), ())), preferred_element_type=F32)


def reversal(rows):
    r = lax.broadcasted_iota(jnp.int32, (rows, rows), 0)
    c = lax.broadcasted_iota(jnp.int32, (rows, rows), 1)
    return jnp.where(r + c == rows - 1, 1.0, 0.0).astype(BF)


def diagonal_sums(square):
    rows, width = square.shape
    padded = jnp.concatenate([square, jnp.zeros((rows, rows), F32)], axis=1)
    skewed = pltpu.roll(padded, 0, 1, stride=1, stride_axis=0)
    total = jnp.sum(skewed, axis=0, keepdims=True)
    total = pltpu.roll(jnp.broadcast_to(total, (8, width + rows)), width + 1, 1)
    return total[:1, :width]


def pick(mine, theirs, meta, index):
    own, slot = place(meta, index)
    return jnp.where(own, mine[slot], theirs[slot])


def own_body(lags, total, meta, sup, filt, flip, x, xt, w, wt,
             conv_out, adj_out, sums_out, fwd_out, bwd_out, xs, xl, ws, wl, masks, reach):
    group = pl.program_id(0)
    rows = xs.shape[1]
    cap = xs.shape[0]
    first, _, count, _ = chip_meta(meta)

    @pl.when(group == 0)
    def _():
        for s in range(cap):
            reach[s] = jnp.minimum(readers_of(sup, first + s, total, lags), count - s)
            reach[cap + s] = sources_of(sup, first + s, total, lags)
        for k in range(lags):
            for s in range(cap):
                live = jnp.where(k < reach[s], 1.0, 0.0)
                masks[k, :, s * rows : (s + 1) * rows] = jnp.full((16, rows), live, F32).astype(BF)

    taps = filt[pl.ds(group, 1), :].astype(BF).astype(F32)
    width = taps.shape[1]
    pad = jnp.zeros((1, rows), F32)
    spread = jnp.broadcast_to(jnp.concatenate([taps, pad], axis=1), (rows, width + rows))
    bwd_out[0] = pltpu.roll(spread, 0, 1, stride=1, stride_axis=0)[:, :width].astype(BF)
    taps = flip[pl.ds(group, 1), :].astype(BF).astype(F32)
    spread = jnp.broadcast_to(jnp.concatenate([taps, pad], axis=1), (rows, width + rows))
    fwd_out[0] = pltpu.roll(spread, width + 1, 1, stride=1, stride_axis=0)[:, :width].astype(BF)

    for s in range(cap):
        tile = pick(x, xt.at[0], meta, s)
        xs[s] = tile
        xl[:, s * rows : (s + 1) * rows] = tile
        tile = pick(w, wt.at[0], meta, s)
        ws[s] = tile
        wl[:, s * rows : (s + 1) * rows] = tile
    for i in range(cap):
        near = column_mask(width, (lags - reach[cap + i]) * rows, width)[:, (lags - 1 - i) * rows :]
        left = masked(fwd_out[0, :, (lags - 1 - i) * rows :], near)
        conv_out[i] = dot(left, xs[0 : i + 1].reshape((i + 1) * rows, rows))
    for s in range(cap):
        size = (cap - s) * rows
        left = masked(bwd_out[0, :, :size], column_mask(size, 0, reach[s] * rows))
        adj_out[s] = dot(left, ws[s:cap].reshape(size, rows))
    turned = dot(reversal(rows), xl[...]).astype(BF)
    squares = []
    for k in range(lags):
        size = (cap - k) * rows
        left = masked(turned[:, :size], masks[k, :, :size])
        squares.append(dot_nt(left, wl[:, k * rows :]))
    sums_out[pl.ds(group, 1), :] = diagonal_sums(jnp.concatenate(squares, axis=1))


def own_pairs(meta, sup, filt, flip, x, w, theirs, lags):
    slots, rows, width = x.shape
    half = width // 2
    groups = half // GROUP
    total = sup.shape[0]
    taps = filt.shape[1]
    cap = 2 * slots

    def lane(g, m, s):
        return (0, 0, m[3] * groups + g)

    in_specs = [
        pl.BlockSpec((groups, taps), lambda g, m, s: (m[3], 0)),
        pl.BlockSpec((groups, taps), lambda g, m, s: (m[3], 0)),
        pl.BlockSpec((slots, rows, GROUP), lane),
        pl.BlockSpec((1, slots, rows, GROUP), lambda g, m, s: (0, 0, 0, g)),
        pl.BlockSpec((slots, rows, GROUP), lane),
        pl.BlockSpec((1, slots, rows, GROUP), lambda g, m, s: (1, 0, 0, g)),
    ]
    tiles = pl.BlockSpec((cap, rows, GROUP), lambda g, m, s: (0, 0, g))
    bands = pl.BlockSpec((1, rows, taps), lambda g, m, s: (g, 0, 0))
    return pl.pallas_call(
        functools.partial(own_body, lags, total),
        grid_spec=pltpu.PrefetchScalarGridSpec(
            num_scalar_prefetch=2,
            grid=(groups,),
            in_specs=in_specs,
            out_specs=[tiles, tiles, pl.BlockSpec((groups, taps), lambda g, m, s: (0, 0)), bands, bands],
            scratch_shapes=[
                pltpu.VMEM((cap, rows, GROUP), BF),
                pltpu.VMEM((rows, cap * GROUP), BF),
                pltpu.VMEM((cap, rows, GROUP), BF),
                pltpu.VMEM((rows, cap * GROUP), BF),
                pltpu.VMEM((lags, 16, cap * GROUP), BF),
                pltpu.SMEM((2 * cap,), jnp.int32),
            ],
        ),
        out_shape=[
            jax.ShapeDtypeStruct((cap, rows, half), F32),
            jax.ShapeDtypeStruct((cap, rows, half), F32),
            jax.ShapeDtypeStruct((groups, taps), F32),
            jax.ShapeDtypeStruct((groups, rows, taps), BF),
            jax.ShapeDtypeStruct((groups, rows, taps), BF),
        ],
        compiler_params=params(),
        cost_estimate=pl.CostEstimate(flops=8_000_000_000, bytes_accessed=16 << 20, transcendentals=0),
        name="own_pairs",
    )(meta, sup, filt, flip, x, theirs, w, theirs)


def cross_body(lags, total, meta, sup, prior, x, xt, w, wt, xh, wh, sums_out, xl, wl, masks):
    group = pl.program_id(0)
    rows = xl.shape[0]
    spots = xl.shape[1] // rows
    cap = spots - NEAR
    first, _, count, _ = chip_meta(meta)

    @pl.when(group == 0)
    def _():
        for p in range(spots):
            s = p - NEAR
            found = readers_of(sup, first + s, total, lags)
            deep = s <= count - NEAR - 1
            for k in range(lags):
                t = s + k
                if s < 0:
                    live = (t >= 0) & (deep | (t < count))
                else:
                    live = deep & (t >= count)
                live = live & (k < found)
                masks[k, :, p * rows : (p + 1) * rows] = jnp.full((16, rows), jnp.where(live, 1.0, 0.0), F32).astype(BF)

    for p in range(NEAR):
        xl[:, p * rows : (p + 1) * rows] = xh[p]
    for s in range(cap):
        xl[:, (s + NEAR) * rows : (s + NEAR + 1) * rows] = pick(x, xt.at[0], meta, s)
    for t in range(spots):
        own = pick(w, wt.at[0], meta, t)
        wl[:, t * rows : (t + 1) * rows] = jnp.where(t < count, own, wh[jnp.clip(t - count, 0, NEAR - 1)])
    turned = dot(reversal(rows), xl[...]).astype(BF)
    squares = []
    for k in range(lags):
        low, high = max(0, NEAR - k), min(spots, spots + NEAR - k)
        left = masked(turned[:, low * rows : high * rows], masks[k, :, low * rows : high * rows])
        squares.append(dot_nt(left, wl[:, (low - NEAR + k) * rows : (high - NEAR + k) * rows]))
    row = pl.ds(group, 1)
    sums_out[row, :] = prior[row, :] + diagonal_sums(jnp.concatenate(squares, axis=1))


def cross_squares(meta, sup, prior, x, w, theirs, x_halo, w_halo, lags):
    slots, rows, width = x.shape
    half = width // 2
    groups = half // GROUP
    taps = prior.shape[1]
    spots = 2 * slots + NEAR

    def lane(g, m, s):
        return (0, 0, m[3] * groups + g)

    halo = pl.BlockSpec((NEAR, rows, GROUP), lambda g, m, s: (0, 0, g))
    whole = pl.BlockSpec((groups, taps), lambda g, m, s: (0, 0))
    return pl.pallas_call(
        functools.partial(cross_body, lags, sup.shape[0]),
        grid_spec=pltpu.PrefetchScalarGridSpec(
            num_scalar_prefetch=2,
            grid=(groups,),
            in_specs=[
                whole,
                pl.BlockSpec((slots, rows, GROUP), lane),
                pl.BlockSpec((1, slots, rows, GROUP), lambda g, m, s: (0, 0, 0, g)),
                pl.BlockSpec((slots, rows, GROUP), lane),
                pl.BlockSpec((1, slots, rows, GROUP), lambda g, m, s: (1, 0, 0, g)),
                halo,
                halo,
            ],
            out_specs=whole,
            scratch_shapes=[
                pltpu.VMEM((rows, spots * GROUP), BF),
                pltpu.VMEM((rows, spots * GROUP), BF),
                pltpu.VMEM((lags, 16, spots * GROUP), BF),
            ],
        ),
        out_shape=jax.ShapeDtypeStruct((groups, taps), F32),
        compiler_params=params(),
        cost_estimate=pl.CostEstimate(flops=3_000_000_000, bytes_accessed=6 << 20, transcendentals=0),
        name="cross_squares",
    )(meta, sup, prior, x, theirs, w, theirs, x_halo, w_halo)


def last_body(lags, total, slots, meta, sup, conv, adj, fwd, bwd, xn, xf, wn, wf, cot, cot_t,
              gate_out, input_out, send_out, xs, ws, reach):
    group = pl.program_id(0)
    rows = conv.shape[1]
    cap = 2 * slots
    first, low, count, core = chip_meta(meta)
    far = lags - 1 - NEAR

    @pl.when(group == 0)
    def _():
        for i in range(lags - 1):
            reach[i] = sources_of(sup, first + i, total, lags)
            reach[lags + i] = readers_of(sup, first + count - 1 - i, total, lags)

    xs[0:far] = xf[...]
    xs[far : lags - 1] = xn[...]
    ws[0:NEAR] = wn[...]
    ws[NEAR : lags - 1] = wf[...]
    for i in range(lags - 1):
        size = (lags - 1 - i) * rows
        mask = column_mask(size, (lags - reach[i]) * rows, lags * rows)
        conv[i] += dot(masked(fwd[0, :, :size], mask), xs[i : lags - 1].reshape(size, rows))
    for c in range(lags - 1):
        s = count - 1 - c
        size = (lags - 1 - c) * rows
        mask = column_mask(size, 0, (reach[lags + c] - 1 - c) * rows)
        term = dot(masked(bwd[0, :, (c + 1) * rows :], mask), ws[0 : lags - 1 - c].reshape(size, rows))

        @pl.when(s >= 0)
        def _():
            adj[jnp.maximum(s, 0)] += term

    high = count - low
    for slot in range(slots):
        for own in (True, False):
            second = core if own else 1 - core
            index = jnp.minimum(slot + second * low, cap - 1)
            live = slot < jnp.where(second == 1, high, low)
            cot_tile = (cot if own else cot_t)[slot]
            grad = jnp.where(live, cot_tile.astype(F32) * conv[index], 0.0).astype(BF)
            back = jnp.where(live, adj[index], 0.0).astype(BF)
            if own:
                gate_out[slot] = grad
                input_out[slot] = back
            else:
                send_out[0, slot] = grad
                send_out[1, slot] = back


def last_pairs(meta, sup, conv, adj, fwd, bwd, xn, xf, wn, wf, cot, cot_theirs, lags):
    slots, rows, width = cot.shape
    half = width // 2
    groups = half // GROUP
    taps = fwd.shape[2]
    far = lags - 1 - NEAR

    def lane(g, m, s):
        return (0, 0, m[3] * groups + g)

    def plain(tiles):
        return pl.BlockSpec((tiles, rows, GROUP), lambda g, m, s: (0, 0, g))

    bands = pl.BlockSpec((1, rows, taps), lambda g, m, s: (g, 0, 0))
    own = pl.BlockSpec((slots, rows, GROUP), lane)
    return pl.pallas_call(
        functools.partial(last_body, lags, sup.shape[0], slots),
        grid_spec=pltpu.PrefetchScalarGridSpec(
            num_scalar_prefetch=2,
            grid=(groups,),
            in_specs=[
                plain(2 * slots),
                plain(2 * slots),
                bands,
                bands,
                plain(NEAR),
                plain(far),
                plain(NEAR),
                plain(far),
                own,
                plain(slots),
            ],
            out_specs=[own, own, pl.BlockSpec((2, slots, rows, GROUP), lambda g, m, s: (0, 0, 0, g))],
            scratch_shapes=[
                pltpu.VMEM((lags - 1, rows, GROUP), BF),
                pltpu.VMEM((lags - 1, rows, GROUP), BF),
                pltpu.SMEM((2 * lags,), jnp.int32),
            ],
        ),
        out_shape=[
            jax.ShapeDtypeStruct(cot.shape, BF),
            jax.ShapeDtypeStruct(cot.shape, BF),
            jax.ShapeDtypeStruct((2, slots, rows, half), BF),
        ],
        compiler_params=params(),
        cost_estimate=pl.CostEstimate(flops=4_000_000_000, bytes_accessed=20 << 20, transcendentals=0),
        name="last_pairs",
    )(meta, sup, conv, adj, fwd, bwd, xn, xf, wn, wf, cot, cot_theirs)


def join(meta, gate, inp, got):
    slots, rows, width = gate.shape
    half = width // 2
    blank = pl.BlockSpec(memory_space=pl.ANY)
    out = pl.BlockSpec((1, rows, half), lambda s, m: (s, 0, 1 - m[3]))
    return pl.pallas_call(
        join_body_blocks,
        grid_spec=pltpu.PrefetchScalarGridSpec(
            num_scalar_prefetch=1,
            grid=(slots,),
            in_specs=[blank, blank, pl.BlockSpec((2, 1, rows, half), lambda s, m: (0, s, 0, 0))],
            out_specs=[out, out],
        ),
        out_shape=[jax.ShapeDtypeStruct(gate.shape, BF)] * 2,
        input_output_aliases={1: 0, 2: 1},
        compiler_params=params(),
        name="join",
    )(meta, gate, inp, got)


def join_body_blocks(meta, gate_in, input_in, got, gate_out, input_out):
    gate_out[0] = got[0, 0]
    input_out[0] = got[1, 0]


def per_device(conv_input, gate_signal, cotangent, filters, tile_owner, support):
    slots, rows, width = conv_input.shape
    lags = support.shape[1]
    filter_count, taps = filters.shape
    total = tile_owner.shape[0]
    me = lax.axis_index("ctx")
    core = me % 2
    entry = jnp.arange(8, dtype=jnp.int32)
    before = jnp.sum((tile_owner[None, :] < (me - core + entry)[:, None]).astype(jnp.int32), axis=1)
    meta = jnp.where(entry == 3, core, before)
    far = lags - 1 - NEAR

    w, send, cot_send = prep(meta, gate_signal, cotangent, conv_input)
    theirs = swapped(send, "ctx", 1)
    xs, ws = pack(meta, conv_input, w, theirs, NEAR, lambda s, n: n - NEAR + s, lambda s, n: s)
    xn = shifted(xs, "ctx", 2)
    wn = shifted(ws, "ctx", -2)
    cot_theirs = swapped(cot_send, "ctx", 1)
    conv, adj, sums, fwd, bwd = own_pairs(
        meta, support, filters, filters[:, ::-1], conv_input, w, theirs, lags
    )
    xn, wn, conv, adj, sums = lax.optimization_barrier((xn, wn, conv, adj, sums))
    xs, ws = pack(
        meta, conv_input, w, theirs, far, lambda s, n: n - NEAR - far + s, lambda s, n: NEAR + s, xn, wn
    )
    xf = shifted(xs, "ctx", 2)
    wf = shifted(ws, "ctx", -2)
    sums = cross_squares(meta, support, sums, conv_input, w, theirs, xn, wn, lags)
    xf, wf, sums = lax.optimization_barrier((xf, wf, sums))
    for mask in (2, 4, 8, 16, 32):
        sums = sums + swapped(sums, "ctx", mask)
    for mask in (1, 2):
        sums = sums + swapped(sums, "ch", mask)
    gate, inp, back = last_pairs(
        meta, support, conv, adj, fwd, bwd, xn, xf, wn, wf, cotangent, cot_theirs, lags
    )
    gate, inp = join(meta, gate, inp, swapped(back, "ctx", 1))
    norm = 1.0 / math.sqrt(total * rows * width * lax.axis_size("ch") / filter_count)
    sums = sums * norm
    partner = swapped(sums, "ctx", 1)
    low = jnp.where(core == 0, sums, partner)
    high = jnp.where(core == 0, partner, sums)
    return gate, inp, jnp.concatenate([low, high], axis=0)


def solution(mesh):
    return jax.shard_map(
        per_device,
        mesh=mesh,
        in_specs=(P("ctx", None, "ch"), P("ctx", None, "ch"), P("ctx", None, "ch"), P(), P(), P()),
        out_specs=(P("ctx", None, "ch"), P("ctx", None, "ch"), P()),
        check_vma=False,
    )
```

time: 1300 us -> 151 us (0.12)
  local copies, waits for them, and re-layouts: 807 us -> 8.42 us
  waiting for transfers between devices: 241 us -> 23 us
  other arithmetic: 126 us -> 2.13 us
  matrix products: 78 us -> 0 us
  Pallas kernels: 0 us -> 72.4 us
  starting transfers between devices: 22.1 us -> 42.6 us
  between operations: 15.1 us -> 0.74 us
    gather x8 -> x0, local copies, waits for them, and re-layouts: 497 us -> none  [the longest x2 483 us: filter_blocks(): jnp.take(narrow, jnp.clip(lag_offsets, 0, filters.shape[1] - 1), axis=1)]
    psum x1 -> x0, waiting for transfers between devices: 241 us -> none  [per_device(): filter_grad = lax.psum(local_filters, ('ctx', 'ch')) * norm_factor]
    reshape x16 -> x0, local copies, waits for them, and re-layouts: 92.7 us -> none  [the longest x8 49.4 us: lag_sums(): skewed.reshape(filter_count, side_length, 2 * side_length - 1)]
    dot_general x24 -> x0, matrix products: 78 us -> none  [the longest x8 42.7 us: per_device(): jnp.einsum('fij,sjrfc->sirfc', blocks[:, lag_index], shaped, preferred_el...]
    pallas_call x0 -> x7, Pallas kernels: none -> 72.4 us  [the longest x1 19 us: last_pairs(): pl.pallas_call(functools.partial(last_body, lags, sup.shape[0], slots), g...]
    scatter-add x8 -> x0, other arithmetic: 69.9 us -> none  [per_device(): partial_value.at[back_rows[:, lag_index]]]
    slice x20 -> x0, local copies, waits for them, and re-layouts: 62.8 us -> none  [the longest x9 37.9 us: per_device(): selected[:, lag_index]]
    rev x8 -> x1, local copies, waits for them, and re-layouts: 54.3 us -> 2.76 us  [per_device(): filters[:, ::-1]]
  transfers between devices with their start and end apart: 9 -> 15, of which waited for: 1 -> 11; matrix products, arithmetic and copies ran while one was open for 78% -> 3% of each run, Pallas kernels for 0% -> 25%
where the time goes in v1:
time: 151 us; the launch traced here: 149 us
  Pallas kernels  72.4 us (48%)
  starting transfers between devices  42.6 us (28%)
  waiting for transfers between devices  23 us (15%)
  local copies, waits for them, and re-layouts  8.42 us (6%)
  other arithmetic  2.13 us (1%)
    ppermute x11, starting transfers between devices, swapped(): return lax.ppermute(value, axis, [(a, a ^ mask) for a in range(count)])  35.3 us
    pallas_call x1, Pallas kernels, last_pairs(): pl.pallas_call(functools.partial(last_body, lags, sup.shape[0], slots), g...  19 us
    pallas_call x1, Pallas kernels, own_pairs(): pl.pallas_call(functools.partial(own_body, lags, total), grid_spec=pltpu....  17.8 us
    ppermute x11, waiting for transfers between devices, swapped(): return lax.ppermute(value, axis, [(a, a ^ mask) for a in range(count)])  17.3 us
    pallas_call x1, Pallas kernels, cross_squares(): pl.pallas_call(functools.partial(cross_body, lags, sup.shape[0]), grid_sp...  15 us
    pallas_call x2, Pallas kernels, pack(): pl.pallas_call(functools.partial(pack_body, x_index, w_index, far), grid_...  9.67 us
    ppermute x4, starting transfers between devices, shifted(): return lax.ppermute(value, axis, pairs)  7.28 us
    pallas_call x1, Pallas kernels, prep(): pl.pallas_call(prep_body, grid_spec=pltpu.PrefetchScalarGridSpec(num_scal...  6.46 us
  transfers between devices with their start and end apart: 15, of which 11 were waited for; matrix products, arithmetic and copies ran while one was open for 3% of the time, Pallas kernels for 25%

profile of v1, /device:TPU:1, one launch (start us, length us, event | category | flops | bytes accessed | tf_op | source)
XLA Modules:
  0.0 149.4 jit_solution(15249713253825365312)
XLA Ops:
  2.1 6.5 %prep.1 = (bf16[4,128,2048]{2,1,0:T(8,128)(2,1)}, bf16[2,4,128,1024]{3,2,1,0:T(8,128)(2,1)}, bf16[4,128,1024]{2,1,0:T(8,128)(2,1)}) custom-call(s32[8]{0:T(128)} %compare_select_fusion.meta, bf16[4,128,2048]{2,1,0:T(8,128)(2,1)} %gate.1, bf16[4,128,2048]{2,1,0:T(8,128)(2,1)} %cot.3, bf16[4,128,2048]{2,1,0:T(8,128)(2,1)} %x.5), custom_call_target="tpu_custom_call" | custom-call | tf_op jit(solution)/shard_map/prep/pallas_call | solution.py:59
  8.6 3.2 %collective-permute-start = (bf16[2,4,128,1024]{3,2,1,0:T(8,128)(2,1)}, bf16[2,4,128,1024]{3,2,1,0:T(8,128)(2,1)S(1)}, u32[]{:S(2)}, u32[]{:S(2)}) collective-permute-start(bf16[2,4,128,1024]{3,2,1,0:T(8,128)(2,1)} %get-tuple-element.28), channel_id=1, source_target_pairs={{0,4},{4,0},{8,12},{12,8},{16,20},{20,16},{24,28},{28,24},{32,36},... | collective-permute-start | bytes 6291464 | tf_op jit(solution)/shard_map/ppermute | solution.py:30
  11.8 4.0 %collective-permute-done.xt.wt = bf16[2,4,128,1024]{3,2,1,0:T(8,128)(2,1)S(1)} collective-permute-done((bf16[2,4,128,1024]{3,2,1,0:T(8,128)(2,1)}, bf16[2,4,128,1024]{3,2,1,0:T(8,128)(2,1)S(1)}, u32[]{:S(2)}, u32[]{:S(2)}) %collective-permute-start) | collective-permute-done | bytes 2097184 | tf_op jit(solution)/shard_map/ppermute | solution.py:30
  15.8 1.3 copy-done
  17.1 5.0 %pack.2 = (bf16[4,128,1024]{2,1,0:T(8,128)(2,1)}, bf16[4,128,1024]{2,1,0:T(8,128)(2,1)}) custom-call(s32[8]{0:T(128)} %compare_select_fusion.meta, bf16[4,128,2048]{2,1,0:T(8,128)(2,1)} %x.5, bf16[2,4,128,1024]{3,2,1,0:T(8,128)(2,1)} %copy-done, bf16[4,128,2048]{2,1,0:T(8,128)(2,1)} %get-tuple-element.29.wm.w, bf16[2,4,128,1024]{3,2,1,0:T(8,128)(2,1)} %copy-done), custom_call_target="tpu_custom_call" | custom-call | tf_op jit(solution)/shard_map/pack/pallas_call | solution.py:128
  22.1 1.5 %collective-permute-start.1 = (bf16[4,128,1024]{2,1,0:T(8,128)(2,1)}, bf16[4,128,1024]{2,1,0:T(8,128)(2,1)S(1)}, u32[]{:S(2)}, u32[]{:S(2)}) collective-permute-start(bf16[4,128,1024]{2,1,0:T(8,128)(2,1)} %get-tuple-element.30), channel_id=1, source_target_pairs={{0,8},{4,12},{8,16},{12,20},{16,24},{20,28},{24,32},{28,36},{32,40... | collective-permute-start | bytes 3145736 | tf_op jit(solution)/shard_map/ppermute | solution.py:25
  23.7 1.3 collective-permute-start.2
  25.7 2.8 %rev.3.flip = f32[16,1024]{1,0:T(8,128)} reverse(f32[16,1024]{1,0:T(8,128)S(1)} %copy-done.7), dimensions={1} | reverse | bytes 131072 | tf_op jit(solution)/shard_map/rev | solution.py:516
  29.2 17.8 %own_pairs.1 = (f32[8,128,1024]{2,1,0:T(8,128)}, f32[8,128,1024]{2,1,0:T(8,128)}, f32[8,1024]{1,0:T(8,128)}, bf16[8,128,1024]{2,1,0:T(8,128)(2,1)}, bf16[8,128,1024]{2,1,0:T(8,128)(2,1)}) custom-call(s32[8]{0:T(128)} %compare_select_fusion.meta, s32[192,8]{1,0:T(8,128)} %copy.16.sup, f32[16,1024]{1,0:T(8,128)} %filt.1, f32[16,1024]{1,0:T(8,128)} %rev.3.flip, ...), custom_call_target="tpu_custom_call" | custom-call | flops 8000000000 | bytes 16777216 | tf_op jit(solution)/shard_map/own_pairs/pallas_call | solution.py:265
  47.1 2.7 %collective-permute-done.2.rest_1_.wh.wn = bf16[4,128,1024]{2,1,0:T(8,128)(2,1)S(1)} collective-permute-done((bf16[4,128,1024]{2,1,0:T(8,128)(2,1)}, bf16[4,128,1024]{2,1,0:T(8,128)(2,1)S(1)}, u32[]{:S(2)}, u32[]{:S(2)}) %collective-permute-start.2) | collective-permute-done | bytes 1048608 | tf_op jit(solution)/shard_map/ppermute | solution.py:25
  50.8 4.7 %pack.3 = (bf16[3,128,1024]{2,1,0:T(8,128)(2,1)}, bf16[3,128,1024]{2,1,0:T(8,128)(2,1)}) custom-call(s32[8]{0:T(128)} %compare_select_fusion.meta, bf16[4,128,2048]{2,1,0:T(8,128)(2,1)} %x.5, bf16[2,4,128,1024]{3,2,1,0:T(8,128)(2,1)} %copy-done, bf16[4,128,2048]{2,1,0:T(8,128)(2,1)} %get-tuple-element.29.wm.w, bf16[2,4,128,1024]{3,2,1,0:T(8,128)(2,1)} %copy-done, ...), custom_call_target="tpu_custom_call" | custom-call | tf_op jit(solution)/shard_map/pack/pallas_call | solution.py:128
  55.5 3.2 %collective-permute-start.3 = (bf16[3,128,1024]{2,1,0:T(8,128)(2,1)}, bf16[3,128,1024]{2,1,0:T(8,128)(2,1)S(1)}, u32[]{:S(2)}, u32[]{:S(2)}) collective-permute-start(bf16[3,128,1024]{2,1,0:T(8,128)(2,1)} %get-tuple-element.41), channel_id=1, source_target_pairs={{0,8},{4,12},{8,16},{12,20},{16,24},{20,28},{24,32},{28,36},{32,40... | collective-permute-start | bytes 2359304 | tf_op jit(solution)/shard_map/ppermute | solution.py:25
  59.9 15.0 %cross_squares.1 = f32[8,1024]{1,0:T(8,128)} custom-call(s32[8]{0:T(128)} %compare_select_fusion.meta, s32[192,8]{1,0:T(8,128)} %copy.16.sup, f32[8,1024]{1,0:T(8,128)} %get-tuple-element.43.prior, bf16[4,128,2048]{2,1,0:T(8,128)(2,1)} %x.5, bf16[2,4,128,1024]{3,2,1,0:T(8,128)(2,1)} %copy-done, bf16[4,128,2048]{2,1,0:T(8,128)(2,1)} %get-tuple-element.29.wm.w, ...), custom_call_target="tpu_custom_call" | custom-call | flops 3000000000 | bytes 6291456 | tf_op jit(solution)/shard_map/cross_squares/pallas_call | solution.py:345
  75.0 3.0 %collective-permute-done.4.wf = bf16[3,128,1024]{2,1,0:T(8,128)(2,1)S(1)} collective-permute-done((bf16[3,128,1024]{2,1,0:T(8,128)(2,1)}, bf16[3,128,1024]{2,1,0:T(8,128)(2,1)S(1)}, u32[]{:S(2)}, u32[]{:S(2)}) %collective-permute-start.4) | collective-permute-done | bytes 786464 | tf_op jit(solution)/shard_map/ppermute | solution.py:25
  79.2 19.0 %last_pairs.1 = (bf16[4,128,2048]{2,1,0:T(8,128)(2,1)}, bf16[4,128,2048]{2,1,0:T(8,128)(2,1)}, bf16[2,4,128,1024]{3,2,1,0:T(8,128)(2,1)}) custom-call(s32[8]{0:T(128)} %compare_select_fusion.meta, s32[192,8]{1,0:T(8,128)} %copy.16.sup, f32[8,128,1024]{2,1,0:T(8,128)} %get-tuple-element.35.conv, f32[8,128,1024]{2,1,0:T(8,128)} %get-tuple-element.36.adj, ...), custom_call_target="tpu_custom_call" | custom-call | flops 4000000000 | bytes 20971520 | tf_op jit(solution)/shard_map/last_pairs/pallas_call | solution.py:437
  98.2 2.8 %collective-permute-start.6 = (bf16[2,4,128,1024]{3,2,1,0:T(8,128)(2,1)}, bf16[2,4,128,1024]{3,2,1,0:T(8,128)(2,1)S(1)}, u32[]{:S(2)}, u32[]{:S(2)}) collective-permute-start(bf16[2,4,128,1024]{3,2,1,0:T(8,128)(2,1)} %get-tuple-element.49), channel_id=1, source_target_pairs={{0,4},{4,0},{8,12},{12,8},{16,20},{20,16},{24,28},{28,24},{32,36},... | collective-permute-start | bytes 6291464 | tf_op jit(solution)/shard_map/ppermute | solution.py:30
  101.0 2.5 %collective-permute-start.7 = (f32[8,1024]{1,0:T(8,128)S(1)}, f32[8,1024]{1,0:T(8,128)S(1)}, u32[]{:S(2)}, u32[]{:S(2)}) collective-permute-start(f32[8,1024]{1,0:T(8,128)S(1)} %copy-done.8), channel_id=1, source_target_pairs={{0,8},{4,12},{8,0},{12,4},{16,24},{20,28},{24,16},{28,20},{32,40},... | collective-permute-start | bytes 98312 | tf_op jit(solution)/shard_map/ppermute | solution.py:30
  103.5 1.6 %collective-permute-done.7 = f32[8,1024]{1,0:T(8,128)S(1)} collective-permute-done((f32[8,1024]{1,0:T(8,128)S(1)}, f32[8,1024]{1,0:T(8,128)S(1)}, u32[]{:S(2)}, u32[]{:S(2)}) %collective-permute-start.7) | collective-permute-done | bytes 32800 | tf_op jit(solution)/shard_map/ppermute | solution.py:30
  105.2 4.1 %collective-permute-start.8 = (f32[8,1024]{1,0:T(8,128)S(1)}, f32[8,1024]{1,0:T(8,128)S(1)}, u32[]{:S(2)}, u32[]{:S(2)}) collective-permute-start(f32[8,1024]{1,0:T(8,128)S(1)} %add.38), channel_id=1, source_target_pairs={{0,16},{4,20},{8,24},{12,28},{16,0},{20,4},{24,8},{28,12},{32,48},... | collective-permute-start | bytes 98312 | tf_op jit(solution)/shard_map/ppermute | solution.py:30
  109.3 1.3 collective-permute-done.8
  110.6 1.4 collective-permute-start.9
  112.0 1.4 collective-permute-done.9
  113.4 6.8 %collective-permute-start.10 = (f32[8,1024]{1,0:T(8,128)S(1)}, f32[8,1024]{1,0:T(8,128)S(1)}, u32[]{:S(2)}, u32[]{:S(2)}) collective-permute-start(f32[8,1024]{1,0:T(8,128)S(1)} %add.40), channel_id=1, source_target_pairs={{0,64},{4,68},{8,72},{12,76},{16,80},{20,84},{24,88},{28,92},{32,9... | collective-permute-start | bytes 98312 | tf_op jit(solution)/shard_map/ppermute | solution.py:30
  120.2 1.3 collective-permute-done.10
  121.5 3.2 %collective-permute-start.11 = (f32[8,1024]{1,0:T(8,128)S(1)}, f32[8,1024]{1,0:T(8,128)S(1)}, u32[]{:S(2)}, u32[]{:S(2)}) collective-permute-start(f32[8,1024]{1,0:T(8,128)S(1)} %add.41), channel_id=1, source_target_pairs={{0,128},{4,132},{8,136},{12,140},{16,144},{20,148},{24,152},{28,15... | collective-permute-start | bytes 98312 | tf_op jit(solution)/shard_map/ppermute | solution.py:30
  124.7 3.5 %collective-permute-done.11 = f32[8,1024]{1,0:T(8,128)S(1)} collective-permute-done((f32[8,1024]{1,0:T(8,128)S(1)}, f32[8,1024]{1,0:T(8,128)S(1)}, u32[]{:S(2)}, u32[]{:S(2)}) %collective-permute-start.11) | collective-permute-done | bytes 32800 | tf_op jit(solution)/shard_map/ppermute | solution.py:30
  129.4 1.9 %collective-permute-done.12 = f32[8,1024]{1,0:T(8,128)S(1)} collective-permute-done((f32[8,1024]{1,0:T(8,128)S(1)}, f32[8,1024]{1,0:T(8,128)S(1)}, u32[]{:S(2)}, u32[]{:S(2)}) %collective-permute-start.12) | collective-permute-done | bytes 32800 | tf_op jit(solution)/shard_map/ppermute | solution.py:30
  131.3 2.7 %collective-permute-start.13 = (f32[8,1024]{1,0:T(8,128)S(1)}, f32[8,1024]{1,0:T(8,128)S(1)}, u32[]{:S(2)}, u32[]{:S(2)}) collective-permute-start(f32[8,1024]{1,0:T(8,128)S(1)} %add.43), channel_id=1, source_target_pairs={{0,2},{1,3},{2,0},{3,1},{4,6},{5,7},{6,4},{7,5},{8,10},{9,11},{10,... | collective-permute-start | bytes 98312 | tf_op jit(solution)/shard_map/ppermute | solution.py:30
  134.0 1.5 %collective-permute-done.13 = f32[8,1024]{1,0:T(8,128)S(1)} collective-permute-done((f32[8,1024]{1,0:T(8,128)S(1)}, f32[8,1024]{1,0:T(8,128)S(1)}, u32[]{:S(2)}, u32[]{:S(2)}) %collective-permute-start.13) | collective-permute-done | bytes 32800 | tf_op jit(solution)/shard_map/ppermute | solution.py:30
  135.6 6.6 %collective-permute-start.14 = (f32[8,1024]{1,0:T(8,128)S(1)}, f32[8,1024]{1,0:T(8,128)S(1)}, u32[]{:S(2)}, u32[]{:S(2)}) collective-permute-start(f32[8,1024]{1,0:T(8,128)S(1)} %add_multiply_fusion), channel_id=1, source_target_pairs={{0,4},{4,0},{8,12},{12,8},{16,20},{20,16},{24,28},{28,24},{32,36},... | collective-permute-start | bytes 98312 | tf_op jit(solution)/shard_map/ppermute | solution.py:30
  143.6 1.3 copy-done.3
  145.0 4.4 %join.1 = (bf16[4,128,2048]{2,1,0:T(8,128)(2,1)}, bf16[4,128,2048]{2,1,0:T(8,128)(2,1)}) custom-call(s32[8]{0:T(128)} %compare_select_fusion.meta, bf16[4,128,2048]{2,1,0:T(8,128)(2,1)} %get-tuple-element.47.gate_in, bf16[4,128,2048]{2,1,0:T(8,128)(2,1)} %get-tuple-element.48.input_in, ...), custom_call_target="tpu_custom_call", output_to_operand_aliasing={{0}: (1, {}), {1}: (2, {})} | custom-call | tf_op jit(solution)/shard_map/join/pallas_call | solution.py:477
  (39 shorter events, 9.2 us)
Async XLA Ops:
  8.6 7.2 %collective-permute-start = (bf16[2,4,128,1024]{3,2,1,0:T(8,128)(2,1)}, bf16[2,4,128,1024]{3,2,1,0:T(8,128)(2,1)S(1)}, u32[]{:S(2)}, u32[]{:S(2)}) collective-permute-start(bf16[2,4,128,1024]{3,2,1,0:T(8,128)(2,1)} %get-tuple-element.28), channel_id=1, source_target_pairs={{0,4},{4,0},{8,12},{12,8},{16,20},{20,16},{24,28},{28,24},{32,36},... | collective-permute-start | bytes 6291464 | tf_op jit(solution)/shard_map/ppermute | solution.py:30
  15.8 1.3 copy-start
  17.1 8.6 %copy-start.7 = (f32[16,1024]{1,0:T(8,128)S(1)}, f32[16,1024]{1,0:T(8,128)}, u32[]{:S(2)}) copy-start(f32[16,1024]{1,0:T(8,128)} %filt.1) | copy-start | bytes 196612
  17.1 11.3 %copy-start.9 = (s32[192,8]{0,1:T(8,128)S(1)}, s32[192,8]{0,1:T(8,128)}, u32[]{:S(2)}) copy-start(s32[192,8]{0,1:T(8,128)} %param.11) | copy-start | bytes 18436
  22.1 24.9 %collective-permute-start.1 = (bf16[4,128,1024]{2,1,0:T(8,128)(2,1)}, bf16[4,128,1024]{2,1,0:T(8,128)(2,1)S(1)}, u32[]{:S(2)}, u32[]{:S(2)}) collective-permute-start(bf16[4,128,1024]{2,1,0:T(8,128)(2,1)} %get-tuple-element.30), channel_id=1, source_target_pairs={{0,8},{4,12},{8,16},{12,20},{16,24},{20,28},{24,32},{28,36},{32,40... | collective-permute-start | bytes 3145736 | tf_op jit(solution)/shard_map/ppermute | solution.py:25
  23.7 26.2 %collective-permute-start.2 = (bf16[4,128,1024]{2,1,0:T(8,128)(2,1)}, bf16[4,128,1024]{2,1,0:T(8,128)(2,1)S(1)}, u32[]{:S(2)}, u32[]{:S(2)}) collective-permute-start(bf16[4,128,1024]{2,1,0:T(8,128)(2,1)} %get-tuple-element.31), channel_id=1, source_target_pairs={{8,0},{12,4},{16,8},{20,12},{24,16},{28,20},{32,24},{36,28},{40,32... | collective-permute-start | bytes 3145736 | tf_op jit(solution)/shard_map/ppermute | solution.py:25
  25.0 53.0 %collective-permute-start.5 = (bf16[4,128,1024]{2,1,0:T(8,128)(2,1)}, bf16[4,128,1024]{2,1,0:T(8,128)(2,1)S(1)}, u32[]{:S(2)}, u32[]{:S(2)}) collective-permute-start(bf16[4,128,1024]{2,1,0:T(8,128)(2,1)} %get-tuple-element.46), channel_id=1, source_target_pairs={{0,4},{4,0},{8,12},{12,8},{16,20},{20,16},{24,28},{28,24},{32,36},... | collective-permute-start | bytes 3145736 | tf_op jit(solution)/shard_map/ppermute | solution.py:30
  47.1 2.7 %copy-start.1 = (bf16[4,128,1024]{2,1,0:T(8,128)(2,1)}, bf16[4,128,1024]{2,1,0:T(8,128)(2,1)S(1)}, u32[]{:S(2)}) copy-start(bf16[4,128,1024]{2,1,0:T(8,128)(2,1)S(1)} %collective-permute-done.1.rest_0_.xh.xn) | copy-start | bytes 3145732
  49.8 1.0 copy-start.2
  55.5 19.5 %collective-permute-start.3 = (bf16[3,128,1024]{2,1,0:T(8,128)(2,1)}, bf16[3,128,1024]{2,1,0:T(8,128)(2,1)S(1)}, u32[]{:S(2)}, u32[]{:S(2)}) collective-permute-start(bf16[3,128,1024]{2,1,0:T(8,128)(2,1)} %get-tuple-element.41), channel_id=1, source_target_pairs={{0,8},{4,12},{8,16},{12,20},{16,24},{20,28},{24,32},{28,36},{32,40... | collective-permute-start | bytes 2359304 | tf_op jit(solution)/shard_map/ppermute | solution.py:25
  58.6 19.3 %collective-permute-start.4 = (bf16[3,128,1024]{2,1,0:T(8,128)(2,1)}, bf16[3,128,1024]{2,1,0:T(8,128)(2,1)S(1)}, u32[]{:S(2)}, u32[]{:S(2)}) collective-permute-start(bf16[3,128,1024]{2,1,0:T(8,128)(2,1)} %get-tuple-element.42), channel_id=1, source_target_pairs={{8,0},{12,4},{16,8},{20,12},{24,16},{28,20},{32,24},{36,28},{40,32... | collective-permute-start | bytes 2359304 | tf_op jit(solution)/shard_map/ppermute | solution.py:25
  75.0 3.0 %copy-start.5 = (bf16[3,128,1024]{2,1,0:T(8,128)(2,1)}, bf16[3,128,1024]{2,1,0:T(8,128)(2,1)S(1)}, u32[]{:S(2)}) copy-start(bf16[3,128,1024]{2,1,0:T(8,128)(2,1)S(1)} %collective-permute-done.3.xf) | copy-start | bytes 2359300
  78.0 0.9 copy-start.6
  78.0 1.3 copy-start.4
  79.2 21.8 %copy-start.8 = (f32[8,1024]{1,0:T(8,128)S(1)}, f32[8,1024]{1,0:T(8,128)}, u32[]{:S(2)}) copy-start(f32[8,1024]{1,0:T(8,128)} %cross_squares.1) | copy-start | bytes 98308
  98.2 45.4 %collective-permute-start.6 = (bf16[2,4,128,1024]{3,2,1,0:T(8,128)(2,1)}, bf16[2,4,128,1024]{3,2,1,0:T(8,128)(2,1)S(1)}, u32[]{:S(2)}, u32[]{:S(2)}) collective-permute-start(bf16[2,4,128,1024]{3,2,1,0:T(8,128)(2,1)} %get-tuple-element.49), channel_id=1, source_target_pairs={{0,4},{4,0},{8,12},{12,8},{16,20},{20,16},{24,28},{28,24},{32,36},... | collective-permute-start | bytes 6291464 | tf_op jit(solution)/shard_map/ppermute | solution.py:30
  101.0 4.1 %collective-permute-start.7 = (f32[8,1024]{1,0:T(8,128)S(1)}, f32[8,1024]{1,0:T(8,128)S(1)}, u32[]{:S(2)}, u32[]{:S(2)}) collective-permute-start(f32[8,1024]{1,0:T(8,128)S(1)} %copy-done.8), channel_id=1, source_target_pairs={{0,8},{4,12},{8,0},{12,4},{16,24},{20,28},{24,16},{28,20},{32,40},... | collective-permute-start | bytes 98312 | tf_op jit(solution)/shard_map/ppermute | solution.py:30
  105.2 5.4 %collective-permute-start.8 = (f32[8,1024]{1,0:T(8,128)S(1)}, f32[8,1024]{1,0:T(8,128)S(1)}, u32[]{:S(2)}, u32[]{:S(2)}) collective-permute-start(f32[8,1024]{1,0:T(8,128)S(1)} %add.38), channel_id=1, source_target_pairs={{0,16},{4,20},{8,24},{12,28},{16,0},{20,4},{24,8},{28,12},{32,48},... | collective-permute-start | bytes 98312 | tf_op jit(solution)/shard_map/ppermute | solution.py:30
  110.6 2.8 %collective-permute-start.9 = (f32[8,1024]{1,0:T(8,128)S(1)}, f32[8,1024]{1,0:T(8,128)S(1)}, u32[]{:S(2)}, u32[]{:S(2)}) collective-permute-start(f32[8,1024]{1,0:T(8,128)S(1)} %add.39), channel_id=1, source_target_pairs={{0,32},{4,36},{8,40},{12,44},{16,48},{20,52},{24,56},{28,60},{32,0... | collective-permute-start | bytes 98312 | tf_op jit(solution)/shard_map/ppermute | solution.py:30
  113.4 8.1 %collective-permute-start.10 = (f32[8,1024]{1,0:T(8,128)S(1)}, f32[8,1024]{1,0:T(8,128)S(1)}, u32[]{:S(2)}, u32[]{:S(2)}) collective-permute-start(f32[8,1024]{1,0:T(8,128)S(1)} %add.40), channel_id=1, source_target_pairs={{0,64},{4,68},{8,72},{12,76},{16,80},{20,84},{24,88},{28,92},{32,9... | collective-permute-start | bytes 98312 | tf_op jit(solution)/shard_map/ppermute | solution.py:30
  121.5 6.7 %collective-permute-start.11 = (f32[8,1024]{1,0:T(8,128)S(1)}, f32[8,1024]{1,0:T(8,128)S(1)}, u32[]{:S(2)}, u32[]{:S(2)}) collective-permute-start(f32[8,1024]{1,0:T(8,128)S(1)} %add.41), channel_id=1, source_target_pairs={{0,128},{4,132},{8,136},{12,140},{16,144},{20,148},{24,152},{28,15... | collective-permute-start | bytes 98312 | tf_op jit(solution)/shard_map/ppermute | solution.py:30
  128.2 3.1 %collective-permute-start.12 = (f32[8,1024]{1,0:T(8,128)S(1)}, f32[8,1024]{1,0:T(8,128)S(1)}, u32[]{:S(2)}, u32[]{:S(2)}) collective-permute-start(f32[8,1024]{1,0:T(8,128)S(1)} %add.42), channel_id=1, source_target_pairs={{0,1},{1,0},{2,3},{3,2},{4,5},{5,4},{6,7},{7,6},{8,9},{9,8},{10,11... | collective-permute-start | bytes 98312 | tf_op jit(solution)/shard_map/ppermute | solution.py:30
  131.3 4.3 %collective-permute-start.13 = (f32[8,1024]{1,0:T(8,128)S(1)}, f32[8,1024]{1,0:T(8,128)S(1)}, u32[]{:S(2)}, u32[]{:S(2)}) collective-permute-start(f32[8,1024]{1,0:T(8,128)S(1)} %add.43), channel_id=1, source_target_pairs={{0,2},{1,3},{2,0},{3,1},{4,6},{5,7},{6,4},{7,5},{8,10},{9,11},{10,... | collective-permute-start | bytes 98312 | tf_op jit(solution)/shard_map/ppermute | solution.py:30
  135.6 7.4 %collective-permute-start.14 = (f32[8,1024]{1,0:T(8,128)S(1)}, f32[8,1024]{1,0:T(8,128)S(1)}, u32[]{:S(2)}, u32[]{:S(2)}) collective-permute-start(f32[8,1024]{1,0:T(8,128)S(1)} %add_multiply_fusion), channel_id=1, source_target_pairs={{0,4},{4,0},{8,12},{12,8},{16,20},{20,16},{24,28},{28,24},{32,36},... | collective-permute-start | bytes 98312 | tf_op jit(solution)/shard_map/ppermute | solution.py:30
  143.6 1.3 copy-start.3

commit v2 on v1

v2 whole, which is shorter than its diff:
```python
import functools
import math

import jax
import jax.numpy as jnp
from jax import lax
from jax.experimental import pallas as pl
from jax.experimental.pallas import tpu as pltpu
from jax.sharding import PartitionSpec as P

GROUP = 128
NEAR = 4
PIECE = 2
BF = jnp.bfloat16
F32 = jnp.float32
VMEM_LIMIT = 20 * 1024 * 1024


def params():
    return pltpu.CompilerParams(vmem_limit_bytes=VMEM_LIMIT)


def shifted(value, axis, steps):
    count = lax.axis_size(axis)
    pairs = [(a, a + steps) for a in range(max(0, -steps), min(count, count - steps))]
    return lax.ppermute(value, axis, pairs)


def swapped(value, axis, mask):
    count = lax.axis_size(axis)
    return lax.ppermute(value, axis, [(a, a ^ mask) for a in range(count)])


def chip_meta(meta):
    first, second, end, core = meta[0], meta[1], meta[2], meta[3]
    return first, second - first, end - first, core


def place(meta, index):
    _, low, _, core = chip_meta(meta)
    on_second = (index >= low).astype(jnp.int32)
    slot = jnp.clip(index - on_second * low, 0, 3)
    return on_second == core, slot


def prep_body(meta, gate, cot, x, cot_all, w_out, send, cot_out, w_other, sems):
    slots, rows, half = w_other.shape
    step = pl.program_id(0)
    other = pl.ds(pl.multiple_of((1 - meta[3]) * half, half), half)
    copies = [
        pltpu.make_async_copy(x.at[:, :, other], send.at[0], sems.at[0]),
        pltpu.make_async_copy(cot_all.at[:, :, other], cot_out, sems.at[1]),
    ]

    @pl.when(step == 0)
    def _():
        for copy in copies:
            copy.start()

    w_out[0] = (gate[0].astype(F32) * cot[0].astype(F32)).astype(BF)
    w_other[step] = w_out[0, :, other]
    pltpu.make_async_copy(w_other.at[step], send.at[1, step], sems.at[2 + step]).start()

    @pl.when(step == slots - 1)
    def _():
        for copy in copies:
            copy.wait()
        for s in range(slots):
            pltpu.make_async_copy(w_other.at[s], send.at[1, s], sems.at[2 + s]).wait()


def prep(meta, gate, cot, x):
    slots, rows, width = x.shape
    half = width // 2
    full = pl.BlockSpec((1, rows, width), lambda s, m: (s, 0, 0))
    loose = pl.BlockSpec(memory_space=pl.ANY)
    return pl.pallas_call(
        prep_body,
        grid_spec=pltpu.PrefetchScalarGridSpec(
            num_scalar_prefetch=1,
            grid=(slots,),
            in_specs=[full, full, loose, loose],
            out_specs=[full, loose, loose],
            scratch_shapes=[
                pltpu.VMEM((slots, rows, half), BF),
                pltpu.SemaphoreType.DMA((2 + slots,)),
            ],
        ),
        out_shape=[
            jax.ShapeDtypeStruct(x.shape, BF),
            jax.ShapeDtypeStruct((2, slots, rows, half), BF),
            jax.ShapeDtypeStruct((slots, rows, half), BF),
        ],
        compiler_params=params(),
        cost_estimate=pl.CostEstimate(flops=2 << 20, bytes_accessed=12 << 20, transcendentals=0),
        name="prep",
    )(meta, gate, cot, x, cot)


def pack_body(tiles, x_at, w_at, halos, meta, x, w, theirs, *rest):
    x_halos, w_halos = rest[:halos], rest[halos : 2 * halos]
    x_out, w_out, sems = rest[2 * halos :]
    half = x_out.shape[2]
    _, _, count, core = chip_meta(meta)
    lanes = pl.ds(pl.multiple_of(core * half, half), half)
    for which, (own, out) in enumerate(((x, x_out), (w, w_out))):
        for j in range(tiles):
            sem = sems.at[which * tiles + j]
            index = (x_at if which == 0 else w_at)(j, count)
            mine, slot = place(meta, index)
            depth = -1 - index if which == 0 else index - count
            here = depth < 0

            @pl.when(here & mine)
            def _():
                pltpu.make_async_copy(own.at[slot, :, lanes], out.at[j], sem).start()

            @pl.when(here & jnp.logical_not(mine))
            def _():
                pltpu.make_async_copy(theirs.at[which, slot], out.at[j], sem).start()

            for h in range(halos):
                halo = (x_halos if which == 0 else w_halos)[h]
                inside = jnp.clip(depth - h * PIECE, 0, PIECE - 1)
                row = PIECE - 1 - inside if which == 0 else inside

                @pl.when((depth >= h * PIECE) & (depth < (h + 1) * PIECE))
                def _():
                    pltpu.make_async_copy(halo.at[row], out.at[j], sem).start()

    for which, out in enumerate((x_out, w_out)):
        for j in range(tiles):
            pltpu.make_async_copy(theirs.at[which, 0], out.at[j], sems.at[which * tiles + j]).wait()


def pack(meta, x, w, theirs, tiles, x_at, w_at, x_halos=(), w_halos=()):
    slots, rows, width = x.shape
    half = width // 2
    halos = len(x_halos)
    loose = pl.BlockSpec(memory_space=pl.ANY)
    return pl.pallas_call(
        functools.partial(pack_body, tiles, x_at, w_at, halos),
        grid_spec=pltpu.PrefetchScalarGridSpec(
            num_scalar_prefetch=1,
            grid=(1,),
            in_specs=[loose] * (3 + 2 * halos),
            out_specs=[loose, loose],
            scratch_shapes=[pltpu.SemaphoreType.DMA((2 * tiles,))],
        ),
        out_shape=[jax.ShapeDtypeStruct((tiles, rows, half), BF)] * 2,
        compiler_params=params(),
        cost_estimate=pl.CostEstimate(flops=0, bytes_accessed=tiles << 20, transcendentals=0),
        name="pack",
    )(meta, x, w, theirs, *x_halos, *w_halos)


def readers_of(sup, tile, total, lags):
    found = jnp.int32(0)
    for lag in range(lags):
        at = jnp.clip(tile + lag, 0, total - 1)
        live = (tile >= 0) & (tile + lag < total) & (sup[at, lag] >= 0)
        found += live.astype(jnp.int32)
    return found


def sources_of(sup, tile, total, lags):
    at = jnp.clip(tile, 0, total - 1)
    found = jnp.int32(0)
    for lag in range(lags):
        found += (sup[at, lag] >= 0).astype(jnp.int32)
    return found


def column_mask(width, low, high):
    lane = lax.broadcasted_iota(jnp.int32, (16, width), 1)
    return jnp.where((lane >= low) & (lane < high), 1.0, 0.0).astype(BF)


def masked(value, mask):
    rows, width = value.shape
    return (value.reshape(rows // 16, 16, width) * mask[None]).reshape(rows, width)


def dot(a, b):
    return jnp.dot(a, b, preferred_element_type=F32)


def reversal(rows):
    r = lax.broadcasted_iota(jnp.int32, (rows, rows), 0)
    c = lax.broadcasted_iota(jnp.int32, (rows, rows), 1)
    return jnp.where(r + c == rows - 1, 1.0, 0.0).astype(BF)


def diagonal_sums(square):
    rows, width = square.shape
    padded = jnp.concatenate([square, jnp.zeros((rows, rows), F32)], axis=1)
    skewed = pltpu.roll(padded, 0, 1, stride=1, stride_axis=0)
    total = jnp.sum(skewed, axis=0, keepdims=True)
    total = pltpu.roll(jnp.broadcast_to(total, (8, width + rows)), width + 1, 1)
    return total[:1, :width]


def pick(mine, theirs, meta, index):
    own, slot = place(meta, index)
    return jnp.where(own, mine[slot], theirs[slot])


def own_body(lags, total, base, chained, meta, sup, filt, flip, x, xt, w, wt, *rest):
    rest = rest[4:] if chained else rest
    conv_out, adj_out, fwd_out, bwd_out, sums_out, xs, xl, ws, turned, masks, reach = rest
    step = pl.program_id(0)
    group = base + step
    cap, rows, _ = xs.shape
    first, _, count, _ = chip_meta(meta)

    @pl.when(step == 0)
    def _():
        sums_out[...] = jnp.zeros_like(sums_out)
        for s in range(cap):
            reach[s] = jnp.minimum(readers_of(sup, first + s, total, lags), count - s)
            reach[cap + s] = sources_of(sup, first + s, total, lags)
        for k in range(lags):
            for s in range(cap):
                live = jnp.where(k < reach[s], 1.0, 0.0)
                masks[k, :, s * rows : (s + 1) * rows] = jnp.full((16, rows), live, F32).astype(BF)

    taps = filt[pl.ds(group, 1), :].astype(BF).astype(F32)
    width = taps.shape[1]
    pad = jnp.zeros((1, rows), F32)
    spread = jnp.broadcast_to(jnp.concatenate([taps, pad], axis=1), (rows, width + rows))
    bwd_out[0] = pltpu.roll(spread, 0, 1, stride=1, stride_axis=0)[:, :width].astype(BF)
    taps = flip[pl.ds(group, 1), :].astype(BF).astype(F32)
    spread = jnp.broadcast_to(jnp.concatenate([taps, pad], axis=1), (rows, width + rows))
    fwd_out[0] = pltpu.roll(spread, width + 1, 1, stride=1, stride_axis=0)[:, :width].astype(BF)

    for s in range(cap):
        tile = pick(x, xt.at[0], meta, s)
        xs[s] = tile
        xl[:, s * rows : (s + 1) * rows] = tile
        tile = pick(w, wt.at[0], meta, s)
        ws[s] = tile
        turned[s] = tile.T
    for i in range(cap):
        near = column_mask((i + 1) * rows, (i + 1 - reach[cap + i]) * rows, width)
        left = masked(fwd_out[0, :, (lags - 1 - i) * rows :], near)
        conv_out[i] = dot(left, xs[0 : i + 1].reshape((i + 1) * rows, rows))
    for s in range(cap):
        size = (cap - s) * rows
        left = masked(bwd_out[0, :, :size], column_mask(size, 0, reach[s] * rows))
        adj_out[s] = dot(left, ws[s:cap].reshape(size, rows))
    back = dot(reversal(rows), xl[...]).astype(BF)
    squares = []
    for k in range(lags):
        size = (cap - k) * rows
        left = masked(back[:, :size], masks[k, :, :size])
        squares.append(dot(left, turned[k:cap].reshape(size, rows)))
    sums_out[pl.ds(group, 1), :] = diagonal_sums(jnp.concatenate(squares, axis=1))


def own_pairs(meta, sup, filt, flip, x, w, theirs, lags, base, steps, prior):
    slots, rows, width = x.shape
    half = width // 2
    groups = half // GROUP
    total = sup.shape[0]
    taps = filt.shape[1]
    cap = 2 * slots

    def lane(g, m, s):
        return (0, 0, m[3] * groups + base + g)

    in_specs = [
        pl.BlockSpec((groups, taps), lambda g, m, s: (m[3], 0)),
        pl.BlockSpec((groups, taps), lambda g, m, s: (m[3], 0)),
        pl.BlockSpec((slots, rows, GROUP), lane),
        pl.BlockSpec((1, slots, rows, GROUP), lambda g, m, s: (0, 0, 0, base + g)),
        pl.BlockSpec((slots, rows, GROUP), lane),
        pl.BlockSpec((1, slots, rows, GROUP), lambda g, m, s: (1, 0, 0, base + g)),
    ]
    args = [filt, flip, x, theirs, w, theirs]
    chained = prior is not None
    aliases = {}
    if chained:
        aliases = {2 + len(args) + i: i for i in range(4)}
        in_specs += [pl.BlockSpec(memory_space=pl.ANY)] * 4
        args += list(prior)
    tiles = pl.BlockSpec((cap, rows, GROUP), lambda g, m, s: (0, 0, base + g))
    bands = pl.BlockSpec((1, rows, taps), lambda g, m, s: (base + g, 0, 0))
    return pl.pallas_call(
        functools.partial(own_body, lags, total, base, chained),
        grid_spec=pltpu.PrefetchScalarGridSpec(
            num_scalar_prefetch=2,
            grid=(steps,),
            in_specs=in_specs,
            out_specs=[tiles, tiles, bands, bands, pl.BlockSpec((groups, taps), lambda g, m, s: (0, 0))],
            scratch_shapes=[
                pltpu.VMEM((cap, rows, GROUP), BF),
                pltpu.VMEM((rows, cap * GROUP), BF),
                pltpu.VMEM((cap, rows, GROUP), BF),
                pltpu.VMEM((cap, GROUP, rows), BF),
                pltpu.VMEM((lags, 16, cap * GROUP), BF),
                pltpu.SMEM((2 * cap,), jnp.int32),
            ],
        ),
        out_shape=[
            jax.ShapeDtypeStruct((cap, rows, half), F32),
            jax.ShapeDtypeStruct((cap, rows, half), F32),
            jax.ShapeDtypeStruct((groups, rows, taps), BF),
            jax.ShapeDtypeStruct((groups, rows, taps), BF),
            jax.ShapeDtypeStruct((groups, taps), F32),
        ],
        input_output_aliases=aliases,
        compiler_params=params(),
        cost_estimate=pl.CostEstimate(flops=steps * 1_000_000_000, bytes_accessed=steps << 21, transcendentals=0),
        name="own_pairs",
    )(meta, sup, *args)


def cross_body(lags, total, meta, sup, prior, more, x, xt, w, wt, xn, xm, wn, wm, sums_out, xl, near, deep, masks):
    group = pl.program_id(0)
    rows = xl.shape[0]
    blocks = lags - 1
    first, _, count, _ = chip_meta(meta)
    split = blocks - NEAR

    @pl.when(group == 0)
    def _():
        for p in range(blocks):
            s = p - blocks if p >= split else count - 1 - (blocks - 1 - p)
            found = readers_of(sup, first + s, total, lags)
            if p < split:
                found = jnp.where(s >= 0, found, 0)
            for k in range(lags):
                live = jnp.where(k < found, 1.0, 0.0)
                masks[k, :, p * rows : (p + 1) * rows] = jnp.full((16, rows), live, F32).astype(BF)

    for p in range(split):
        xl[:, p * rows : (p + 1) * rows] = pick(x, xt.at[0], meta, count - 1 - (blocks - 1 - p))
    for p in range(PIECE):
        xl[:, (split + p) * rows : (split + p + 1) * rows] = xm[p]
        xl[:, (split + PIECE + p) * rows : (split + PIECE + p + 1) * rows] = xn[p]
    for t in range(blocks):
        own = pick(w, wt.at[0], meta, t)
        above = jnp.clip(t - count, 0, NEAR - 1)
        halo = jnp.where(above < PIECE, wn[jnp.minimum(above, PIECE - 1)], wm[jnp.maximum(above - PIECE, 0)])
        near[t] = jnp.where(t < count, own, halo).T
    for a in range(split):
        deep[a] = (wn[a] if a < PIECE else wm[a - PIECE]).T
    back = dot(reversal(rows), xl[...]).astype(BF)
    squares = [jnp.zeros((rows, rows), F32)]
    for k in range(1, lags):
        size = min(NEAR, k)
        low = (blocks - size) * rows
        left = masked(back[:, low:], masks[k, :, low:])
        square = dot(left, near[k - size : k].reshape(size * rows, rows))
        size = k - NEAR
        if size > 0:
            low = (split - size) * rows
            left = masked(back[:, low : split * rows], masks[k, :, low : split * rows])
            square += dot(left, deep[0:size].reshape(size * rows, rows))
        squares.append(square)
    row = pl.ds(group, 1)
    sums_out[row, :] = prior[row, :] + more[row, :] + diagonal_sums(jnp.concatenate(squares, axis=1))


def cross_squares(meta, sup, prior, more, x, w, theirs, x_halos, w_halos, lags):
    slots, rows, width = x.shape
    half = width // 2
    groups = half // GROUP
    taps = prior.shape[1]
    blocks = lags - 1

    def lane(g, m, s):
        return (0, 0, m[3] * groups + g)

    halo = pl.BlockSpec((PIECE, rows, GROUP), lambda g, m, s: (0, 0, g))
    whole = pl.BlockSpec((groups, taps), lambda g, m, s: (0, 0))
    return pl.pallas_call(
        functools.partial(cross_body, lags, sup.shape[0]),
        grid_spec=pltpu.PrefetchScalarGridSpec(
            num_scalar_prefetch=2,
            grid=(groups,),
            in_specs=[
                whole,
                whole,
                pl.BlockSpec((slots, rows, GROUP), lane),
                pl.BlockSpec((1, slots, rows, GROUP), lambda g, m, s: (0, 0, 0, g)),
                pl.BlockSpec((slots, rows, GROUP), lane),
                pl.BlockSpec((1, slots, rows, GROUP), lambda g, m, s: (1, 0, 0, g)),
                halo,
                halo,
                halo,
                halo,
            ],
            out_specs=whole,
            scratch_shapes=[
                pltpu.VMEM((rows, blocks * GROUP), BF),
                pltpu.VMEM((blocks, GROUP, rows), BF),
                pltpu.VMEM((blocks - NEAR, GROUP, rows), BF),
                pltpu.VMEM((lags, 16, blocks * GROUP), BF),
            ],
        ),
        out_shape=jax.ShapeDtypeStruct((groups, taps), F32),
        compiler_params=params(),
        cost_estimate=pl.CostEstimate(flops=3_000_000_000, bytes_accessed=6 << 20, transcendentals=0),
        name="cross_squares",
    )(meta, sup, prior, more, x, theirs, w, theirs, *x_halos, *w_halos)


def near_body(lags, total, slots, chained, meta, sup, conv, adj, fwd, bwd, xn, xm, wn, wm, cot, cot_t, *rest):
    rest = rest[5:] if chained else rest
    gate_out, input_out, send_out, conv_out, adj_out, xs, ws, reach = rest
    step = pl.program_id(0)
    rows = conv.shape[1]
    cap = 2 * slots
    first, low, count, core = chip_meta(meta)
    blocks = lags - 1

    @pl.when(step == 0)
    def _():
        for i in range(blocks):
            reach[i] = sources_of(sup, first + i, total, lags)
            reach[lags + i] = readers_of(sup, first + count - 1 - i, total, lags)

    xs[0:PIECE] = xm[...]
    xs[PIECE:NEAR] = xn[...]
    ws[0:PIECE] = wn[...]
    ws[PIECE:NEAR] = wm[...]
    for i in range(blocks):
        farthest = min(blocks, i + NEAR)
        start = (blocks - farthest) * rows
        size = (farthest - i) * rows
        mask = column_mask(size, (lags - reach[i]) * rows - start, lags * rows)
        left = masked(fwd[0, :, start : start + size], mask)
        conv[i] += dot(left, xs[i + NEAR - farthest : NEAR].reshape(size, rows))
    for c in range(blocks):
        s = count - 1 - c
        tiles = min(NEAR, blocks - c)
        size = tiles * rows
        start = (c + 1) * rows
        mask = column_mask(size, 0, reach[lags + c] * rows - start)
        term = dot(masked(bwd[0, :, start : start + size], mask), ws[0:tiles].reshape(size, rows))

        @pl.when(s >= 0)
        def _():
            adj[jnp.maximum(s, 0)] += term

    for i in range(blocks - NEAR):
        conv_out[i] = conv[i]
        adj_out[i] = adj[jnp.maximum(count - 1 - i, 0)]
    high = count - low
    for slot in range(slots):
        for own in (True, False):
            second = core if own else 1 - core
            index = jnp.minimum(slot + second * low, cap - 1)
            live = slot < jnp.where(second == 1, high, low)
            cot_tile = (cot if own else cot_t)[slot]
            grad = jnp.where(live, cot_tile.astype(F32) * conv[index], 0.0).astype(BF)
            back = jnp.where(live, adj[index], 0.0).astype(BF)
            if own:
                gate_out[slot] = grad
                input_out[slot] = back
            else:
                send_out[0, slot] = grad
                send_out[1, slot] = back


def near_pairs(meta, sup, conv, adj, fwd, bwd, x_halos, w_halos, cot, cot_theirs, lags, base, steps, prior):
    slots, rows, width = cot.shape
    half = width // 2
    groups = half // GROUP
    taps = fwd.shape[2]
    far = lags - 1 - NEAR

    def lane(g, m, s):
        return (0, 0, m[3] * groups + base + g)

    def plain(tiles):
        return pl.BlockSpec((tiles, rows, GROUP), lambda g, m, s: (0, 0, base + g))

    bands = pl.BlockSpec((1, rows, taps), lambda g, m, s: (base + g, 0, 0))
    own = pl.BlockSpec((slots, rows, GROUP), lane)
    in_specs = [plain(2 * slots), plain(2 * slots), bands, bands] + [plain(PIECE)] * 4 + [own, plain(slots)]
    args = [conv, adj, fwd, bwd, *x_halos, *w_halos, cot, cot_theirs]
    chained = prior is not None
    aliases = {}
    if chained:
        aliases = {2 + len(args) + i: i for i in range(5)}
        in_specs += [pl.BlockSpec(memory_space=pl.ANY)] * 5
        args += list(prior)
    return pl.pallas_call(
        functools.partial(near_body, lags, sup.shape[0], slots, chained),
        grid_spec=pltpu.PrefetchScalarGridSpec(
            num_scalar_prefetch=2,
            grid=(steps,),
            in_specs=in_specs,
            out_specs=[
                own,
                own,
                pl.BlockSpec((2, slots, rows, GROUP), lambda g, m, s: (0, 0, 0, base + g)),
                plain(far),
                plain(far),
            ],
            scratch_shapes=[
                pltpu.VMEM((NEAR, rows, GROUP), BF),
                pltpu.VMEM((NEAR, rows, GROUP), BF),
                pltpu.SMEM((2 * lags,), jnp.int32),
            ],
        ),
        out_shape=[
            jax.ShapeDtypeStruct(cot.shape, BF),
            jax.ShapeDtypeStruct(cot.shape, BF),
            jax.ShapeDtypeStruct((2, slots, rows, half), BF),
            jax.ShapeDtypeStruct((far, rows, half), F32),
            jax.ShapeDtypeStruct((far, rows, half), F32),
        ],
        input_output_aliases=aliases,
        compiler_params=params(),
        cost_estimate=pl.CostEstimate(flops=steps * 400_000_000, bytes_accessed=steps << 21, transcendentals=0),
        name="near_pairs",
    )(meta, sup, *args)


def far_body(lags, total, meta, sup, conv, adj, fwd, bwd, xa, xb, wa, wb, cot, cot_t, gate_in, input_in, send_in,
             gate_out, input_out, send_out, xs, ws, done, reach, sems):
    step = pl.program_id(0)
    far, rows, half = done.shape[0] // 2, done.shape[1], done.shape[2]
    first, _, count, core = chip_meta(meta)

    @pl.when(step == 0)
    def _():
        for i in range(far):
            reach[i] = sources_of(sup, first + i, total, lags)
            reach[lags + i] = readers_of(sup, first + count - 1 - i, total, lags)

    xs[0 : far - PIECE] = xb[...]
    xs[far - PIECE : far] = xa[...]
    ws[0:PIECE] = wa[...]
    ws[PIECE:far] = wb[...]
    lanes = pl.ds(pl.multiple_of(step * GROUP, GROUP), GROUP)
    for i in range(far):
        size = (far - i) * rows
        mask = column_mask(size, (lags - reach[i]) * rows, lags * rows)
        total_conv = conv[i] + dot(masked(fwd[0, :, :size], mask), xs[i:far].reshape(size, rows))
        done[i, :, lanes] = (pick(cot, cot_t, meta, i).astype(F32) * total_conv).astype(BF)
    for c in range(far):
        start = (c + NEAR + 1) * rows
        size = (far - c) * rows
        mask = column_mask(size, 0, reach[lags + c] * rows - start)
        term = dot(masked(bwd[0, :, start:], mask), ws[0 : far - c].reshape(size, rows))
        done[far + c, :, lanes] = (adj[c] + term).astype(BF)

    @pl.when(step == pl.num_programs(0) - 1)
    def _():
        home = pl.ds(pl.multiple_of(core * half, half), half)
        for r in range(2 * far):
            index = r if r < far else count - 1 - (r - far)
            mine, slot = place(meta, index)
            out = gate_out if r < far else input_out

            @pl.when(mine)
            def _():
                pltpu.make_async_copy(done.at[r], out.at[slot, :, home], sems.at[r]).start()

            @pl.when(jnp.logical_not(mine))
            def _():
                pltpu.make_async_copy(done.at[r], send_out.at[r // far, slot], sems.at[r]).start()

        for r in range(2 * far):
            pltpu.make_async_copy(done.at[r], send_out.at[r // far, 0], sems.at[r]).wait()


def far_pairs(meta, sup, conv, adj, fwd, bwd, x_halos, w_halos, cot, cot_theirs, gate, inp, send, lags):
    slots, rows, width = cot.shape
    half = width // 2
    groups = half // GROUP
    taps = fwd.shape[2]
    far = lags - 1 - NEAR

    def plain(tiles):
        return pl.BlockSpec((tiles, rows, GROUP), lambda g, m, s: (0, 0, g))

    bands = pl.BlockSpec((1, rows, taps), lambda g, m, s: (g, 0, 0))
    own = pl.BlockSpec((slots, rows, GROUP), lambda g, m, s: (0, 0, m[3] * groups + g))
    loose = pl.BlockSpec(memory_space=pl.ANY)
    return pl.pallas_call(
        functools.partial(far_body, lags, sup.shape[0]),
        grid_spec=pltpu.PrefetchScalarGridSpec(
            num_scalar_prefetch=2,
            grid=(groups,),
            in_specs=[
                plain(far),
                plain(far),
                bands,
                bands,
                plain(PIECE),
                plain(far - PIECE),
                plain(PIECE),
                plain(far - PIECE),
                own,
                plain(slots),
                loose,
                loose,
                loose,
            ],
            out_specs=[loose, loose, loose],
            scratch_shapes=[
                pltpu.VMEM((far, rows, GROUP), BF),
                pltpu.VMEM((far, rows, GROUP), BF),
                pltpu.VMEM((2 * far, rows, half), BF),
                pltpu.SMEM((2 * lags,), jnp.int32),
                pltpu.SemaphoreType.DMA((2 * far,)),
            ],
        ),
        out_shape=[
            jax.ShapeDtypeStruct(gate.shape, BF),
            jax.ShapeDtypeStruct(inp.shape, BF),
            jax.ShapeDtypeStruct(send.shape, BF),
        ],
        input_output_aliases={12: 0, 13: 1, 14: 2},
        compiler_params=params(),
        cost_estimate=pl.CostEstimate(flops=800_000_000, bytes_accessed=8 << 20, transcendentals=0),
        name="far_pairs",
    )(meta, sup, conv, adj, fwd, bwd, *x_halos, *w_halos, cot, cot_theirs, gate, inp, send)


def join_body(meta, gate_in, input_in, got, gate_out, input_out, sems):
    half = got.shape[3]
    other = pl.ds(pl.multiple_of((1 - meta[3]) * half, half), half)
    copies = [
        pltpu.make_async_copy(got.at[0], gate_out.at[:, :, other], sems.at[0]),
        pltpu.make_async_copy(got.at[1], input_out.at[:, :, other], sems.at[1]),
    ]
    for copy in copies:
        copy.start()
    for copy in copies:
        copy.wait()


def join(meta, gate, inp, got):
    loose = pl.BlockSpec(memory_space=pl.ANY)
    return pl.pallas_call(
        join_body,
        grid_spec=pltpu.PrefetchScalarGridSpec(
            num_scalar_prefetch=1,
            grid=(1,),
            in_specs=[loose, loose, loose],
            out_specs=[loose, loose],
            scratch_shapes=[pltpu.SemaphoreType.DMA((2,))],
        ),
        out_shape=[jax.ShapeDtypeStruct(gate.shape, BF)] * 2,
        input_output_aliases={1: 0, 2: 1},
        compiler_params=params(),
        name="join",
    )(meta, gate, inp, got)


def per_device(conv_input, gate_signal, cotangent, filters, tile_owner, support):
    slots, rows, width = conv_input.shape
    lags = support.shape[1]
    filter_count, taps = filters.shape
    total = tile_owner.shape[0]
    tie = lax.optimization_barrier
    me = lax.axis_index("ctx")
    core = me % 2
    entry = jnp.arange(8, dtype=jnp.int32)
    before = jnp.sum((tile_owner[None, :] < (me - core + entry)[:, None]).astype(jnp.int32), axis=1)
    meta = jnp.where(entry == 3, core, before)

    def up(value):
        return shifted(value, "ctx", 2)

    def down(value):
        return shifted(value, "ctx", -2)

    w, send, cot_send = prep(meta, gate_signal, cotangent, conv_input)
    theirs = swapped(send, "ctx", 1)
    x, flip = conv_input, filters[:, ::-1]
    xs, ws = pack(meta, x, w, theirs, 2, lambda j, n: n - 2 + j, lambda j, n: j)
    x0, w0 = up(xs), down(ws)
    xs, ws = pack(meta, x, w, theirs, 2, lambda j, n: n - 4 + j, lambda j, n: 2 + j)
    x1, w1 = up(xs), down(ws)
    cot_theirs = swapped(cot_send, "ctx", 1)
    half_groups = width // 2 // GROUP // 2
    one = own_pairs(meta, support, filters, flip, x, w, theirs, lags, 0, half_groups, None)
    x0, w0, one = tie((x0, w0, one))
    xs, ws = pack(meta, x, w, theirs, 2, lambda j, n: n - 6 + j, lambda j, n: 4 + j, (x0,), (w0,))
    xs, ws, one = tie((xs, ws, one))
    x2, w2 = up(xs), down(ws)
    *parts, first_sums = one
    *parts, sums = own_pairs(
        meta, support, filters, flip, x, w, theirs, lags, half_groups, half_groups, parts
    )
    x1, w1, parts, sums = tie((x1, w1, parts, sums))
    conv, adj, fwd, bwd = parts
    sums = cross_squares(meta, support, sums, first_sums, x, w, theirs, (x0, x1), (w0, w1), lags)

    def step(sums, axis, mask, filler):
        moved = swapped(sums, axis, mask)
        if filler is None:
            return sums + moved, None
        sums, out = tie((sums + moved, filler(sums)))
        return sums, out

    def relay(sums):
        _, a, b = tie((sums, x0, x1))
        return pack(meta, x, w, theirs, 1, lambda j, n: n - 7 + j, lambda j, n: 6 + j, (a, b), (w0, w1))

    sums, (xs, ws) = step(sums, "ctx", 2, relay)
    x3, w3 = up(xs), down(ws)

    def close(base, prior):
        def run(sums):
            _, c = tie((sums, conv))
            return near_pairs(
                meta, support, c, adj, fwd, bwd, (x0, x1), (w0, w1), cotangent, cot_theirs, lags,
                base, half_groups, prior,
            )

        return run

    sums, near = step(sums, "ctx", 4, close(0, None))
    sums, near = step(sums, "ch", 1, close(half_groups, near))
    gate, inp, back, conv, adj = near
    sums, _ = step(sums, "ch", 2, None)

    def finish(sums):
        _, c = tie((sums, conv))
        return far_pairs(
            meta, support, c, adj, fwd, bwd, (x2, x3), (w2, w3), cotangent, cot_theirs, gate, inp, back, lags
        )

    sums, (gate, inp, back) = step(sums, "ctx", 8, finish)
    got = swapped(back, "ctx", 1)
    sums, _ = step(sums, "ctx", 16, None)
    sums, _ = step(sums, "ctx", 32, None)
    gate, inp = join(meta, gate, inp, got)
    norm = 1.0 / math.sqrt(total * rows * width * lax.axis_size("ch") / filter_count)
    sums = sums * norm
    partner = swapped(sums, "ctx", 1)
    low = jnp.where(core == 0, sums, partner)
    high = jnp.where(core == 0, partner, sums)
    return gate, inp, jnp.concatenate([low, high], axis=0)


def solution(mesh):
    return jax.shard_map(
        per_device,
        mesh=mesh,
        in_specs=(P("ctx", None, "ch"), P("ctx", None, "ch"), P("ctx", None, "ch"), P(), P(), P()),
        out_specs=(P("ctx", None, "ch"), P("ctx", None, "ch"), P()),
        check_vma=False,
    )
```

time: 151 us -> 216 us (1.43)
  Pallas kernels: 72.4 us -> 133 us
  starting transfers between devices: 42.6 us -> 60.5 us
  waiting for transfers between devices: 23 us -> 10.7 us
    pallas_call x5 -> x10, Pallas kernels: 51 us -> 120 us  [the longest x1 65.2 us: join(): pl.pallas_call(join_body, grid_spec=pltpu.PrefetchScalarGridSpec(num_scal...]
    ppermute x4 -> x8, starting transfers between devices: 7.28 us -> 19.5 us  [shifted(): return lax.ppermute(value, axis, pairs)]
    ppermute x11, waiting for transfers between devices: 17.3 us -> 10.7 us  [swapped(): return lax.ppermute(value, axis, [(a, a ^ mask) for a in range(count)])]
    ppermute x4 -> x8, waiting for transfers between devices: 5.74 us -> 0.02 us  [shifted(): return lax.ppermute(value, axis, pairs)]
    ppermute x11, starting transfers between devices: 35.3 us -> 41 us  [swapped(): return lax.ppermute(value, axis, [(a, a ^ mask) for a in range(count)])]
    pallas_call x1, Pallas kernels: 6.46 us -> 2.07 us  [prep(): pl.pallas_call(prep_body, grid_spec=pltpu.PrefetchScalarGridSpec(num_scal...]
    pallas_call x1, Pallas kernels: 15 us -> 10.9 us  [cross_squares(): pl.pallas_call(functools.partial(cross_body, lags, sup.shape[0]), grid_sp...]
    unnamed x21 -> x19, local copies, waits for them, and re-layouts: 5.66 us -> 8.08 us
  transfers between devices with their start and end apart: 15 -> 19, of which waited for: 11 -> 6; matrix products, arithmetic and copies ran while one was open for 3% -> 1% of each run, Pallas kernels for 25% -> 26%
where the time goes in v2:
time: 216 us; the launch traced here: 215 us
  Pallas kernels  133 us (62%)
  starting transfers between devices  60.5 us (28%)
  waiting for transfers between devices  10.7 us (5%)
  local copies, waits for them, and re-layouts  8.65 us (4%)
    pallas_call x1, Pallas kernels, join(): pl.pallas_call(join_body, grid_spec=pltpu.PrefetchScalarGridSpec(num_scal...  65.2 us
    ppermute x11, starting transfers between devices, swapped(): return lax.ppermute(value, axis, [(a, a ^ mask) for a in range(count)])  41 us
    pallas_call x2, Pallas kernels, near_pairs(): pl.pallas_call(functools.partial(near_body, lags, sup.shape[0], slots, ch...  22.4 us
    pallas_call x2, Pallas kernels, own_pairs(): pl.pallas_call(functools.partial(own_body, lags, total, base, chained), g...  19.9 us
    ppermute x8, starting transfers between devices, shifted(): return lax.ppermute(value, axis, pairs)  19.5 us
    pallas_call x1, Pallas kernels, cross_squares(): pl.pallas_call(functools.partial(cross_body, lags, sup.shape[0]), grid_sp...  10.9 us
    ppermute x11, waiting for transfers between devices, swapped(): return lax.ppermute(value, axis, [(a, a ^ mask) for a in range(count)])  10.7 us
    unnamed x19, local copies, waits for them, and re-layouts  8.08 us
  transfers between devices with their start and end apart: 19, of which 6 were waited for; matrix products, arithmetic and copies ran while one was open for 1% of the time, Pallas kernels for 26%

profile of v2, /device:TPU:1, one launch (start us, length us, event | category | flops | bytes accessed | tf_op | source)
XLA Modules:
  0.0 215.1 jit_solution(157616312445115986)
XLA Ops:
  1.5 1.6 copy-done
  3.1 1.6 copy-done.4
  4.7 1.6 copy-done.6
  6.3 2.1 prep.1
  8.4 3.3 %collective-permute-start = (bf16[2,4,128,1024]{3,2,1,0:T(8,128)(2,1)S(1)}, bf16[2,4,128,1024]{3,2,1,0:T(8,128)(2,1)S(1)}, u32[]{:S(2)}, u32[]{:S(2)}) collective-permute-start(bf16[2,4,128,1024]{3,2,1,0:T(8,128)(2,1)S(1)} %get-tuple-element.85), channel_id=1, source_target_pairs={{0,4},{4,0},{8,12},{12,8},{16,20},{20,16},{24,28},{28,24},{32,36},... | collective-permute-start | bytes 6291464 | tf_op jit(solution)/shard_map/ppermute | solution.py:31
  11.7 3.8 %collective-permute-done.theirs.xt.wt = bf16[2,4,128,1024]{3,2,1,0:T(8,128)(2,1)S(1)} collective-permute-done((bf16[2,4,128,1024]{3,2,1,0:T(8,128)(2,1)S(1)}, bf16[2,4,128,1024]{3,2,1,0:T(8,128)(2,1)S(1)}, u32[]{:S(2)}, u32[]{:S(2)}) %collective-permute-start) | collective-permute-done | bytes 2097184 | tf_op jit(solution)/shard_map/ppermute | solution.py:31
  15.5 1.6 pack.5
  17.1 2.3 %collective-permute-start.3 = (bf16[2,128,1024]{2,1,0:T(8,128)(2,1)}, bf16[2,128,1024]{2,1,0:T(8,128)(2,1)}, u32[]{:S(2)}, u32[]{:S(2)}) collective-permute-start(bf16[2,128,1024]{2,1,0:T(8,128)(2,1)} %get-tuple-element.88), channel_id=1, source_target_pairs={{0,8},{4,12},{8,16},{12,20},{16,24},{20,28},{24,32},{28,36},{32,40... | collective-permute-start | bytes 1572872 | tf_op jit(solution)/shard_map/ppermute | solution.py:26
  22.1 1.6 copy-done.1
  23.7 1.6 copy-done.3
  26.0 4.3 %collective-permute-start.1 = (bf16[2,128,1024]{2,1,0:T(8,128)(2,1)S(1)}, bf16[2,128,1024]{2,1,0:T(8,128)(2,1)S(1)}, u32[]{:S(2)}, u32[]{:S(2)}) collective-permute-start(bf16[2,128,1024]{2,1,0:T(8,128)(2,1)S(1)} %get-tuple-element.86), channel_id=1, source_target_pairs={{0,8},{4,12},{8,16},{12,20},{16,24},{20,28},{24,32},{28,36},{32,40... | collective-permute-start | bytes 1572872 | tf_op jit(solution)/shard_map/ppermute | solution.py:26
  31.6 10.0 %own_pairs.2 = (f32[8,128,1024]{2,1,0:T(8,128)S(1)}, f32[8,128,1024]{2,1,0:T(8,128)S(1)}, bf16[8,128,1024]{2,1,0:T(8,128)(2,1)S(1)}, bf16[8,128,1024]{2,1,0:T(8,128)(2,1)S(1)}, f32[8,1024]{1,0:T(8,128)S(1)}) custom-call(s32[8]{0:T(128)S(1)} %compare_select_fusion.meta, s32[192,8]{1,0:T(8,128)S(1)} %copy.31.sup, f32[16,1024]{1,0:T(8,128)S(1)} %copy-done.7, ...), custom_call_target="tpu_custom_call" | custom-call | flops 4000000000 | bytes 8388608 | tf_op jit(solution)/shard_map/own_pairs/pallas_call | solution.py:288
  42.3 10.0 %own_pairs.3 = (f32[8,128,1024]{2,1,0:T(8,128)S(1)}, f32[8,128,1024]{2,1,0:T(8,128)S(1)}, bf16[8,128,1024]{2,1,0:T(8,128)(2,1)S(1)}, bf16[8,128,1024]{2,1,0:T(8,128)(2,1)S(1)}, f32[8,1024]{1,0:T(8,128)S(1)}) custom-call(s32[8]{0:T(128)S(1)} %compare_select_fusion.meta, ...), custom_call_target="tpu_custom_call", output_to_operand_aliasing={{0}: (8, {}), {1}: (9, {}), {2}: (10, {}), {3}: (11, {})} | custom-call | flops 4000000000 | bytes 8388608 | tf_op jit(solution)/shard_map/own_pairs/pallas_call | solution.py:288
  52.3 5.0 %collective-permute-start.11 = (bf16[2,128,1024]{2,1,0:T(8,128)(2,1)S(1)}, bf16[2,128,1024]{2,1,0:T(8,128)(2,1)S(1)}, u32[]{:S(2)}, u32[]{:S(2)}) collective-permute-start(bf16[2,128,1024]{2,1,0:T(8,128)(2,1)S(1)} %get-tuple-element.149), channel_id=1, source_target_pairs={{0,8},{4,12},{8,16},{12,20},{16,24},{20,28},{24,32},{28,36},{32,40... | collective-permute-start | bytes 1572872 | tf_op jit(solution)/shard_map/ppermute | solution.py:26
  58.6 10.9 %cross_squares.1 = f32[8,1024]{1,0:T(8,128)S(1)} custom-call(s32[8]{0:T(128)S(1)} %compare_select_fusion.meta, s32[192,8]{1,0:T(8,128)S(1)} %copy.31.sup, f32[8,1024]{1,0:T(8,128)S(1)} %get-tuple-element.113.prior, f32[8,1024]{1,0:T(8,128)S(1)} %get-tuple-element.114.more, bf16[4,128,2048]{2,1,0:T(8,128)(2,1)S(1)} %copy-done.1, ...), custom_call_target="tpu_custom_call" | custom-call | flops 3000000000 | bytes 6291456 | tf_op jit(solution)/shard_map/cross_squares/pallas_call | solution.py:377
  69.5 2.2 %collective-permute-start.5 = (f32[8,1024]{1,0:T(8,128)S(1)}, f32[8,1024]{1,0:T(8,128)S(1)}, u32[]{:S(2)}, u32[]{:S(2)}) collective-permute-start(f32[8,1024]{1,0:T(8,128)S(1)} %cross_squares.1), channel_id=1, source_target_pairs={{0,8},{4,12},{8,0},{12,4},{16,24},{20,28},{24,16},{28,20},{32,40},... | collective-permute-start | bytes 98312 | tf_op jit(solution)/shard_map/ppermute | solution.py:31
  71.7 1.6 pack.7
  73.3 4.8 %collective-permute-start.6 = (f32[8,1024]{1,0:T(8,128)S(1)}, f32[8,1024]{1,0:T(8,128)S(1)}, u32[]{:S(2)}, u32[]{:S(2)}) collective-permute-start(f32[8,1024]{1,0:T(8,128)S(1)} %add.38), channel_id=1, source_target_pairs={{0,16},{4,20},{8,24},{12,28},{16,0},{20,4},{24,8},{28,12},{32,48},... | collective-permute-start | bytes 98312 | tf_op jit(solution)/shard_map/ppermute | solution.py:31
  78.1 2.8 %collective-permute-start.12 = (bf16[1,128,1024]{2,1,0:T(8,128)(2,1)S(1)}, bf16[1,128,1024]{2,1,0:T(8,128)(2,1)S(1)}, u32[]{:S(2)}, u32[]{:S(2)}) collective-permute-start(bf16[1,128,1024]{2,1,0:T(8,128)(2,1)S(1)} %get-tuple-element.150), channel_id=1, source_target_pairs={{0,8},{4,12},{8,16},{12,20},{16,24},{20,28},{24,32},{28,36},{32,40... | collective-permute-start | bytes 786440 | tf_op jit(solution)/shard_map/ppermute | solution.py:26
  82.3 11.2 %near_pairs.2 = (bf16[4,128,2048]{2,1,0:T(8,128)(2,1)}, bf16[4,128,2048]{2,1,0:T(8,128)(2,1)}, bf16[2,4,128,1024]{3,2,1,0:T(8,128)(2,1)S(1)}, f32[3,128,1024]{2,1,0:T(8,128)S(1)}, f32[3,128,1024]{2,1,0:T(8,128)S(1)}) custom-call(s32[8]{0:T(128)S(1)} %compare_select_fusion.meta, s32[192,8]{1,0:T(8,128)S(1)} %copy.31.sup, ...), custom_call_target="tpu_custom_call" | custom-call | flops 1600000000 | bytes 8388608 | tf_op jit(solution)/shard_map/near_pairs/pallas_call | solution.py:490
  93.5 1.5 collective-permute-start.8
  95.0 11.2 %near_pairs.3 = (bf16[4,128,2048]{2,1,0:T(8,128)(2,1)}, bf16[4,128,2048]{2,1,0:T(8,128)(2,1)}, bf16[2,4,128,1024]{3,2,1,0:T(8,128)(2,1)S(1)}, f32[3,128,1024]{2,1,0:T(8,128)S(1)}, f32[3,128,1024]{2,1,0:T(8,128)S(1)}) custom-call(s32[8]{0:T(128)S(1)} %compare_select_fusion.meta, ...), custom_call_target="tpu_custom_call", output_to_operand_aliasing={{0}: (12, {}), {1}: (13, {}), {2}: (14, {}), {3}: (15, {}),... | custom-call | flops 1600000000 | bytes 8388608 | tf_op jit(solution)/shard_map/near_pairs/pallas_call | solution.py:490
  106.2 2.5 %collective-permute-start.9 = (f32[8,1024]{1,0:T(8,128)S(1)}, f32[8,1024]{1,0:T(8,128)S(1)}, u32[]{:S(2)}, u32[]{:S(2)}) collective-permute-start(f32[8,1024]{1,0:T(8,128)S(1)} %add.40), channel_id=1, source_target_pairs={{0,2},{1,3},{2,0},{3,1},{4,6},{5,7},{6,4},{7,5},{8,10},{9,11},{10,... | collective-permute-start | bytes 98312 | tf_op jit(solution)/shard_map/ppermute | solution.py:31
  108.7 1.8 collective-permute-done.9
  110.6 5.0 %collective-permute-start.10 = (f32[8,1024]{1,0:T(8,128)S(1)}, f32[8,1024]{1,0:T(8,128)S(1)}, u32[]{:S(2)}, u32[]{:S(2)}) collective-permute-start(f32[8,1024]{1,0:T(8,128)S(1)} %add.41), channel_id=1, source_target_pairs={{0,32},{4,36},{8,40},{12,44},{16,48},{20,52},{24,56},{28,60},{32,0... | collective-permute-start | bytes 98312 | tf_op jit(solution)/shard_map/ppermute | solution.py:31
  116.9 7.4 %far_pairs.1 = (bf16[4,128,2048]{2,1,0:T(8,128)(2,1)}, bf16[4,128,2048]{2,1,0:T(8,128)(2,1)}, bf16[2,4,128,1024]{3,2,1,0:T(8,128)(2,1)S(1)}) custom-call(s32[8]{0:T(128)S(1)} %compare_select_fusion.meta, s32[192,8]{1,0:T(8,128)S(1)} %copy.31.sup, ...), custom_call_target="tpu_custom_call", output_to_operand_aliasing={{0}: (12, {}), {1}: (13, {}), {2}: (14, {})} | custom-call | flops 800000000 | bytes 8388608 | tf_op jit(solution)/shard_map/far_pairs/pallas_call | solution.py:585
  124.3 4.8 %collective-permute-start.15 = (bf16[2,4,128,1024]{3,2,1,0:T(8,128)(2,1)S(1)}, bf16[2,4,128,1024]{3,2,1,0:T(8,128)(2,1)}, u32[]{:S(2)}, u32[]{:S(2)}) collective-permute-start(bf16[2,4,128,1024]{3,2,1,0:T(8,128)(2,1)S(1)} %get-tuple-element.161), channel_id=1, source_target_pairs={{0,4},{4,0},{8,12},{12,8},{16,20},{20,16},{24,28},{28,24},{32,36},... | collective-permute-start | bytes 6291464 | tf_op jit(solution)/shard_map/ppermute | solution.py:31
  129.1 6.6 %collective-permute-start.16 = (f32[8,1024]{1,0:T(8,128)S(1)}, f32[8,1024]{1,0:T(8,128)S(1)}, u32[]{:S(2)}, u32[]{:S(2)}) collective-permute-start(f32[8,1024]{1,0:T(8,128)S(1)} %add.42), channel_id=1, source_target_pairs={{0,64},{4,68},{8,72},{12,76},{16,80},{20,84},{24,88},{28,92},{32,9... | collective-permute-start | bytes 98312 | tf_op jit(solution)/shard_map/ppermute | solution.py:31
  135.7 1.6 collective-permute-done.16
  137.3 8.1 %collective-permute-start.17 = (f32[8,1024]{1,0:T(8,128)S(1)}, f32[8,1024]{1,0:T(8,128)S(1)}, u32[]{:S(2)}, u32[]{:S(2)}) collective-permute-start(f32[8,1024]{1,0:T(8,128)S(1)} %add.43), channel_id=1, source_target_pairs={{0,128},{4,132},{8,136},{12,140},{16,144},{20,148},{24,152},{28,15... | collective-permute-start | bytes 98312 | tf_op jit(solution)/shard_map/ppermute | solution.py:31
  146.8 1.5 collective-permute-start.18
  149.7 65.2 %join.1 = (bf16[4,128,2048]{2,1,0:T(8,128)(2,1)}, bf16[4,128,2048]{2,1,0:T(8,128)(2,1)}) custom-call(s32[8]{0:T(128)S(1)} %compare_select_fusion.meta, bf16[4,128,2048]{2,1,0:T(8,128)(2,1)} %get-tuple-element.159.gate_in, bf16[4,128,2048]{2,1,0:T(8,128)(2,1)} %get-tuple-element.160.input_in, ...), custom_call_target="tpu_custom_call", output_to_operand_aliasing={{0}: (1, {}), {1}: (2, {})} | custom-call | tf_op jit(solution)/shard_map/join/pallas_call | solution.py:641
  (50 shorter events, 13.1 us)
Async XLA Ops:
  1.5 1.6 copy-start
  3.1 1.6 copy-start.4
  4.7 1.6 copy-start.6
  8.4 8.7 %copy-start.2 = (bf16[4,128,2048]{2,1,0:T(8,128)(2,1)}, bf16[4,128,2048]{2,1,0:T(8,128)(2,1)S(1)}, u32[]{:S(2)}) copy-start(bf16[4,128,2048]{2,1,0:T(8,128)(2,1)S(1)} %get-tuple-element.84.w) | copy-start | bytes 6291460
  8.4 7.1 %collective-permute-start = (bf16[2,4,128,1024]{3,2,1,0:T(8,128)(2,1)S(1)}, bf16[2,4,128,1024]{3,2,1,0:T(8,128)(2,1)S(1)}, u32[]{:S(2)}, u32[]{:S(2)}) collective-permute-start(bf16[2,4,128,1024]{3,2,1,0:T(8,128)(2,1)S(1)} %get-tuple-element.85), channel_id=1, source_target_pairs={{0,4},{4,0},{8,12},{12,8},{16,20},{20,16},{24,28},{28,24},{32,36},... | collective-permute-start | bytes 6291464 | tf_op jit(solution)/shard_map/ppermute | solution.py:31
  15.5 5.9 %copy-start.7 = (f32[16,1024]{1,0:T(8,128)S(1)}, f32[16,1024]{1,0:T(8,128)}, u32[]{:S(2)}) copy-start(f32[16,1024]{1,0:T(8,128)} %filt.3) | copy-start | bytes 196612
  15.5 6.4 %copy-start.8 = (s32[192,8]{0,1:T(8,128)S(1)}, s32[192,8]{0,1:T(8,128)}, u32[]{:S(2)}) copy-start(s32[192,8]{0,1:T(8,128)} %param.11) | copy-start | bytes 18436
  17.1 24.5 %collective-permute-start.3 = (bf16[2,128,1024]{2,1,0:T(8,128)(2,1)}, bf16[2,128,1024]{2,1,0:T(8,128)(2,1)}, u32[]{:S(2)}, u32[]{:S(2)}) collective-permute-start(bf16[2,128,1024]{2,1,0:T(8,128)(2,1)} %get-tuple-element.88), channel_id=1, source_target_pairs={{0,8},{4,12},{8,16},{12,20},{16,24},{20,28},{24,32},{28,36},{32,40... | collective-permute-start | bytes 1572872 | tf_op jit(solution)/shard_map/ppermute | solution.py:26
  19.3 22.2 %collective-permute-start.4 = (bf16[2,128,1024]{2,1,0:T(8,128)(2,1)}, bf16[2,128,1024]{2,1,0:T(8,128)(2,1)}, u32[]{:S(2)}, u32[]{:S(2)}) collective-permute-start(bf16[2,128,1024]{2,1,0:T(8,128)(2,1)} %get-tuple-element.89), channel_id=1, source_target_pairs={{8,0},{12,4},{16,8},{20,12},{24,16},{28,20},{32,24},{36,28},{40,32... | collective-permute-start | bytes 1572872 | tf_op jit(solution)/shard_map/ppermute | solution.py:26
  20.6 60.3 %collective-permute-start.7 = (bf16[4,128,1024]{2,1,0:T(8,128)(2,1)}, bf16[4,128,1024]{2,1,0:T(8,128)(2,1)S(1)}, u32[]{:S(2)}, u32[]{:S(2)}) collective-permute-start(bf16[4,128,1024]{2,1,0:T(8,128)(2,1)} %get-tuple-element.127), channel_id=1, source_target_pairs={{0,4},{4,0},{8,12},{12,8},{16,20},{20,16},{24,28},{28,24},{32,36},... | collective-permute-start | bytes 3145736 | tf_op jit(solution)/shard_map/ppermute | solution.py:31
  22.1 1.6 copy-start.1
  23.7 1.6 copy-start.3
  26.0 26.3 %collective-permute-start.1 = (bf16[2,128,1024]{2,1,0:T(8,128)(2,1)S(1)}, bf16[2,128,1024]{2,1,0:T(8,128)(2,1)S(1)}, u32[]{:S(2)}, u32[]{:S(2)}) collective-permute-start(bf16[2,128,1024]{2,1,0:T(8,128)(2,1)S(1)} %get-tuple-element.86), channel_id=1, source_target_pairs={{0,8},{4,12},{8,16},{12,20},{16,24},{20,28},{24,32},{28,36},{32,40... | collective-permute-start | bytes 1572872 | tf_op jit(solution)/shard_map/ppermute | solution.py:26
  30.3 22.0 %collective-permute-start.2 = (bf16[2,128,1024]{2,1,0:T(8,128)(2,1)S(1)}, bf16[2,128,1024]{2,1,0:T(8,128)(2,1)S(1)}, u32[]{:S(2)}, u32[]{:S(2)}) collective-permute-start(bf16[2,128,1024]{2,1,0:T(8,128)(2,1)S(1)} %get-tuple-element.87), channel_id=1, source_target_pairs={{8,0},{12,4},{16,8},{20,12},{24,16},{28,20},{32,24},{36,28},{40,32... | collective-permute-start | bytes 1572872 | tf_op jit(solution)/shard_map/ppermute | solution.py:26
  52.3 64.5 %collective-permute-start.11 = (bf16[2,128,1024]{2,1,0:T(8,128)(2,1)S(1)}, bf16[2,128,1024]{2,1,0:T(8,128)(2,1)S(1)}, u32[]{:S(2)}, u32[]{:S(2)}) collective-permute-start(bf16[2,128,1024]{2,1,0:T(8,128)(2,1)S(1)} %get-tuple-element.149), channel_id=1, source_target_pairs={{0,8},{4,12},{8,16},{12,20},{16,24},{20,28},{24,32},{28,36},{32,40... | collective-permute-start | bytes 1572872 | tf_op jit(solution)/shard_map/ppermute | solution.py:26
  57.3 59.6 %collective-permute-start.13 = (bf16[2,128,1024]{2,1,0:T(8,128)(2,1)S(1)}, bf16[2,128,1024]{2,1,0:T(8,128)(2,1)S(1)}, u32[]{:S(2)}, u32[]{:S(2)}) collective-permute-start(bf16[2,128,1024]{2,1,0:T(8,128)(2,1)S(1)} %get-tuple-element.151), channel_id=1, source_target_pairs={{8,0},{12,4},{16,8},{20,12},{24,16},{28,20},{32,24},{36,28},{40,32... | collective-permute-start | bytes 1572872 | tf_op jit(solution)/shard_map/ppermute | solution.py:26
  69.5 12.8 %copy-start.5 = (bf16[4,128,2048]{2,1,0:T(8,128)(2,1)S(1)}, bf16[4,128,2048]{2,1,0:T(8,128)(2,1)}, u32[]{:S(2)}) copy-start(bf16[4,128,2048]{2,1,0:T(8,128)(2,1)} %cot.7) | copy-start | bytes 6291460
  69.5 3.8 %collective-permute-start.5 = (f32[8,1024]{1,0:T(8,128)S(1)}, f32[8,1024]{1,0:T(8,128)S(1)}, u32[]{:S(2)}, u32[]{:S(2)}) collective-permute-start(f32[8,1024]{1,0:T(8,128)S(1)} %cross_squares.1), channel_id=1, source_target_pairs={{0,8},{4,12},{8,0},{12,4},{16,24},{20,28},{24,16},{28,20},{32,40},... | collective-permute-start | bytes 98312 | tf_op jit(solution)/shard_map/ppermute | solution.py:31
  73.3 20.2 %collective-permute-start.6 = (f32[8,1024]{1,0:T(8,128)S(1)}, f32[8,1024]{1,0:T(8,128)S(1)}, u32[]{:S(2)}, u32[]{:S(2)}) collective-permute-start(f32[8,1024]{1,0:T(8,128)S(1)} %add.38), channel_id=1, source_target_pairs={{0,16},{4,20},{8,24},{12,28},{16,0},{20,4},{24,8},{28,12},{32,48},... | collective-permute-start | bytes 98312 | tf_op jit(solution)/shard_map/ppermute | solution.py:31
  78.1 38.7 %collective-permute-start.12 = (bf16[1,128,1024]{2,1,0:T(8,128)(2,1)S(1)}, bf16[1,128,1024]{2,1,0:T(8,128)(2,1)S(1)}, u32[]{:S(2)}, u32[]{:S(2)}) collective-permute-start(bf16[1,128,1024]{2,1,0:T(8,128)(2,1)S(1)} %get-tuple-element.150), channel_id=1, source_target_pairs={{0,8},{4,12},{8,16},{12,20},{16,24},{20,28},{24,32},{28,36},{32,40... | collective-permute-start | bytes 786440 | tf_op jit(solution)/shard_map/ppermute | solution.py:26
  81.0 35.8 %collective-permute-start.14 = (bf16[1,128,1024]{2,1,0:T(8,128)(2,1)S(1)}, bf16[1,128,1024]{2,1,0:T(8,128)(2,1)S(1)}, u32[]{:S(2)}, u32[]{:S(2)}) collective-permute-start(bf16[1,128,1024]{2,1,0:T(8,128)(2,1)S(1)} %get-tuple-element.152), channel_id=1, source_target_pairs={{8,0},{12,4},{16,8},{20,12},{24,16},{28,20},{32,24},{36,28},{40,32... | collective-permute-start | bytes 786440 | tf_op jit(solution)/shard_map/ppermute | solution.py:26
  93.5 12.7 %collective-permute-start.8 = (f32[8,1024]{1,0:T(8,128)S(1)}, f32[8,1024]{1,0:T(8,128)S(1)}, u32[]{:S(2)}, u32[]{:S(2)}) collective-permute-start(f32[8,1024]{1,0:T(8,128)S(1)} %add.39), channel_id=1, source_target_pairs={{0,1},{1,0},{2,3},{3,2},{4,5},{5,4},{6,7},{7,6},{8,9},{9,8},{10,11... | collective-permute-start | bytes 98312 | tf_op jit(solution)/shard_map/ppermute | solution.py:31
  106.2 4.4 %collective-permute-start.9 = (f32[8,1024]{1,0:T(8,128)S(1)}, f32[8,1024]{1,0:T(8,128)S(1)}, u32[]{:S(2)}, u32[]{:S(2)}) collective-permute-start(f32[8,1024]{1,0:T(8,128)S(1)} %add.40), channel_id=1, source_target_pairs={{0,2},{1,3},{2,0},{3,1},{4,6},{5,7},{6,4},{7,5},{8,10},{9,11},{10,... | collective-permute-start | bytes 98312 | tf_op jit(solution)/shard_map/ppermute | solution.py:31
  110.6 6.3 %collective-permute-start.10 = (f32[8,1024]{1,0:T(8,128)S(1)}, f32[8,1024]{1,0:T(8,128)S(1)}, u32[]{:S(2)}, u32[]{:S(2)}) collective-permute-start(f32[8,1024]{1,0:T(8,128)S(1)} %add.41), channel_id=1, source_target_pairs={{0,32},{4,36},{8,40},{12,44},{16,48},{20,52},{24,56},{28,60},{32,0... | collective-permute-start | bytes 98312 | tf_op jit(solution)/shard_map/ppermute | solution.py:31
  124.3 25.4 %collective-permute-start.15 = (bf16[2,4,128,1024]{3,2,1,0:T(8,128)(2,1)S(1)}, bf16[2,4,128,1024]{3,2,1,0:T(8,128)(2,1)}, u32[]{:S(2)}, u32[]{:S(2)}) collective-permute-start(bf16[2,4,128,1024]{3,2,1,0:T(8,128)(2,1)S(1)} %get-tuple-element.161), channel_id=1, source_target_pairs={{0,4},{4,0},{8,12},{12,8},{16,20},{20,16},{24,28},{28,24},{32,36},... | collective-permute-start | bytes 6291464 | tf_op jit(solution)/shard_map/ppermute | solution.py:31
  129.1 8.3 %collective-permute-start.16 = (f32[8,1024]{1,0:T(8,128)S(1)}, f32[8,1024]{1,0:T(8,128)S(1)}, u32[]{:S(2)}, u32[]{:S(2)}) collective-permute-start(f32[8,1024]{1,0:T(8,128)S(1)} %add.42), channel_id=1, source_target_pairs={{0,64},{4,68},{8,72},{12,76},{16,80},{20,84},{24,88},{28,92},{32,9... | collective-permute-start | bytes 98312 | tf_op jit(solution)/shard_map/ppermute | solution.py:31
  137.3 9.4 %collective-permute-start.17 = (f32[8,1024]{1,0:T(8,128)S(1)}, f32[8,1024]{1,0:T(8,128)S(1)}, u32[]{:S(2)}, u32[]{:S(2)}) collective-permute-start(f32[8,1024]{1,0:T(8,128)S(1)} %add.43), channel_id=1, source_target_pairs={{0,128},{4,132},{8,136},{12,140},{16,144},{20,148},{24,152},{28,15... | collective-permute-start | bytes 98312 | tf_op jit(solution)/shard_map/ppermute | solution.py:31
  146.8 2.3 %collective-permute-start.18 = (f32[8,1024]{1,0:T(8,128)S(1)}, f32[8,1024]{1,0:T(8,128)S(1)}, u32[]{:S(2)}, u32[]{:S(2)}) collective-permute-start(f32[8,1024]{1,0:T(8,128)S(1)} %add_multiply_fusion), channel_id=1, source_target_pairs={{0,4},{4,0},{8,12},{12,8},{16,20},{20,16},{24,28},{28,24},{32,36},... | collective-permute-start | bytes 98312 | tf_op jit(solution)/shard_map/ppermute | solution.py:31

commit v3 on v0

v3 whole, which is shorter than its diff:
```python
import functools
import math

import jax
import jax.numpy as jnp
from jax import lax
from jax.experimental import pallas as pl
from jax.experimental.pallas import tpu as pltpu
from jax.sharding import PartitionSpec as P

GROUP = 128
NEAR = 4
PIECE = 4
BF = jnp.bfloat16
F32 = jnp.float32
VMEM_LIMIT = 8 * 1024 * 1024


def params():
    return pltpu.CompilerParams(vmem_limit_bytes=VMEM_LIMIT)


def shifted(value, axis, steps):
    count = lax.axis_size(axis)
    pairs = [(a, a + steps) for a in range(max(0, -steps), min(count, count - steps))]
    return lax.ppermute(value, axis, pairs)


def swapped(value, axis, mask):
    count = lax.axis_size(axis)
    return lax.ppermute(value, axis, [(a, a ^ mask) for a in range(count)])


def chip_meta(meta):
    first, second, end, core = meta[0], meta[1], meta[2], meta[3]
    return first, second - first, end - first, core


def place(meta, index):
    _, low, _, core = chip_meta(meta)
    on_second = (index >= low).astype(jnp.int32)
    slot = jnp.clip(index - on_second * low, 0, 3)
    return on_second == core, slot


SMEM = pl.BlockSpec(memory_space=pltpu.SMEM)
VMEM = pl.BlockSpec(memory_space=pltpu.VMEM)


def prep_body(meta, gate, cot, x, cot_all, w_out, send, cot_out, w_other, sems):
    slots, rows, half = w_other.shape
    step = pl.program_id(0)
    other = pl.ds(pl.multiple_of((1 - meta[3]) * half, half), half)
    copies = [
        pltpu.make_async_copy(x.at[:, :, other], send.at[0], sems.at[0]),
        pltpu.make_async_copy(cot_all.at[:, :, other], cot_out, sems.at[1]),
    ]

    @pl.when(step == 0)
    def _():
        for copy in copies:
            copy.start()

    w_out[0] = (gate[0].astype(F32) * cot[0].astype(F32)).astype(BF)
    w_other[step] = w_out[0, :, other]
    pltpu.make_async_copy(w_other.at[step], send.at[1, step], sems.at[2 + step]).start()

    @pl.when(step == slots - 1)
    def _():
        for copy in copies:
            copy.wait()
        for s in range(slots):
            pltpu.make_async_copy(w_other.at[s], send.at[1, s], sems.at[2 + s]).wait()


def prep(meta, gate, cot, x):
    slots, rows, width = x.shape
    half = width // 2
    full = pl.BlockSpec((1, rows, width), lambda s, m: (s, 0, 0))
    loose = pl.BlockSpec(memory_space=pl.ANY)
    return pl.pallas_call(
        prep_body,
        grid_spec=pltpu.PrefetchScalarGridSpec(
            num_scalar_prefetch=1,
            grid=(slots,),
            in_specs=[full, full, loose, loose],
            out_specs=[full, loose, loose],
            scratch_shapes=[
                pltpu.VMEM((slots, rows, half), BF),
                pltpu.SemaphoreType.DMA((2 + slots,)),
            ],
        ),
        out_shape=[
            jax.ShapeDtypeStruct(x.shape, BF),
            jax.ShapeDtypeStruct((2, slots, rows, half), BF),
            jax.ShapeDtypeStruct((slots, rows, half), BF),
        ],
        compiler_params=params(),
        cost_estimate=pl.CostEstimate(flops=2 << 20, bytes_accessed=12 << 20, transcendentals=0),
        name="prep",
    )(meta, gate, cot, x, cot)


def pack_body(tiles, x_at, w_at, halos, meta, x, w, theirs, *rest):
    x_halos, w_halos = rest[:halos], rest[halos : 2 * halos]
    x_out, w_out, sems = rest[2 * halos :]
    half = x_out.shape[2]
    _, _, count, core = chip_meta(meta)
    lanes = pl.ds(pl.multiple_of(core * half, half), half)
    for which, (own, out) in enumerate(((x, x_out), (w, w_out))):
        for j in range(tiles):
            sem = sems.at[which * tiles + j]
            index = (x_at if which == 0 else w_at)(j, count)
            mine, slot = place(meta, index)
            depth = -1 - index if which == 0 else index - count
            here = depth < 0

            @pl.when(here & mine)
            def _():
                pltpu.make_async_copy(own.at[slot, :, lanes], out.at[j], sem).start()

            @pl.when(here & jnp.logical_not(mine))
            def _():
                pltpu.make_async_copy(theirs.at[which, slot], out.at[j], sem).start()

            for h in range(halos):
                halo = (x_halos if which == 0 else w_halos)[h]
                inside = jnp.clip(depth - h * PIECE, 0, PIECE - 1)
                row = PIECE - 1 - inside if which == 0 else inside

                @pl.when((depth >= h * PIECE) & (depth < (h + 1) * PIECE))
                def _():
                    pltpu.make_async_copy(halo.at[row], out.at[j], sem).start()

    for which, out in enumerate((x_out, w_out)):
        for j in range(tiles):
            pltpu.make_async_copy(theirs.at[which, 0], out.at[j], sems.at[which * tiles + j]).wait()


def pack(meta, x, w, theirs, tiles, x_at, w_at, x_halos=(), w_halos=()):
    slots, rows, width = x.shape
    half = width // 2
    halos = len(x_halos)
    loose = pl.BlockSpec(memory_space=pl.ANY)
    return pl.pallas_call(
        functools.partial(pack_body, tiles, x_at, w_at, halos),
        grid_spec=pltpu.PrefetchScalarGridSpec(
            num_scalar_prefetch=1,
            grid=(1,),
            in_specs=[loose] * (3 + 2 * halos),
            out_specs=[loose, loose],
            scratch_shapes=[pltpu.SemaphoreType.DMA((2 * tiles,))],
        ),
        out_shape=[jax.ShapeDtypeStruct((tiles, rows, half), BF)] * 2,
        compiler_params=params(),
        cost_estimate=pl.CostEstimate(flops=0, bytes_accessed=tiles << 20, transcendentals=0),
        name="pack",
    )(meta, x, w, theirs, *x_halos, *w_halos)


def readers_of(table, tile, total):
    live = (tile >= 0) & (tile < total)
    return jnp.where(live, table[total + jnp.clip(tile, 0, total - 1)], 0)


def sources_of(table, tile, total):
    return table[jnp.clip(tile, 0, total - 1)]


def kept(live, tile):
    return jnp.where(live, tile, jnp.zeros_like(tile))


def dot(a, b):
    return jnp.dot(a, b, preferred_element_type=F32)


def reversal(rows):
    r = lax.broadcasted_iota(jnp.int32, (rows, rows), 0)
    c = lax.broadcasted_iota(jnp.int32, (rows, rows), 1)
    return jnp.where(r + c == rows - 1, 1.0, 0.0).astype(BF)


def diagonal_sums(square):
    rows, width = square.shape
    padded = jnp.concatenate([square, jnp.zeros((rows, rows), F32)], axis=1)
    skewed = pltpu.roll(padded, 0, 1, stride=1, stride_axis=0)
    total = jnp.sum(skewed, axis=0, keepdims=True)
    total = pltpu.roll(jnp.broadcast_to(total, (8, width + rows)), width + 1, 1)
    return total[:1, :width]


def lanes_of(group):
    return pl.ds(pl.multiple_of(group * GROUP, GROUP), GROUP)


def pick(mine, theirs, meta, index, group, groups):
    own, slot = place(meta, index)
    return jnp.where(own, mine[slot, :, lanes_of(meta[3] * groups + group)], theirs[slot, :, lanes_of(group)])


def band(row, shift):
    rows, width = GROUP, row.shape[1]
    spread = jnp.broadcast_to(jnp.concatenate([row, jnp.zeros((1, rows), F32)], axis=1), (rows, width + rows))
    return pltpu.roll(spread, shift, 1, stride=1, stride_axis=0)[:, :width].astype(BF)


def own_body(lags, total, base, steps, groups, meta, table, filt, x, theirs, w,
             conv_out, adj_out, fwd_out, bwd_out, sums_out, flip, xs, xl, ws, turned):
    cap, rows, _ = xs.shape
    first, _, count, _ = chip_meta(meta)
    width = filt.shape[1]
    ahead = [jnp.minimum(readers_of(table, first + s, total), count - s) for s in range(cap)]
    behind = [sources_of(table, first + i, total) for i in range(cap)]
    mine = filt[pl.ds(pl.multiple_of(meta[3] * groups, groups), groups), :].astype(BF)
    for k in range(lags):
        block = mine[:, (lags - 1 - k) * rows : (lags - k) * rows]
        flip[:, k * rows : (k + 1) * rows] = dot(block, reversal(rows))

    def one(step, carry):
        group = base + step
        row = pl.ds(meta[3] * groups + group, 1)
        bwd_out[step] = band(filt[row, :].astype(BF).astype(F32), 0)
        fwd_out[step] = band(flip[pl.ds(group, 1), :], width + 1)
        for s in range(cap):
            tile = pick(x, theirs.at[0], meta, s, group, groups)
            xs[s] = tile
            xl[:, s * rows : (s + 1) * rows] = tile
            tile = pick(w, theirs.at[1], meta, s, group, groups)
            ws[s] = tile
            turned[s] = tile.T
        lanes = lanes_of(step)
        for i in range(cap):
            right = jnp.concatenate([kept(i - s < behind[i], xs[s]) for s in range(i + 1)], axis=0)
            conv_out[i, :, lanes] = dot(fwd_out[step, :, (lags - 1 - i) * rows :], right)
        for s in range(cap):
            right = jnp.concatenate([kept(k < ahead[s], ws[s + k]) for k in range(cap - s)], axis=0)
            adj_out[s, :, lanes] = dot(bwd_out[step, :, : (cap - s) * rows], right)
        back = dot(reversal(rows), xl[...]).astype(BF)
        squares = []
        for k in range(0, lags, 2):
            right = [
                [kept(q < ahead[s], turned[s + q]) if s + q < cap else jnp.zeros((GROUP, rows), BF) for q in (k, k + 1)]
                for s in range(cap - k)
            ]
            right = jnp.concatenate([jnp.concatenate(pair, axis=1) for pair in right], axis=0)
            squares.append(dot(back[:, : (cap - k) * rows], right))
        sums_out[pl.ds(step, 1), :] = diagonal_sums(jnp.concatenate(squares, axis=1))
        return carry

    lax.fori_loop(0, steps, one, 0)


def own_pairs(meta, table, filt, x, w, theirs, lags, base, steps):
    slots, rows, width = x.shape
    groups = width // 2 // GROUP
    taps = filt.shape[1]
    cap = 2 * slots
    return pl.pallas_call(
        functools.partial(own_body, lags, table.shape[0] // 2, base, steps, groups),
        in_specs=[SMEM, SMEM] + [VMEM] * 4,
        out_specs=[VMEM] * 5,
        scratch_shapes=[
            pltpu.VMEM((groups, taps), F32),
            pltpu.VMEM((cap, rows, GROUP), BF),
            pltpu.VMEM((rows, cap * GROUP), BF),
            pltpu.VMEM((cap, rows, GROUP), BF),
            pltpu.VMEM((cap, GROUP, rows), BF),
        ],
        out_shape=[
            jax.ShapeDtypeStruct((cap, rows, steps * GROUP), F32),
            jax.ShapeDtypeStruct((cap, rows, steps * GROUP), F32),
            jax.ShapeDtypeStruct((steps, rows, taps), BF),
            jax.ShapeDtypeStruct((steps, rows, taps), BF),
            jax.ShapeDtypeStruct((steps, taps), F32),
        ],
        compiler_params=params(),
        cost_estimate=pl.CostEstimate(flops=steps * 1_000_000_000, bytes_accessed=steps << 20, transcendentals=0),
        name="own_pairs",
    )(meta, table, filt, x, theirs, w)


def cross_body(lags, total, groups, meta, table, prior, more, x, theirs, w, xn, wn,
               sums_out, xl, near, deep):
    rows = xl.shape[0]
    blocks = lags - 1
    first, _, count, _ = chip_meta(meta)
    split = blocks - NEAR
    found = []
    for p in range(blocks):
        s = p - blocks if p >= split else count - 1 - (blocks - 1 - p)
        number = readers_of(table, first + s, total)
        found.append(number if p >= split else jnp.where(s >= 0, number, 0))
    steps = prior.shape[0]
    for part in range(2):
        source = (prior, more)[part]

        def one(step, carry):
            group = part * steps + step
            lanes = lanes_of(group)
            for p in range(split):
                index = count - 1 - (blocks - 1 - p)
                xl[:, p * rows : (p + 1) * rows] = pick(x, theirs.at[0], meta, index, group, groups)
            for p in range(NEAR):
                at = split + p
                xl[:, at * rows : (at + 1) * rows] = xn[p, :, lanes]
            for t in range(blocks):
                tile = pick(w, theirs.at[1], meta, t, group, groups)
                if t >= NEAR:
                    tile = jnp.where(t < count, tile, wn[jnp.clip(t - count, 0, PIECE - 1), :, lanes])
                near[t] = tile.T
            for a in range(split):
                deep[a] = wn[a, :, lanes].T
            back = dot(reversal(rows), xl[...]).astype(BF)

            def tile_at(p, k):
                s = p - blocks
                if p >= split and s + k >= 0:
                    return kept(k < found[p], near[s + k])
                if p < split and s + k >= 0:
                    return kept(k < found[p], deep[s + k])
                return jnp.zeros((GROUP, rows), BF)

            squares = []
            for k in range(0, lags, 2):
                low = blocks - 1 - k
                right = [jnp.concatenate([tile_at(p, k), tile_at(p, k + 1)], axis=1) for p in range(low, blocks)]
                squares.append(dot(back[:, low * rows :], jnp.concatenate(right, axis=0)))
            total_sum = diagonal_sums(jnp.concatenate(squares, axis=1))
            sums_out[pl.ds(group, 1), :] = source[pl.ds(step, 1), :] + total_sum
            return carry

        lax.fori_loop(0, steps, one, 0)


def cross_squares(meta, table, prior, more, x, w, theirs, x_halo, w_halo, lags):
    slots, rows, width = x.shape
    groups = width // 2 // GROUP
    taps = prior.shape[1]
    blocks = lags - 1
    return pl.pallas_call(
        functools.partial(cross_body, lags, table.shape[0] // 2, groups),
        in_specs=[SMEM, SMEM] + [VMEM] * 7,
        out_specs=VMEM,
        scratch_shapes=[
            pltpu.VMEM((rows, blocks * GROUP), BF),
            pltpu.VMEM((blocks, GROUP, rows), BF),
            pltpu.VMEM((blocks - NEAR, GROUP, rows), BF),
        ],
        out_shape=jax.ShapeDtypeStruct((groups, taps), F32),
        compiler_params=params(),
        cost_estimate=pl.CostEstimate(flops=3_000_000_000, bytes_accessed=6 << 20, transcendentals=0),
        name="cross_squares",
    )(meta, table, prior, more, x, theirs, w, x_halo, w_halo)


def near_body(lags, total, groups, meta, table, conv_a, conv_b, adj_a, adj_b, fwd_a, fwd_b, bwd_a, bwd_b,
              xn, wn, cot, cot_t, gate_out, input_out, send_out, conv_out, adj_out, accum):
    slots, rows, _ = gate_out.shape
    cap = 2 * slots
    first, low, count, core = chip_meta(meta)
    high = count - low
    blocks = lags - 1
    behind = [sources_of(table, first + i, total) for i in range(blocks)]
    ahead = [readers_of(table, first + count - 1 - c, total) for c in range(blocks)]
    steps = fwd_a.shape[0]
    for part in range(2):
        conv, adj, fwd, bwd = ((conv_a, adj_a, fwd_a, bwd_a), (conv_b, adj_b, fwd_b, bwd_b))[part]

        def one(step, carry):
            group = part * steps + step
            lanes, local = lanes_of(group), lanes_of(step)
            xs = [xn[p, :, lanes] for p in range(NEAR)]
            ws = [wn[p, :, lanes] for p in range(NEAR)]
            for i in range(blocks):
                farthest = min(blocks, i + NEAR)
                start = (blocks - farthest) * rows
                size = (farthest - i) * rows
                right = [kept(lag < behind[i], xs[i + NEAR - lag]) for lag in range(farthest, i, -1)]
                term = dot(fwd[step, :, start : start + size], jnp.concatenate(right, axis=0))
                accum[i] = conv[i, :, local] + term
            accum[blocks] = conv[blocks, :, local]
            for i in range(blocks - NEAR):
                conv_out[i, :, lanes] = accum[i]
            for c in range(blocks):
                tiles = min(NEAR, blocks - c)
                start = (c + 1) * rows
                right = jnp.concatenate([kept(c + 1 + a < ahead[c], ws[a]) for a in range(tiles)], axis=0)
                term = dot(bwd[step, :, start : start + tiles * rows], right)
                accum[cap + blocks + count - 1 - c] = term
            for c in range(blocks, cap):
                accum[cap + blocks + count - 1 - c] = jnp.zeros((rows, GROUP), F32)
            for c in range(blocks - NEAR):
                at = count - 1 - c
                adj_out[c, :, lanes] = adj[at, :, local] + accum[cap + blocks + at]
            for slot in range(slots):
                for own in (True, False):
                    second = core if own else 1 - core
                    index = jnp.minimum(slot + second * low, cap - 1)
                    live = slot < jnp.where(second == 1, high, low)
                    cot_tile = cot[slot, :, lanes_of(core * groups + group)] if own else cot_t[slot, :, lanes]
                    grad = jnp.where(live, cot_tile.astype(F32) * accum[index], 0.0).astype(BF)
                    sum_ = adj[index, :, local] + accum[cap + blocks + index]
                    back = jnp.where(live, sum_, 0.0).astype(BF)
                    if own:
                        gate_out[slot, :, lanes] = grad
                        input_out[slot, :, lanes] = back
                    else:
                        send_out[0, slot, :, lanes] = grad
                        send_out[1, slot, :, lanes] = back
            return carry

        lax.fori_loop(0, steps, one, 0)


def near_pairs(meta, table, one, two, x_halo, w_halo, cot, cot_theirs, lags):
    slots, rows, width = cot.shape
    half = width // 2
    far = lags - 1 - NEAR
    pieces = [value for pair in zip(one, two) for value in pair]
    return pl.pallas_call(
        functools.partial(near_body, lags, table.shape[0] // 2, half // GROUP),
        in_specs=[SMEM, SMEM] + [VMEM] * 12,
        out_specs=[VMEM] * 5,
        scratch_shapes=[
            pltpu.VMEM((4 * slots + lags - 1, rows, GROUP), F32),
        ],
        out_shape=[
            jax.ShapeDtypeStruct((slots, rows, half), BF),
            jax.ShapeDtypeStruct((slots, rows, half), BF),
            jax.ShapeDtypeStruct((2, slots, rows, half), BF),
            jax.ShapeDtypeStruct((far, rows, half), F32),
            jax.ShapeDtypeStruct((far, rows, half), F32),
        ],
        compiler_params=params(),
        cost_estimate=pl.CostEstimate(flops=3_000_000_000, bytes_accessed=8 << 20, transcendentals=0),
        name="near_pairs",
    )(meta, table, *pieces, x_halo, w_halo, cot, cot_theirs)


def far_body(lags, total, groups, meta, table, conv, adj, fwd_a, fwd_b, bwd_a, bwd_b, xf, wf, cot, cot_t,
             gate_in, input_in, send_in, gate_out, input_out, send_out):
    far, rows, _ = xf.shape
    first, _, count, _ = chip_meta(meta)
    behind = [sources_of(table, first + i, total) for i in range(far)]
    ahead = [readers_of(table, first + count - 1 - c, total) for c in range(far)]
    steps = fwd_a.shape[0]
    for part in range(2):
        fwd, bwd = ((fwd_a, bwd_a), (fwd_b, bwd_b))[part]

        def one(step, carry):
            group = part * steps + step
            lanes = lanes_of(group)
            xs = [xf[p, :, lanes] for p in range(far)]
            ws = [wf[p, :, lanes] for p in range(far)]
            results = []
            for i in range(far):
                right = [kept(lags - 1 + i - p < behind[i], xs[p]) for p in range(i, far)]
                term = dot(fwd[step, :, : (far - i) * rows], jnp.concatenate(right, axis=0))
                value = pick(cot, cot_t, meta, i, group, groups).astype(F32) * (conv[i, :, lanes] + term)
                results.append((i, gate_out, 0, value.astype(BF)))
            for c in range(far):
                right = [kept(c + NEAR + 1 + a < ahead[c], ws[a]) for a in range(far - c)]
                term = dot(bwd[step, :, (c + NEAR + 1) * rows :], jnp.concatenate(right, axis=0))
                results.append((count - 1 - c, input_out, 1, (adj[c, :, lanes] + term).astype(BF)))
            for index, out, which, value in results:
                mine, slot = place(meta, index)

                @pl.when(mine)
                def _():
                    out[slot, :, lanes] = value

                @pl.when(jnp.logical_not(mine))
                def _():
                    send_out[which, slot, :, lanes] = value

            return carry

        lax.fori_loop(0, steps, one, 0)


def far_pairs(meta, table, conv, adj, one, two, x_halo, w_halo, cot, cot_theirs, gate, inp, send, lags):
    width = cot.shape[2]
    pieces = [one[2], two[2], one[3], two[3]]
    return pl.pallas_call(
        functools.partial(far_body, lags, table.shape[0] // 2, width // 2 // GROUP),
        in_specs=[SMEM, SMEM] + [VMEM] * 13,
        out_specs=[VMEM] * 3,
        out_shape=[
            jax.ShapeDtypeStruct(gate.shape, BF),
            jax.ShapeDtypeStruct(inp.shape, BF),
            jax.ShapeDtypeStruct(send.shape, BF),
        ],
        input_output_aliases={12: 0, 13: 1, 14: 2},
        compiler_params=params(),
        cost_estimate=pl.CostEstimate(flops=800_000_000, bytes_accessed=4 << 20, transcendentals=0),
        name="far_pairs",
    )(meta, table, conv, adj, *pieces, x_halo, w_halo, cot, cot_theirs, gate, inp, send)


def settle_body(mine, meta, gate, inp, gate_in, input_in, gate_out, input_out, sems):
    slots, _, half = gate.shape
    core = meta[3] if mine else 1 - meta[3]
    lanes = pl.ds(pl.multiple_of(core * half, half), half)
    copies = []
    for which, (source, out) in enumerate(((gate, gate_out), (inp, input_out))):
        for s in range(slots):
            copies.append(pltpu.make_async_copy(source.at[s], out.at[s, :, lanes], sems.at[which * slots + s]))
    for copy in copies:
        copy.start()
    for copy in copies:
        copy.wait()


def place_mine(meta, gate, inp):
    slots, rows, half = gate.shape

    def body(meta, gate, inp, gate_out, input_out, sems):
        settle_body(True, meta, gate, inp, None, None, gate_out, input_out, sems)

    loose = pl.BlockSpec(memory_space=pl.ANY)
    return pl.pallas_call(
        body,
        in_specs=[SMEM, VMEM, VMEM],
        out_specs=[loose, loose],
        scratch_shapes=[pltpu.SemaphoreType.DMA((2 * slots,))],
        out_shape=[jax.ShapeDtypeStruct((slots, rows, 2 * half), BF)] * 2,
        compiler_params=params(),
        name="place_mine",
    )(meta, gate, inp)


def join(meta, got, gate, inp):
    slots = gate.shape[0]

    def body(meta, got, gate_in, input_in, gate_out, input_out, sems):
        settle_body(False, meta, got.at[0], got.at[1], gate_in, input_in, gate_out, input_out, sems)

    loose = pl.BlockSpec(memory_space=pl.ANY)
    return pl.pallas_call(
        body,
        in_specs=[SMEM, VMEM, loose, loose],
        out_specs=[loose, loose],
        scratch_shapes=[pltpu.SemaphoreType.DMA((2 * slots,))],
        out_shape=[jax.ShapeDtypeStruct(gate.shape, BF)] * 2,
        input_output_aliases={2: 0, 3: 1},
        compiler_params=params(),
        name="join",
    )(meta, got, gate, inp)


def per_device(conv_input, gate_signal, cotangent, filters, tile_owner, support):
    slots, rows, width = conv_input.shape
    lags = support.shape[1]
    filter_count, taps = filters.shape
    total = tile_owner.shape[0]
    tie = lax.optimization_barrier
    me = lax.axis_index("ctx")
    core = me % 2
    entry = jnp.arange(8, dtype=jnp.int32)
    before = jnp.sum((tile_owner[None, :] < (me - core + entry)[:, None]).astype(jnp.int32), axis=1)
    meta = jnp.where(entry == 3, core, before)

    behind = jnp.sum((support >= 0).astype(jnp.int32), axis=1)
    ahead = sum(jnp.pad((behind[k:] > k).astype(jnp.int32), (0, k)) for k in range(lags))
    table = jnp.concatenate([behind, ahead])
    meta, table = tie((meta, table))

    def up(value):
        return shifted(value, "ctx", 2)

    def down(value):
        return shifted(value, "ctx", -2)

    w, send, cot_send = prep(meta, gate_signal, cotangent, conv_input)
    theirs = swapped(send, "ctx", 1)
    x = conv_input
    xs, ws = pack(meta, x, w, theirs, PIECE, lambda j, n: n - PIECE + j, lambda j, n: j)
    x0, w0 = up(xs), down(ws)
    cot_theirs = swapped(cot_send, "ctx", 1)
    half_groups = width // 2 // GROUP // 2
    one = own_pairs(meta, table, filters, x, w, theirs, lags, 0, half_groups)
    two = own_pairs(meta, table, filters, x, w, theirs, lags, half_groups, half_groups)
    x0, w0, one, two = tie((x0, w0, one, two))
    *one, first_sums = one
    *two, second_sums = two
    sums = cross_squares(meta, table, first_sums, second_sums, x, w, theirs, x0, w0, lags)

    def stage(sums, axis, masks, filler):
        moved = [swapped(sums, axis, mask) for mask in masks]
        out = filler(tie((sums, meta))[1])
        total_sum = sums + moved[0]
        if len(masks) == 3:
            total_sum = total_sum + (moved[1] + moved[2])
        return tie((total_sum, out))

    def relay(meta):
        return pack(
            meta, x, w, theirs, lags - 1 - NEAR, lambda j, n: n - lags + 1 + j, lambda j, n: NEAR + j, (x0,), (w0,)
        )

    def close(meta):
        return near_pairs(meta, table, one, two, x0, w0, cotangent, cot_theirs, lags)

    sums, (xs, ws) = stage(sums, "ctx", (2, 4, 6), relay)
    x2, w2 = up(xs), down(ws)
    sums, (gate, inp, back, conv, adj) = stage(sums, "ch", (1, 2, 3), close)

    def finish(meta):
        return far_pairs(
            meta, table, conv, adj, one, two, x2, w2, cotangent, cot_theirs, gate, inp, back, lags
        )

    sums, (gate, inp, back) = stage(sums, "ctx", (8, 16, 24), finish)
    got = swapped(back, "ctx", 1)
    sums, (gate, inp) = stage(sums, "ctx", (32,), lambda meta: place_mine(meta, gate, inp))
    norm = 1.0 / math.sqrt(total * rows * width * lax.axis_size("ch") / filter_count)
    sums = sums * norm
    partner = swapped(sums, "ctx", 1)
    gate, inp = join(tie((sums, meta))[1], got, gate, inp)
    partner, gate, inp = tie((partner, gate, inp))
    low = jnp.where(core == 0, sums, partner)
    high = jnp.where(core == 0, partner, sums)
    return gate, inp, jnp.concatenate([low, high], axis=0)


def solution(mesh):
    return jax.shard_map(
        per_device,
        mesh=mesh,
        in_specs=(P("ctx", None, "ch"), P("ctx", None, "ch"), P("ctx", None, "ch"), P(), P(), P()),
        out_specs=(P("ctx", None, "ch"), P("ctx", None, "ch"), P()),
        check_vma=False,
    )
```

time: 1300 us -> 112 us (0.09)
  local copies, waits for them, and re-layouts: 807 us -> 4.79 us
  waiting for transfers between devices: 241 us -> 23.6 us
  other arithmetic: 126 us -> 2.89 us
  matrix products: 78 us -> 0 us
  Pallas kernels: 0 us -> 42.1 us
  starting transfers between devices: 22.1 us -> 37.7 us
  between operations: 15.1 us -> 0.87 us
    gather x8 -> x0, local copies, waits for them, and re-layouts: 497 us -> none  [the longest x2 483 us: filter_blocks(): jnp.take(narrow, jnp.clip(lag_offsets, 0, filters.shape[1] - 1), axis=1)]
    psum x1 -> x0, waiting for transfers between devices: 241 us -> none  [per_device(): filter_grad = lax.psum(local_filters, ('ctx', 'ch')) * norm_factor]
    reshape x16 -> x0, local copies, waits for them, and re-layouts: 92.7 us -> none  [the longest x8 49.4 us: lag_sums(): skewed.reshape(filter_count, side_length, 2 * side_length - 1)]
    dot_general x24 -> x0, matrix products: 78 us -> none  [the longest x8 42.7 us: per_device(): jnp.einsum('fij,sjrfc->sirfc', blocks[:, lag_index], shaped, preferred_el...]
    scatter-add x8 -> x0, other arithmetic: 69.9 us -> none  [per_device(): partial_value.at[back_rows[:, lag_index]]]
    slice x20 -> x0, local copies, waits for them, and re-layouts: 62.8 us -> none  [the longest x9 37.9 us: per_device(): selected[:, lag_index]]
    rev x8 -> x0, local copies, waits for them, and re-layouts: 54.3 us -> none  [lag_sums(): flipped = square[:, :, ::-1]]
    pallas_call x0 -> x10, Pallas kernels: none -> 42.1 us  [the longest x2 15 us: own_pairs(): pl.pallas_call(functools.partial(own_body, lags, table.shape[0] // 2, bas...]
  transfers between devices with their start and end apart: 9 -> 18, of which waited for: 1 -> 7; matrix products, arithmetic and copies ran while one was open for 78% -> 0% of each run, Pallas kernels for 0% -> 32%
where the time goes in v3:
time: 112 us
  Pallas kernels  42.1 us (38%)
  starting transfers between devices  37.7 us (34%)
  waiting for transfers between devices  23.6 us (21%)
  local copies, waits for them, and re-layouts  4.79 us (4%)
  other arithmetic  2.89 us (3%)
    ppermute x14, starting transfers between devices, swapped(): return lax.ppermute(value, axis, [(a, a ^ mask) for a in range(count)])  32.3 us
    pallas_call x2, Pallas kernels, own_pairs(): pl.pallas_call(functools.partial(own_body, lags, table.shape[0] // 2, bas...  15 us
    ppermute x14, waiting for transfers between devices, swapped(): return lax.ppermute(value, axis, [(a, a ^ mask) for a in range(count)])  14.7 us
    ppermute x4, waiting for transfers between devices, shifted(): return lax.ppermute(value, axis, pairs)  8.91 us
    pallas_call x1, Pallas kernels, near_pairs(): pl.pallas_call(functools.partial(near_body, lags, table.shape[0] // 2, ha...  7.64 us
    pallas_call x1, Pallas kernels, cross_squares(): pl.pallas_call(functools.partial(cross_body, lags, table.shape[0] // 2, g...  7.06 us
    ppermute x4, starting transfers between devices, shifted(): return lax.ppermute(value, axis, pairs)  5.45 us
    unnamed x12, local copies, waits for them, and re-layouts  4.79 us
  transfers between devices with their start and end apart: 18, of which 7 were waited for; matrix products, arithmetic and copies ran while one was open for 0% of the time, Pallas kernels for 32%

profile of v3, /device:TPU:1, one launch (start us, length us, event | category | flops | bytes accessed | tf_op | source)
XLA Modules:
  0.0 112.0 jit_solution(1562534710820888468)
XLA Ops:
  1.9 0.9 convert_reduce_fusion.1
  2.9 1.6 %copy-done = bf16[4,128,2048]{2,1,0:T(8,128)(2,1)S(1)} copy-done((bf16[4,128,2048]{2,1,0:T(8,128)(2,1)S(1)}, bf16[4,128,2048]{2,1,0:T(8,128)(2,1)}, u32[]{:S(2)}) %copy-start) | copy-done | bytes 2097176
  4.4 1.6 %copy-done.2 = bf16[4,128,2048]{2,1,0:T(8,128)(2,1)S(1)} copy-done((bf16[4,128,2048]{2,1,0:T(8,128)(2,1)S(1)}, bf16[4,128,2048]{2,1,0:T(8,128)(2,1)}, u32[]{:S(2)}) %copy-start.2) | copy-done | bytes 2097176
  6.0 1.6 %copy-done.4 = bf16[4,128,2048]{2,1,0:T(8,128)(2,1)S(1)} copy-done((bf16[4,128,2048]{2,1,0:T(8,128)(2,1)S(1)}, bf16[4,128,2048]{2,1,0:T(8,128)(2,1)}, u32[]{:S(2)}) %copy-start.4) | copy-done | bytes 2097176
  7.6 2.2 %prep.1 = (bf16[4,128,2048]{2,1,0:T(8,128)(2,1)S(1)}, bf16[2,4,128,1024]{3,2,1,0:T(8,128)(2,1)S(1)}, bf16[4,128,1024]{2,1,0:T(8,128)(2,1)S(1)}) custom-call(s32[8]{0:T(128)S(1)} %compare_select_fusion.meta, bf16[4,128,2048]{2,1,0:T(8,128)(2,1)S(1)} %copy-done.4, bf16[4,128,2048]{2,1,0:T(8,128)(2,1)S(1)} %copy-done, bf16[4,128,2048]{2,1,0:T(8,128)(2,1)S(1)} %copy-done.2, ...), custom_call_target="tpu_custom_call" | custom-call | flops 2097152 | bytes 12582912 | tf_op jit(solution)/shard_map/prep/pallas_call | solution.py:81
  9.8 3.3 %collective-permute-start = (bf16[2,4,128,1024]{3,2,1,0:T(8,128)(2,1)S(1)}, bf16[2,4,128,1024]{3,2,1,0:T(8,128)(2,1)S(1)}, u32[]{:S(2)}, u32[]{:S(2)}) collective-permute-start(bf16[2,4,128,1024]{3,2,1,0:T(8,128)(2,1)S(1)} %get-tuple-element.73), channel_id=1, source_target_pairs={{0,4},{4,0},{8,12},{12,8},{16,20},{20,16},{24,28},{28,24},{32,36},... | collective-permute-start | bytes 6291464 | tf_op jit(solution)/shard_map/ppermute | solution.py:31
  13.2 3.8 %collective-permute-done.theirs = bf16[2,4,128,1024]{3,2,1,0:T(8,128)(2,1)S(1)} collective-permute-done((bf16[2,4,128,1024]{3,2,1,0:T(8,128)(2,1)S(1)}, bf16[2,4,128,1024]{3,2,1,0:T(8,128)(2,1)S(1)}, u32[]{:S(2)}, u32[]{:S(2)}) %collective-permute-start) | collective-permute-done | bytes 2097184 | tf_op jit(solution)/shard_map/ppermute | solution.py:31
  17.0 0.9 pack.2
  17.9 1.5 %collective-permute-start.1 = (bf16[4,128,1024]{2,1,0:T(8,128)(2,1)S(1)}, bf16[4,128,1024]{2,1,0:T(8,128)(2,1)S(1)}, u32[]{:S(2)}, u32[]{:S(2)}) collective-permute-start(bf16[4,128,1024]{2,1,0:T(8,128)(2,1)S(1)} %get-tuple-element.74), channel_id=1, source_target_pairs={{0,8},{4,12},{8,16},{12,20},{16,24},{20,28},{24,32},{28,36},{32,40... | collective-permute-start | bytes 3145736 | tf_op jit(solution)/shard_map/ppermute | solution.py:26
  19.4 1.3 %collective-permute-start.2 = (bf16[4,128,1024]{2,1,0:T(8,128)(2,1)S(1)}, bf16[4,128,1024]{2,1,0:T(8,128)(2,1)S(1)}, u32[]{:S(2)}, u32[]{:S(2)}) collective-permute-start(bf16[4,128,1024]{2,1,0:T(8,128)(2,1)S(1)} %get-tuple-element.75), channel_id=1, source_target_pairs={{8,0},{12,4},{16,8},{20,12},{24,16},{28,20},{32,24},{36,28},{40,32... | collective-permute-start | bytes 3145736 | tf_op jit(solution)/shard_map/ppermute | solution.py:26
  20.7 0.7 collective-permute-start.9
  21.5 7.5 %own_pairs.3 = (f32[8,128,512]{2,1,0:T(8,128)S(1)}, f32[8,128,512]{2,1,0:T(8,128)S(1)}, bf16[4,128,1024]{2,1,0:T(8,128)(2,1)S(1)}, bf16[4,128,1024]{2,1,0:T(8,128)(2,1)S(1)}, f32[4,1024]{1,0:T(4,128)S(1)}) custom-call(s32[8]{0:T(128)S(1)} %compare_select_fusion.meta, s32[384]{0:T(512)S(1)} %pad_add_fusion.table, f32[16,1024]{1,0:T(8,128)S(1)} %copy-done.5, ...), custom_call_target="tpu_custom_call" | custom-call | flops 4000000000 | bytes 4194304 | tf_op jit(solution)/shard_map/own_pairs/pallas_call | solution.py:259
  28.9 7.5 %own_pairs.2 = (f32[8,128,512]{2,1,0:T(8,128)S(1)}, f32[8,128,512]{2,1,0:T(8,128)S(1)}, bf16[4,128,1024]{2,1,0:T(8,128)(2,1)S(1)}, bf16[4,128,1024]{2,1,0:T(8,128)(2,1)S(1)}, f32[4,1024]{1,0:T(4,128)S(1)}) custom-call(s32[8]{0:T(128)S(1)} %compare_select_fusion.meta, s32[384]{0:T(512)S(1)} %pad_add_fusion.table, f32[16,1024]{1,0:T(8,128)S(1)} %copy-done.5, ...), custom_call_target="tpu_custom_call" | custom-call | flops 4000000000 | bytes 4194304 | tf_op jit(solution)/shard_map/own_pairs/pallas_call | solution.py:259
  36.4 5.0 %collective-permute-done.1.xn.rest_0_ = bf16[4,128,1024]{2,1,0:T(8,128)(2,1)S(1)} collective-permute-done((bf16[4,128,1024]{2,1,0:T(8,128)(2,1)S(1)}, bf16[4,128,1024]{2,1,0:T(8,128)(2,1)S(1)}, u32[]{:S(2)}, u32[]{:S(2)}) %collective-permute-start.1) | collective-permute-done | bytes 1048608 | tf_op jit(solution)/shard_map/ppermute | solution.py:26
  41.5 3.9 %collective-permute-done.2.wn.rest_1_ = bf16[4,128,1024]{2,1,0:T(8,128)(2,1)S(1)} collective-permute-done((bf16[4,128,1024]{2,1,0:T(8,128)(2,1)S(1)}, bf16[4,128,1024]{2,1,0:T(8,128)(2,1)S(1)}, u32[]{:S(2)}, u32[]{:S(2)}) %collective-permute-start.2) | collective-permute-done | bytes 1048608 | tf_op jit(solution)/shard_map/ppermute | solution.py:26
  45.3 7.1 %cross_squares.1 = f32[8,1024]{1,0:T(8,128)S(1)} custom-call(s32[8]{0:T(128)S(1)} %compare_select_fusion.meta, s32[384]{0:T(512)S(1)} %pad_add_fusion.table, f32[4,1024]{1,0:T(4,128)S(1)} %get-tuple-element.86.prior, f32[4,1024]{1,0:T(4,128)S(1)} %get-tuple-element.87.more, bf16[4,128,2048]{2,1,0:T(8,128)(2,1)S(1)} %copy-done.3, ...), custom_call_target="tpu_custom_call" | custom-call | flops 3000000000 | bytes 6291456 | tf_op jit(solution)/shard_map/cross_squares/pallas_call | solution.py:341
  52.4 4.9 %collective-permute-start.5 = (f32[8,1024]{1,0:T(8,128)S(1)}, f32[8,1024]{1,0:T(8,128)S(1)}, u32[]{:S(2)}, u32[]{:S(2)}) collective-permute-start(f32[8,1024]{1,0:T(8,128)S(1)} %cross_squares.1), channel_id=1, source_target_pairs={{0,24},{4,28},{8,16},{12,20},{16,8},{20,12},{24,0},{28,4},{32,56},... | collective-permute-start | bytes 98312 | tf_op jit(solution)/shard_map/ppermute | solution.py:31
  58.0 0.8 pack.3
  58.8 2.7 %collective-permute-done.4 = f32[8,1024]{1,0:T(8,128)S(1)} collective-permute-done((f32[8,1024]{1,0:T(8,128)S(1)}, f32[8,1024]{1,0:T(8,128)S(1)}, u32[]{:S(2)}, u32[]{:S(2)}) %collective-permute-start.4) | collective-permute-done | bytes 32800 | tf_op jit(solution)/shard_map/ppermute | solution.py:31
  61.6 1.3 %collective-permute-start.13 = (bf16[3,128,1024]{2,1,0:T(8,128)(2,1)S(1)}, bf16[3,128,1024]{2,1,0:T(8,128)(2,1)S(1)}, u32[]{:S(2)}, u32[]{:S(2)}) collective-permute-start(bf16[3,128,1024]{2,1,0:T(8,128)(2,1)S(1)} %get-tuple-element.113), channel_id=1, source_target_pairs={{0,8},{4,12},{8,16},{12,20},{16,24},{20,28},{24,32},{28,36},{32,40... | collective-permute-start | bytes 2359304 | tf_op jit(solution)/shard_map/ppermute | solution.py:26
  62.9 1.3 %collective-permute-start.14 = (bf16[3,128,1024]{2,1,0:T(8,128)(2,1)S(1)}, bf16[3,128,1024]{2,1,0:T(8,128)(2,1)S(1)}, u32[]{:S(2)}, u32[]{:S(2)}) collective-permute-start(bf16[3,128,1024]{2,1,0:T(8,128)(2,1)S(1)} %get-tuple-element.114), channel_id=1, source_target_pairs={{8,0},{12,4},{16,8},{20,12},{24,16},{28,20},{32,24},{36,28},{40,32... | collective-permute-start | bytes 2359304 | tf_op jit(solution)/shard_map/ppermute | solution.py:26
  64.2 2.6 %collective-permute-start.8 = (f32[8,1024]{1,0:T(8,128)S(1)}, f32[8,1024]{1,0:T(8,128)S(1)}, u32[]{:S(2)}, u32[]{:S(2)}) collective-permute-start(f32[8,1024]{1,0:T(8,128)S(1)} %add_add_fusion.2), channel_id=1, source_target_pairs={{0,3},{1,2},{2,1},{3,0},{4,7},{5,6},{6,5},{7,4},{8,11},{9,10},{10,... | collective-permute-start | bytes 98312 | tf_op jit(solution)/shard_map/ppermute | solution.py:31
  67.6 7.6 %near_pairs.1 = (bf16[4,128,1024]{2,1,0:T(8,128)(2,1)S(1)}, bf16[4,128,1024]{2,1,0:T(8,128)(2,1)S(1)}, bf16[2,4,128,1024]{3,2,1,0:T(8,128)(2,1)S(1)}, f32[3,128,1024]{2,1,0:T(8,128)S(1)}, f32[3,128,1024]{2,1,0:T(8,128)S(1)}) custom-call(s32[8]{0:T(128)S(1)} %compare_select_fusion.meta, s32[384]{0:T(512)S(1)} %pad_add_fusion.table, ...), custom_call_target="tpu_custom_call" | custom-call | flops 3000000000 | bytes 8388608 | tf_op jit(solution)/shard_map/near_pairs/pallas_call | solution.py:421
  75.3 11.6 %collective-permute-start.12 = (f32[8,1024]{1,0:T(8,128)S(1)}, f32[8,1024]{1,0:T(8,128)S(1)}, u32[]{:S(2)}, u32[]{:S(2)}) collective-permute-start(f32[8,1024]{1,0:T(8,128)S(1)} %add_add_fusion.1), channel_id=1, source_target_pairs={{0,96},{4,100},{8,104},{12,108},{16,112},{20,116},{24,120},{28,124... | collective-permute-start | bytes 98312 | tf_op jit(solution)/shard_map/ppermute | solution.py:31
  87.3 3.2 %collective-permute-done.12 = f32[8,1024]{1,0:T(8,128)S(1)} collective-permute-done((f32[8,1024]{1,0:T(8,128)S(1)}, f32[8,1024]{1,0:T(8,128)S(1)}, u32[]{:S(2)}, u32[]{:S(2)}) %collective-permute-start.12) | collective-permute-done | bytes 32800 | tf_op jit(solution)/shard_map/ppermute | solution.py:31
  90.5 1.0 collective-permute-done.11
  91.5 3.6 %far_pairs.1 = (bf16[4,128,1024]{2,1,0:T(8,128)(2,1)S(1)}, bf16[4,128,1024]{2,1,0:T(8,128)(2,1)S(1)}, bf16[2,4,128,1024]{3,2,1,0:T(8,128)(2,1)S(1)}) custom-call(s32[8]{0:T(128)S(1)} %compare_select_fusion.meta, s32[384]{0:T(512)S(1)} %pad_add_fusion.table, ...), custom_call_target="tpu_custom_call", output_to_operand_aliasing={{0}: (12, {}), {1}: (13, {}), {2}: (14, {})} | custom-call | flops 800000000 | bytes 4194304 | tf_op jit(solution)/shard_map/far_pairs/pallas_call | solution.py:485
  95.1 5.0 %collective-permute-start.17 = (bf16[2,4,128,1024]{3,2,1,0:T(8,128)(2,1)S(1)}, bf16[2,4,128,1024]{3,2,1,0:T(8,128)(2,1)}, u32[]{:S(2)}, u32[]{:S(2)}) collective-permute-start(bf16[2,4,128,1024]{3,2,1,0:T(8,128)(2,1)S(1)} %get-tuple-element.129), channel_id=1, source_target_pairs={{0,4},{4,0},{8,12},{12,8},{16,20},{20,16},{24,28},{28,24},{32,36},... | collective-permute-start | bytes 6291464 | tf_op jit(solution)/shard_map/ppermute | solution.py:31
  100.1 1.6 %collective-permute-start.15 = (f32[8,1024]{1,0:T(8,128)S(1)}, f32[8,1024]{1,0:T(8,128)S(1)}, u32[]{:S(2)}, u32[]{:S(2)}) collective-permute-start(f32[8,1024]{1,0:T(8,128)S(1)} %add_add_fusion), channel_id=1, source_target_pairs={{0,128},{4,132},{8,136},{12,140},{16,144},{20,148},{24,152},{28,15... | collective-permute-start | bytes 98312 | tf_op jit(solution)/shard_map/ppermute | solution.py:31
  101.7 1.9 %place_mine.1 = (bf16[4,128,2048]{2,1,0:T(8,128)(2,1)}, bf16[4,128,2048]{2,1,0:T(8,128)(2,1)}) custom-call(s32[8]{0:T(128)S(1)} %compare_select_fusion.meta, bf16[4,128,1024]{2,1,0:T(8,128)(2,1)S(1)} %get-tuple-element.123.gate, bf16[4,128,1024]{2,1,0:T(8,128)(2,1)S(1)} %get-tuple-element.124.inp), custom_call_target="tpu_custom_call" | custom-call | tf_op jit(solution)/shard_map/place_mine/pallas_call | solution.py:522
  103.7 4.0 %collective-permute-done.15 = f32[8,1024]{1,0:T(8,128)S(1)} collective-permute-done((f32[8,1024]{1,0:T(8,128)S(1)}, f32[8,1024]{1,0:T(8,128)S(1)}, u32[]{:S(2)}, u32[]{:S(2)}) %collective-permute-start.15) | collective-permute-done | bytes 32800 | tf_op jit(solution)/shard_map/ppermute | solution.py:31
  108.3 3.0 %join.1 = (bf16[4,128,2048]{2,1,0:T(8,128)(2,1)}, bf16[4,128,2048]{2,1,0:T(8,128)(2,1)}) custom-call(s32[8]{0:T(128)S(1)} %compare_select_fusion.meta, bf16[2,4,128,1024]{3,2,1,0:T(8,128)(2,1)} %collective-permute-done.17.got, bf16[4,128,2048]{2,1,0:T(8,128)(2,1)} %get-tuple-element.130.gate_in, ...), custom_call_target="tpu_custom_call", output_to_operand_aliasing={{0}: (2, {}), {1}: (3, {})} | custom-call | tf_op jit(solution)/shard_map/join/pallas_call | solution.py:540
  (46 shorter events, 4.6 us)
Async XLA Ops:
  2.8 1.6 %copy-start = (bf16[4,128,2048]{2,1,0:T(8,128)(2,1)S(1)}, bf16[4,128,2048]{2,1,0:T(8,128)(2,1)}, u32[]{:S(2)}) copy-start(bf16[4,128,2048]{2,1,0:T(8,128)(2,1)} %cot.5) | copy-start | bytes 6291460
  4.4 1.6 %copy-start.2 = (bf16[4,128,2048]{2,1,0:T(8,128)(2,1)S(1)}, bf16[4,128,2048]{2,1,0:T(8,128)(2,1)}, u32[]{:S(2)}) copy-start(bf16[4,128,2048]{2,1,0:T(8,128)(2,1)} %x.25) | copy-start | bytes 6291460
  6.0 1.6 %copy-start.4 = (bf16[4,128,2048]{2,1,0:T(8,128)(2,1)S(1)}, bf16[4,128,2048]{2,1,0:T(8,128)(2,1)}, u32[]{:S(2)}) copy-start(bf16[4,128,2048]{2,1,0:T(8,128)(2,1)} %gate.1) | copy-start | bytes 6291460
  7.6 9.3 %copy-start.3 = (bf16[4,128,2048]{2,1,0:T(8,128)(2,1)S(1)}, bf16[4,128,2048]{2,1,0:T(8,128)(2,1)}, u32[]{:S(2)}) copy-start(bf16[4,128,2048]{2,1,0:T(8,128)(2,1)} %x.25) | copy-start | bytes 6291460
  9.8 7.1 %collective-permute-start = (bf16[2,4,128,1024]{3,2,1,0:T(8,128)(2,1)S(1)}, bf16[2,4,128,1024]{3,2,1,0:T(8,128)(2,1)S(1)}, u32[]{:S(2)}, u32[]{:S(2)}) collective-permute-start(bf16[2,4,128,1024]{3,2,1,0:T(8,128)(2,1)S(1)} %get-tuple-element.73), channel_id=1, source_target_pairs={{0,4},{4,0},{8,12},{12,8},{16,20},{20,16},{24,28},{28,24},{32,36},... | collective-permute-start | bytes 6291464 | tf_op jit(solution)/shard_map/ppermute | solution.py:31
  17.0 4.5 %copy-start.5 = (f32[16,1024]{1,0:T(8,128)S(1)}, f32[16,1024]{1,0:T(8,128)}, u32[]{:S(2)}) copy-start(f32[16,1024]{1,0:T(8,128)} %filt.3) | copy-start | bytes 196612
  17.9 23.6 %collective-permute-start.1 = (bf16[4,128,1024]{2,1,0:T(8,128)(2,1)S(1)}, bf16[4,128,1024]{2,1,0:T(8,128)(2,1)S(1)}, u32[]{:S(2)}, u32[]{:S(2)}) collective-permute-start(bf16[4,128,1024]{2,1,0:T(8,128)(2,1)S(1)} %get-tuple-element.74), channel_id=1, source_target_pairs={{0,8},{4,12},{8,16},{12,20},{16,24},{20,28},{24,32},{28,36},{32,40... | collective-permute-start | bytes 3145736 | tf_op jit(solution)/shard_map/ppermute | solution.py:26
  19.4 25.9 %collective-permute-start.2 = (bf16[4,128,1024]{2,1,0:T(8,128)(2,1)S(1)}, bf16[4,128,1024]{2,1,0:T(8,128)(2,1)S(1)}, u32[]{:S(2)}, u32[]{:S(2)}) collective-permute-start(bf16[4,128,1024]{2,1,0:T(8,128)(2,1)S(1)} %get-tuple-element.75), channel_id=1, source_target_pairs={{8,0},{12,4},{16,8},{20,12},{24,16},{28,20},{32,24},{36,28},{40,32... | collective-permute-start | bytes 3145736 | tf_op jit(solution)/shard_map/ppermute | solution.py:26
  20.7 46.6 %collective-permute-start.9 = (bf16[4,128,1024]{2,1,0:T(8,128)(2,1)S(1)}, bf16[4,128,1024]{2,1,0:T(8,128)(2,1)S(1)}, u32[]{:S(2)}, u32[]{:S(2)}) collective-permute-start(bf16[4,128,1024]{2,1,0:T(8,128)(2,1)S(1)} %get-tuple-element.103), channel_id=1, source_target_pairs={{0,4},{4,0},{8,12},{12,8},{16,20},{20,16},{24,28},{28,24},{32,36},... | collective-permute-start | bytes 3145736 | tf_op jit(solution)/shard_map/ppermute | solution.py:31
  52.4 15.2 %copy-start.1 = (bf16[4,128,2048]{2,1,0:T(8,128)(2,1)S(1)}, bf16[4,128,2048]{2,1,0:T(8,128)(2,1)}, u32[]{:S(2)}) copy-start(bf16[4,128,2048]{2,1,0:T(8,128)(2,1)} %cot.5) | copy-start | bytes 6291460
  52.4 6.4 %collective-permute-start.5 = (f32[8,1024]{1,0:T(8,128)S(1)}, f32[8,1024]{1,0:T(8,128)S(1)}, u32[]{:S(2)}, u32[]{:S(2)}) collective-permute-start(f32[8,1024]{1,0:T(8,128)S(1)} %cross_squares.1), channel_id=1, source_target_pairs={{0,24},{4,28},{8,16},{12,20},{16,8},{20,12},{24,0},{28,4},{32,56},... | collective-permute-start | bytes 98312 | tf_op jit(solution)/shard_map/ppermute | solution.py:31
  57.3 4.3 %collective-permute-start.4 = (f32[8,1024]{1,0:T(8,128)S(1)}, f32[8,1024]{1,0:T(8,128)S(1)}, u32[]{:S(2)}, u32[]{:S(2)}) collective-permute-start(f32[8,1024]{1,0:T(8,128)S(1)} %cross_squares.1), channel_id=1, source_target_pairs={{0,16},{4,20},{8,24},{12,28},{16,0},{20,4},{24,8},{28,12},{32,48},... | collective-permute-start | bytes 98312 | tf_op jit(solution)/shard_map/ppermute | solution.py:31
  57.3 4.3 %collective-permute-start.3 = (f32[8,1024]{1,0:T(8,128)S(1)}, f32[8,1024]{1,0:T(8,128)S(1)}, u32[]{:S(2)}, u32[]{:S(2)}) collective-permute-start(f32[8,1024]{1,0:T(8,128)S(1)} %cross_squares.1), channel_id=1, source_target_pairs={{0,8},{4,12},{8,0},{12,4},{16,24},{20,28},{24,16},{28,20},{32,40},... | collective-permute-start | bytes 98312 | tf_op jit(solution)/shard_map/ppermute | solution.py:31
  61.6 29.9 %collective-permute-start.13 = (bf16[3,128,1024]{2,1,0:T(8,128)(2,1)S(1)}, bf16[3,128,1024]{2,1,0:T(8,128)(2,1)S(1)}, u32[]{:S(2)}, u32[]{:S(2)}) collective-permute-start(bf16[3,128,1024]{2,1,0:T(8,128)(2,1)S(1)} %get-tuple-element.113), channel_id=1, source_target_pairs={{0,8},{4,12},{8,16},{12,20},{16,24},{20,28},{24,32},{28,36},{32,40... | collective-permute-start | bytes 2359304 | tf_op jit(solution)/shard_map/ppermute | solution.py:26
  62.9 28.6 %collective-permute-start.14 = (bf16[3,128,1024]{2,1,0:T(8,128)(2,1)S(1)}, bf16[3,128,1024]{2,1,0:T(8,128)(2,1)S(1)}, u32[]{:S(2)}, u32[]{:S(2)}) collective-permute-start(bf16[3,128,1024]{2,1,0:T(8,128)(2,1)S(1)} %get-tuple-element.114), channel_id=1, source_target_pairs={{8,0},{12,4},{16,8},{20,12},{24,16},{28,20},{32,24},{36,28},{40,32... | collective-permute-start | bytes 2359304 | tf_op jit(solution)/shard_map/ppermute | solution.py:26
  64.2 11.0 %collective-permute-start.8 = (f32[8,1024]{1,0:T(8,128)S(1)}, f32[8,1024]{1,0:T(8,128)S(1)}, u32[]{:S(2)}, u32[]{:S(2)}) collective-permute-start(f32[8,1024]{1,0:T(8,128)S(1)} %add_add_fusion.2), channel_id=1, source_target_pairs={{0,3},{1,2},{2,1},{3,0},{4,7},{5,6},{6,5},{7,4},{8,11},{9,10},{10,... | collective-permute-start | bytes 98312 | tf_op jit(solution)/shard_map/ppermute | solution.py:31
  66.8 8.4 %collective-permute-start.7 = (f32[8,1024]{1,0:T(8,128)S(1)}, f32[8,1024]{1,0:T(8,128)S(1)}, u32[]{:S(2)}, u32[]{:S(2)}) collective-permute-start(f32[8,1024]{1,0:T(8,128)S(1)} %add_add_fusion.2), channel_id=1, source_target_pairs={{0,2},{1,3},{2,0},{3,1},{4,6},{5,7},{6,4},{7,5},{8,10},{9,11},{10,... | collective-permute-start | bytes 98312 | tf_op jit(solution)/shard_map/ppermute | solution.py:31
  67.3 7.9 %collective-permute-start.6 = (f32[8,1024]{1,0:T(8,128)S(1)}, f32[8,1024]{1,0:T(8,128)S(1)}, u32[]{:S(2)}, u32[]{:S(2)}) collective-permute-start(f32[8,1024]{1,0:T(8,128)S(1)} %add_add_fusion.2), channel_id=1, source_target_pairs={{0,1},{1,0},{2,3},{3,2},{4,5},{5,4},{6,7},{7,6},{8,9},{9,8},{10,11... | collective-permute-start | bytes 98312 | tf_op jit(solution)/shard_map/ppermute | solution.py:31
  75.3 15.2 %collective-permute-start.12 = (f32[8,1024]{1,0:T(8,128)S(1)}, f32[8,1024]{1,0:T(8,128)S(1)}, u32[]{:S(2)}, u32[]{:S(2)}) collective-permute-start(f32[8,1024]{1,0:T(8,128)S(1)} %add_add_fusion.1), channel_id=1, source_target_pairs={{0,96},{4,100},{8,104},{12,108},{16,112},{20,116},{24,120},{28,124... | collective-permute-start | bytes 98312 | tf_op jit(solution)/shard_map/ppermute | solution.py:31
  86.9 4.6 %collective-permute-start.11 = (f32[8,1024]{1,0:T(8,128)S(1)}, f32[8,1024]{1,0:T(8,128)S(1)}, u32[]{:S(2)}, u32[]{:S(2)}) collective-permute-start(f32[8,1024]{1,0:T(8,128)S(1)} %add_add_fusion.1), channel_id=1, source_target_pairs={{0,64},{4,68},{8,72},{12,76},{16,80},{20,84},{24,88},{28,92},{32,9... | collective-permute-start | bytes 98312 | tf_op jit(solution)/shard_map/ppermute | solution.py:31
  86.9 4.6 %collective-permute-start.10 = (f32[8,1024]{1,0:T(8,128)S(1)}, f32[8,1024]{1,0:T(8,128)S(1)}, u32[]{:S(2)}, u32[]{:S(2)}) collective-permute-start(f32[8,1024]{1,0:T(8,128)S(1)} %add_add_fusion.1), channel_id=1, source_target_pairs={{0,32},{4,36},{8,40},{12,44},{16,48},{20,52},{24,56},{28,60},{32,0... | collective-permute-start | bytes 98312 | tf_op jit(solution)/shard_map/ppermute | solution.py:31
  95.1 13.2 %collective-permute-start.17 = (bf16[2,4,128,1024]{3,2,1,0:T(8,128)(2,1)S(1)}, bf16[2,4,128,1024]{3,2,1,0:T(8,128)(2,1)}, u32[]{:S(2)}, u32[]{:S(2)}) collective-permute-start(bf16[2,4,128,1024]{3,2,1,0:T(8,128)(2,1)S(1)} %get-tuple-element.129), channel_id=1, source_target_pairs={{0,4},{4,0},{8,12},{12,8},{16,20},{20,16},{24,28},{28,24},{32,36},... | collective-permute-start | bytes 6291464 | tf_op jit(solution)/shard_map/ppermute | solution.py:31
  100.1 7.5 %collective-permute-start.15 = (f32[8,1024]{1,0:T(8,128)S(1)}, f32[8,1024]{1,0:T(8,128)S(1)}, u32[]{:S(2)}, u32[]{:S(2)}) collective-permute-start(f32[8,1024]{1,0:T(8,128)S(1)} %add_add_fusion), channel_id=1, source_target_pairs={{0,128},{4,132},{8,136},{12,140},{16,144},{20,148},{24,152},{28,15... | collective-permute-start | bytes 98312 | tf_op jit(solution)/shard_map/ppermute | solution.py:31
  107.6 3.7 %collective-permute-start.16 = (f32[8,1024]{1,0:T(8,128)S(1)}, f32[8,1024]{1,0:T(8,128)S(1)}, u32[]{:S(2)}, u32[]{:S(2)}) collective-permute-start(f32[8,1024]{1,0:T(8,128)S(1)} %broadcast_multiply_fusion), channel_id=1, source_target_pairs={{0,4},{4,0},{8,12},{12,8},{16,20},{20,16},{24,28},{28,24},{32,36},... | collective-permute-start | bytes 98312 | tf_op jit(solution)/shard_map/ppermute | solution.py:31

commit v4 on v3

--- a/solution.py
+++ b/solution.py
@@ -14,10 +14,12 @@
 BF = jnp.bfloat16
 F32 = jnp.float32
 VMEM_LIMIT = 8 * 1024 * 1024
-
-
-def params():
-    return pltpu.CompilerParams(vmem_limit_bytes=VMEM_LIMIT)
+LEAD_LIMIT = 56 * 1024 * 1024
+REST_LIMIT = 50 * 1024 * 1024
+
+
+def params(limit=VMEM_LIMIT):
+    return pltpu.CompilerParams(vmem_limit_bytes=limit)
 
 
 def shifted(value, axis, steps):
@@ -47,66 +49,131 @@
 VMEM = pl.BlockSpec(memory_space=pltpu.VMEM)
 
 
-def prep_body(meta, gate, cot, x, cot_all, w_out, send, cot_out, w_other, sems):
-    slots, rows, half = w_other.shape
-    step = pl.program_id(0)
-    other = pl.ds(pl.multiple_of((1 - meta[3]) * half, half), half)
-    copies = [
-        pltpu.make_async_copy(x.at[:, :, other], send.at[0], sems.at[0]),
-        pltpu.make_async_copy(cot_all.at[:, :, other], cot_out, sems.at[1]),
-    ]
-
-    @pl.when(step == 0)
-    def _():
-        for copy in copies:
-            copy.start()
-
-    w_out[0] = (gate[0].astype(F32) * cot[0].astype(F32)).astype(BF)
-    w_other[step] = w_out[0, :, other]
-    pltpu.make_async_copy(w_other.at[step], send.at[1, step], sems.at[2 + step]).start()
-
-    @pl.when(step == slots - 1)
-    def _():
-        for copy in copies:
-            copy.wait()
-        for s in range(slots):
-            pltpu.make_async_copy(w_other.at[s], send.at[1, s], sems.at[2 + s]).wait()
-
-
-def prep(meta, gate, cot, x):
+HBM = pl.BlockSpec(memory_space=pltpu.HBM)
+
+
+def lower_bound(owner, value):
+    low, high = jnp.int32(0), jnp.int32(owner.shape[0])
+    for _ in range(owner.shape[0].bit_length()):
+        middle = jnp.minimum((low + high) // 2, owner.shape[0] - 1)
+        below = (owner[middle] < value) & (low < high)
+        low, high = jnp.where(below, middle + 1, low), jnp.where(below, high, jnp.minimum(high, middle))
+    return low
+
+
+def halves_body(mine, me, gate, cot, x, x_out, cot_out, gates, sems):
+    slots, _, half = gates.shape
+    core = me % 2 if mine else 1 - me % 2
+    lanes = pl.ds(pl.multiple_of(core * half, half), half)
+    copies = []
+    for which, (source, target) in enumerate(((gate, gates), (cot, cot_out), (x, x_out))):
+        copies.append(
+            [pltpu.make_async_copy(source.at[s, :, lanes], target.at[s], sems.at[which * slots + s]) for s in range(slots)]
+        )
+    for s in range(slots):
+        copies[0][s].start()
+        copies[1][s].start()
+    for s in range(slots):
+        copies[2][s].start()
+    return copies
+
+
+def product_body(copies, gates, cot_out, w_out):
+    for s in range(gates.shape[0]):
+        copies[0][s].wait()
+        copies[1][s].wait()
+        w_out[s] = (gates[s].astype(F32) * cot_out[s].astype(F32)).astype(BF)
+    for copy in copies[2]:
+        copy.wait()
+
+
+def lead_body(me, owner, gate, cot, x, send, meta, gates, cots, sems):
+    copies = halves_body(False, me[0], gate, cot, x, send.at[0], cots, gates, sems)
+    core = me[0] % 2
+    base = me[0] - core
+    for i in range(3):
+        meta[i] = lower_bound(owner, base + i)
+    meta[3] = core
+    for i in range(4, 8):
+        meta[i] = 0
+    product_body(copies, gates, cots, send.at[1])
+
+
+def lead(me, owner, gate, cot, x):
     slots, rows, width = x.shape
     half = width // 2
-    full = pl.BlockSpec((1, rows, width), lambda s, m: (s, 0, 0))
-    loose = pl.BlockSpec(memory_space=pl.ANY)
-    return pl.pallas_call(
-        prep_body,
-        grid_spec=pltpu.PrefetchScalarGridSpec(
-            num_scalar_prefetch=1,
-            grid=(slots,),
-            in_specs=[full, full, loose, loose],
-            out_specs=[full, loose, loose],
-            scratch_shapes=[
-                pltpu.VMEM((slots, rows, half), BF),
-                pltpu.SemaphoreType.DMA((2 + slots,)),
-            ],
-        ),
+    return pl.pallas_call(
+        lead_body,
+        in_specs=[SMEM, SMEM, HBM, HBM, HBM],
+        out_specs=[VMEM, SMEM],
+        scratch_shapes=[pltpu.VMEM((slots, rows, half), BF)] * 2 + [pltpu.SemaphoreType.DMA((3 * slots,))],
         out_shape=[
-            jax.ShapeDtypeStruct(x.shape, BF),
             jax.ShapeDtypeStruct((2, slots, rows, half), BF),
-            jax.ShapeDtypeStruct((slots, rows, half), BF),
-        ],
-        compiler_params=params(),
-        cost_estimate=pl.CostEstimate(flops=2 << 20, bytes_accessed=12 << 20, transcendentals=0),
-        name="prep",
-    )(meta, gate, cot, x, cot)
+            jax.ShapeDtypeStruct((8,), jnp.int32),
+        ],
+        compiler_params=params(LEAD_LIMIT),
+        cost_estimate=pl.CostEstimate(flops=1 << 20, bytes_accessed=6 << 20, transcendentals=0),
+        name="lead",
+    )(me, owner, gate, cot, x)
+
+
+READS = 16
+
+
+def rest_body(meta, support, gate, cot, x, x_out, w_out, cot_out, cot_send, reach, gates, sems):
+    copies = halves_body(True, meta[3], gate, cot, x, x_out, cot_out, gates, sems)
+    slots, _, half = gates.shape
+    other = pl.ds(pl.multiple_of((1 - meta[3]) * half, half), half)
+    extra = [
+        pltpu.make_async_copy(cot.at[s, :, other], cot_send.at[s], sems.at[3 * slots + s]) for s in range(slots)
+    ]
+    for copy in extra:
+        copy.start()
+    lags, total = support.shape
+    first = meta[0]
+    cap = 2 * gates.shape[0]
+    for s in range(-NEAR, cap):
+        tile = first + s
+        found = jnp.int32(0)
+        for lag in range(lags):
+            at = jnp.clip(tile + lag, 0, total - 1)
+            found += ((tile >= 0) & (tile + lag < total) & (support[lag, at] >= 0)).astype(jnp.int32)
+        reach[s + NEAR] = found
+    for i in range(cap):
+        at = jnp.clip(first + i, 0, total - 1)
+        found = jnp.int32(0)
+        for lag in range(lags):
+            found += (support[lag, at] >= 0).astype(jnp.int32)
+        reach[READS + i] = found
+    for i in range(NEAR + cap, READS):
+        reach[i] = 0
+    for i in range(READS + cap, 2 * READS):
+        reach[i] = 0
+    product_body(copies, gates, cot_out, w_out)
+    for copy in extra:
+        copy.wait()
+
+
+def rest(meta, support, gate, cot, x):
+    slots, rows, width = x.shape
+    half = width // 2
+    return pl.pallas_call(
+        rest_body,
+        in_specs=[SMEM, SMEM, HBM, HBM, HBM],
+        out_specs=[VMEM, VMEM, VMEM, VMEM, SMEM],
+        scratch_shapes=[pltpu.VMEM((slots, rows, half), BF), pltpu.SemaphoreType.DMA((4 * slots,))],
+        out_shape=[jax.ShapeDtypeStruct((slots, rows, half), BF)] * 4
+        + [jax.ShapeDtypeStruct((2 * READS,), jnp.int32)],
+        compiler_params=params(REST_LIMIT),
+        cost_estimate=pl.CostEstimate(flops=1 << 20, bytes_accessed=6 << 20, transcendentals=0),
+        name="rest",
+    )(meta, support, gate, cot, x)
 
 
 def pack_body(tiles, x_at, w_at, halos, meta, x, w, theirs, *rest):
     x_halos, w_halos = rest[:halos], rest[halos : 2 * halos]
     x_out, w_out, sems = rest[2 * halos :]
-    half = x_out.shape[2]
-    _, _, count, core = chip_meta(meta)
-    lanes = pl.ds(pl.multiple_of(core * half, half), half)
+    _, _, count, _ = chip_meta(meta)
     for which, (own, out) in enumerate(((x, x_out), (w, w_out))):
         for j in range(tiles):
             sem = sems.at[which * tiles + j]
@@ -117,7 +184,7 @@
 
             @pl.when(here & mine)
             def _():
-                pltpu.make_async_copy(own.at[slot, :, lanes], out.at[j], sem).start()
+                pltpu.make_async_copy(own.at[slot], out.at[j], sem).start()
 
             @pl.when(here & jnp.logical_not(mine))
             def _():
@@ -138,33 +205,19 @@
 
 
 def pack(meta, x, w, theirs, tiles, x_at, w_at, x_halos=(), w_halos=()):
-    slots, rows, width = x.shape
-    half = width // 2
+    _, rows, half = x.shape
     halos = len(x_halos)
     loose = pl.BlockSpec(memory_space=pl.ANY)
     return pl.pallas_call(
         functools.partial(pack_body, tiles, x_at, w_at, halos),
-        grid_spec=pltpu.PrefetchScalarGridSpec(
-            num_scalar_prefetch=1,
-            grid=(1,),
-            in_specs=[loose] * (3 + 2 * halos),
-            out_specs=[loose, loose],
-            scratch_shapes=[pltpu.SemaphoreType.DMA((2 * tiles,))],
-        ),
+        in_specs=[SMEM] + [loose] * (3 + 2 * halos),
+        out_specs=[loose, loose],
+        scratch_shapes=[pltpu.SemaphoreType.DMA((2 * tiles,))],
         out_shape=[jax.ShapeDtypeStruct((tiles, rows, half), BF)] * 2,
         compiler_params=params(),
         cost_estimate=pl.CostEstimate(flops=0, bytes_accessed=tiles << 20, transcendentals=0),
         name="pack",
     )(meta, x, w, theirs, *x_halos, *w_halos)
-
-
-def readers_of(table, tile, total):
-    live = (tile >= 0) & (tile < total)
-    return jnp.where(live, table[total + jnp.clip(tile, 0, total - 1)], 0)
-
-
-def sources_of(table, tile, total):
-    return table[jnp.clip(tile, 0, total - 1)]
 
 
 def kept(live, tile):
@@ -194,9 +247,9 @@
     return pl.ds(pl.multiple_of(group * GROUP, GROUP), GROUP)
 
 
-def pick(mine, theirs, meta, index, group, groups):
+def pick(mine, theirs, meta, index, group):
     own, slot = place(meta, index)
-    return jnp.where(own, mine[slot, :, lanes_of(meta[3] * groups + group)], theirs[slot, :, lanes_of(group)])
+    return jnp.where(own, mine[slot, :, lanes_of(group)], theirs[slot, :, lanes_of(group)])
 
 
 def band(row, shift):
@@ -205,13 +258,13 @@
     return pltpu.roll(spread, shift, 1, stride=1, stride_axis=0)[:, :width].astype(BF)
 
 
-def own_body(lags, total, base, steps, groups, meta, table, filt, x, theirs, w,
+def own_body(lags, base, steps, groups, meta, reach, filt, x, theirs, w,
              conv_out, adj_out, fwd_out, bwd_out, sums_out, flip, xs, xl, ws, turned):
     cap, rows, _ = xs.shape
-    first, _, count, _ = chip_meta(meta)
+    _, _, count, _ = chip_meta(meta)
     width = filt.shape[1]
-    ahead = [jnp.minimum(readers_of(table, first + s, total), count - s) for s in range(cap)]
-    behind = [sources_of(table, first + i, total) for i in range(cap)]
+    ahead = [jnp.minimum(reach[s + NEAR], count - s) for s in range(cap)]
+    behind = [reach[READS + i] for i in range(cap)]
     mine = filt[pl.ds(pl.multiple_of(meta[3] * groups, groups), groups), :].astype(BF)
     for k in range(lags):
         block = mine[:, (lags - 1 - k) * rows : (lags - k) * rows]
@@ -223,10 +276,10 @@
         bwd_out[step] = band(filt[row, :].astype(BF).astype(F32), 0)
         fwd_out[step] = band(flip[pl.ds(group, 1), :], width + 1)
         for s in range(cap):
-            tile = pick(x, theirs.at[0], meta, s, group, groups)
+            tile = pick(x, theirs.at[0], meta, s, group)
             xs[s] = tile
             xl[:, s * rows : (s + 1) * rows] = tile
-            tile = pick(w, theirs.at[1], meta, s, group, groups)
+            tile = pick(w, theirs.at[1], meta, s, group)
             ws[s] = tile
             turned[s] = tile.T
         lanes = lanes_of(step)
@@ -251,13 +304,13 @@
     lax.fori_loop(0, steps, one, 0)
 
 
-def own_pairs(meta, table, filt, x, w, theirs, lags, base, steps):
-    slots, rows, width = x.shape
-    groups = width // 2 // GROUP
+def own_pairs(meta, reach, filt, x, w, theirs, lags, base, steps):
+    slots, rows, half = x.shape
+    groups = half // GROUP
     taps = filt.shape[1]
     cap = 2 * slots
     return pl.pallas_call(
-        functools.partial(own_body, lags, table.shape[0] // 2, base, steps, groups),
+        functools.partial(own_body, lags, base, steps, groups),
         in_specs=[SMEM, SMEM] + [VMEM] * 4,
         out_specs=[VMEM] * 5,
         scratch_shapes=[
@@ -277,19 +330,19 @@
         compiler_params=params(),
         cost_estimate=pl.CostEstimate(flops=steps * 1_000_000_000, bytes_accessed=steps << 20, transcendentals=0),
         name="own_pairs",
-    )(meta, table, filt, x, theirs, w)
-
-
-def cross_body(lags, total, groups, meta, table, prior, more, x, theirs, w, xn, wn,
+    )(meta, reach, filt, x, theirs, w)
+
+
+def cross_body(lags, norm, meta, reach, prior, more, x, theirs, w, xn, wn,
                sums_out, xl, near, deep):
     rows = xl.shape[0]
     blocks = lags - 1
-    first, _, count, _ = chip_meta(meta)
+    _, _, count, _ = chip_meta(meta)
     split = blocks - NEAR
     found = []
     for p in range(blocks):
         s = p - blocks if p >= split else count - 1 - (blocks - 1 - p)
-        number = readers_of(table, first + s, total)
+        number = reach[s + NEAR]
         found.append(number if p >= split else jnp.where(s >= 0, number, 0))
     steps = prior.shape[0]
     for part in range(2):
@@ -300,12 +353,12 @@
             lanes = lanes_of(group)
             for p in range(split):
                 index = count - 1 - (blocks - 1 - p)
-                xl[:, p * rows : (p + 1) * rows] = pick(x, theirs.at[0], meta, index, group, groups)
+                xl[:, p * rows : (p + 1) * rows] = pick(x, theirs.at[0], meta, index, group)
             for p in range(NEAR):
                 at = split + p
                 xl[:, at * rows : (at + 1) * rows] = xn[p, :, lanes]
             for t in range(blocks):
-                tile = pick(w, theirs.at[1], meta, t, group, groups)
+                tile = pick(w, theirs.at[1], meta, t, group)
                 if t >= NEAR:
                     tile = jnp.where(t < count, tile, wn[jnp.clip(t - count, 0, PIECE - 1), :, lanes])
                 near[t] = tile.T
@@ -327,19 +380,19 @@
                 right = [jnp.concatenate([tile_at(p, k), tile_at(p, k + 1)], axis=1) for p in range(low, blocks)]
                 squares.append(dot(back[:, low * rows :], jnp.concatenate(right, axis=0)))
             total_sum = diagonal_sums(jnp.concatenate(squares, axis=1))
-            sums_out[pl.ds(group, 1), :] = source[pl.ds(step, 1), :] + total_sum
+            sums_out[pl.ds(group, 1), :] = (source[pl.ds(step, 1), :] + total_sum) * norm
             return carry
 
-        lax.fori_loop(0, steps, one, 0)
-
-
-def cross_squares(meta, table, prior, more, x, w, theirs, x_halo, w_halo, lags):
-    slots, rows, width = x.shape
-    groups = width // 2 // GROUP
+        lax.fori_loop(0, steps, one, 0, unroll=2)
+
+
+def cross_squares(meta, reach, prior, more, x, w, theirs, x_halo, w_halo, lags, norm):
+    slots, rows, half = x.shape
+    groups = half // GROUP
     taps = prior.shape[1]
     blocks = lags - 1
     return pl.pallas_call(
-        functools.partial(cross_body, lags, table.shape[0] // 2, groups),
+        functools.partial(cross_body, lags, norm),
         in_specs=[SMEM, SMEM] + [VMEM] * 7,
         out_specs=VMEM,
         scratch_shapes=[
@@ -351,18 +404,18 @@
         compiler_params=params(),
         cost_estimate=pl.CostEstimate(flops=3_000_000_000, bytes_accessed=6 << 20, transcendentals=0),
         name="cross_squares",
-    )(meta, table, prior, more, x, theirs, w, x_halo, w_halo)
-
-
-def near_body(lags, total, groups, meta, table, conv_a, conv_b, adj_a, adj_b, fwd_a, fwd_b, bwd_a, bwd_b,
+    )(meta, reach, prior, more, x, theirs, w, x_halo, w_halo)
+
+
+def near_body(lags, meta, reach, conv_a, conv_b, adj_a, adj_b, fwd_a, fwd_b, bwd_a, bwd_b,
               xn, wn, cot, cot_t, gate_out, input_out, send_out, conv_out, adj_out, accum):
     slots, rows, _ = gate_out.shape
     cap = 2 * slots
-    first, low, count, core = chip_meta(meta)
+    _, low, count, core = chip_meta(meta)
     high = count - low
     blocks = lags - 1
-    behind = [sources_of(table, first + i, total) for i in range(blocks)]
-    ahead = [readers_of(table, first + count - 1 - c, total) for c in range(blocks)]
+    behind = [reach[READS + i] for i in range(blocks)]
+    ahead = [reach[NEAR + count - 1 - c] for c in range(blocks)]
     steps = fwd_a.shape[0]
     for part in range(2):
         conv, adj, fwd, bwd = ((conv_a, adj_a, fwd_a, bwd_a), (conv_b, adj_b, fwd_b, bwd_b))[part]
@@ -398,7 +451,7 @@
                     second = core if own else 1 - core
                     index = jnp.minimum(slot + second * low, cap - 1)
                     live = slot < jnp.where(second == 1, high, low)
-                    cot_tile = cot[slot, :, lanes_of(core * groups + group)] if own else cot_t[slot, :, lanes]
+                    cot_tile = (cot if own else cot_t)[slot, :, lanes]
                     grad = jnp.where(live, cot_tile.astype(F32) * accum[index], 0.0).astype(BF)
                     sum_ = adj[index, :, local] + accum[cap + blocks + index]
                     back = jnp.where(live, sum_, 0.0).astype(BF)
@@ -413,13 +466,12 @@
         lax.fori_loop(0, steps, one, 0)
 
 
-def near_pairs(meta, table, one, two, x_halo, w_halo, cot, cot_theirs, lags):
-    slots, rows, width = cot.shape
-    half = width // 2
+def near_pairs(meta, reach, one, two, x_halo, w_halo, cot, cot_theirs, lags):
+    slots, rows, half = cot.shape
     far = lags - 1 - NEAR
     pieces = [value for pair in zip(one, two) for value in pair]
     return pl.pallas_call(
-        functools.partial(near_body, lags, table.shape[0] // 2, half // GROUP),
+        functools.partial(near_body, lags),
         in_specs=[SMEM, SMEM] + [VMEM] * 12,
         out_specs=[VMEM] * 5,
         scratch_shapes=[
@@ -435,15 +487,15 @@
         compiler_params=params(),
         cost_estimate=pl.CostEstimate(flops=3_000_000_000, bytes_accessed=8 << 20, transcendentals=0),
         name="near_pairs",
-    )(meta, table, *pieces, x_halo, w_halo, cot, cot_theirs)
-
-
-def far_body(lags, total, groups, meta, table, conv, adj, fwd_a, fwd_b, bwd_a, bwd_b, xf, wf, cot, cot_t,
+    )(meta, reach, *pieces, x_halo, w_halo, cot, cot_theirs)
+
+
+def far_body(lags, meta, reach, conv, adj, fwd_a, fwd_b, bwd_a, bwd_b, xf, wf, cot, cot_t,
              gate_in, input_in, send_in, gate_out, input_out, send_out):
     far, rows, _ = xf.shape
-    first, _, count, _ = chip_meta(meta)
-    behind = [sources_of(table, first + i, total) for i in range(far)]
-    ahead = [readers_of(table, first + count - 1 - c, total) for c in range(far)]
+    _, _, count, _ = chip_meta(meta)
+    behind = [reach[READS + i] for i in range(far)]
+    ahead = [reach[NEAR + count - 1 - c] for c in range(far)]
     steps = fwd_a.shape[0]
     for part in range(2):
         fwd, bwd = ((fwd_a, bwd_a), (fwd_b, bwd_b))[part]
@@ -457,7 +509,7 @@
             for i in range(far):
                 right = [kept(lags - 1 + i - p < behind[i], xs[p]) for p in range(i, far)]
                 term = dot(fwd[step, :, : (far - i) * rows], jnp.concatenate(right, axis=0))
-                value = pick(cot, cot_t, meta, i, group, groups).astype(F32) * (conv[i, :, lanes] + term)
+                value = pick(cot, cot_t, meta, i, group).astype(F32) * (conv[i, :, lanes] + term)
                 results.append((i, gate_out, 0, value.astype(BF)))
             for c in range(far):
                 right = [kept(c + NEAR + 1 + a < ahead[c], ws[a]) for a in range(far - c)]
@@ -479,11 +531,10 @@
         lax.fori_loop(0, steps, one, 0)
 
 
-def far_pairs(meta, table, conv, adj, one, two, x_halo, w_halo, cot, cot_theirs, gate, inp, send, lags):
-    width = cot.shape[2]
+def far_pairs(meta, reach, conv, adj, one, two, x_halo, w_halo, cot, cot_theirs, gate, inp, send, lags):
     pieces = [one[2], two[2], one[3], two[3]]
     return pl.pallas_call(
-        functools.partial(far_body, lags, table.shape[0] // 2, width // 2 // GROUP),
+        functools.partial(far_body, lags),
         in_specs=[SMEM, SMEM] + [VMEM] * 13,
         out_specs=[VMEM] * 3,
         out_shape=[
@@ -495,7 +546,7 @@
         compiler_params=params(),
         cost_estimate=pl.CostEstimate(flops=800_000_000, bytes_accessed=4 << 20, transcendentals=0),
         name="far_pairs",
-    )(meta, table, conv, adj, *pieces, x_halo, w_halo, cot, cot_theirs, gate, inp, send)
+    )(meta, reach, conv, adj, *pieces, x_halo, w_halo, cot, cot_theirs, gate, inp, send)
 
 
 def settle_body(mine, meta, gate, inp, gate_in, input_in, gate_out, input_out, sems):
@@ -530,23 +581,31 @@
     )(meta, gate, inp)
 
 
-def join(meta, got, gate, inp):
+def join(meta, got, gate, inp, sums, moved):
     slots = gate.shape[0]
-
-    def body(meta, got, gate_in, input_in, gate_out, input_out, sems):
+    groups, taps = sums.shape
+
+    def body(meta, got, gate_in, input_in, sums, pair, other, other_pair, gate_out, input_out, filter_out, sems):
+        core = meta[3]
+        filter_out[pl.ds(pl.multiple_of(core * groups, groups), groups), :] = sums[...] + pair[...]
+        filter_out[pl.ds(pl.multiple_of((1 - core) * groups, groups), groups), :] = other[...] + other_pair[...]
         settle_body(False, meta, got.at[0], got.at[1], gate_in, input_in, gate_out, input_out, sems)
 
     loose = pl.BlockSpec(memory_space=pl.ANY)
     return pl.pallas_call(
         body,
-        in_specs=[SMEM, VMEM, loose, loose],
-        out_specs=[loose, loose],
+        in_specs=[SMEM, VMEM, loose, loose, VMEM, VMEM, VMEM, VMEM],
+        out_specs=[loose, loose, VMEM],
         scratch_shapes=[pltpu.SemaphoreType.DMA((2 * slots,))],
-        out_shape=[jax.ShapeDtypeStruct(gate.shape, BF)] * 2,
+        out_shape=[
+            jax.ShapeDtypeStruct(gate.shape, BF),
+            jax.ShapeDtypeStruct(inp.shape, BF),
+            jax.ShapeDtypeStruct((2 * groups, taps), F32),
+        ],
         input_output_aliases={2: 0, 3: 1},
         compiler_params=params(),
         name="join",
-    )(meta, got, gate, inp)
+    )(meta, got, gate, inp, sums, *moved)
 
 
 def per_device(conv_input, gate_signal, cotangent, filters, tile_owner, support):
@@ -557,14 +616,6 @@
     tie = lax.optimization_barrier
     me = lax.axis_index("ctx")
     core = me % 2
-    entry = jnp.arange(8, dtype=jnp.int32)
-    before = jnp.sum((tile_owner[None, :] < (me - core + entry)[:, None]).astype(jnp.int32), axis=1)
-    meta = jnp.where(entry == 3, core, before)
-
-    behind = jnp.sum((support >= 0).astype(jnp.int32), axis=1)
-    ahead = sum(jnp.pad((behind[k:] > k).astype(jnp.int32), (0, k)) for k in range(lags))
-    table = jnp.concatenate([behind, ahead])
-    meta, table = tie((meta, table))
 
     def up(value):
         return shifted(value, "ctx", 2)
@@ -572,19 +623,20 @@
     def down(value):
         return shifted(value, "ctx", -2)
 
-    w, send, cot_send = prep(meta, gate_signal, cotangent, conv_input)
+    norm = 1.0 / math.sqrt(total * rows * width * lax.axis_size("ch") / filter_count)
+    send, meta = lead(me.reshape(1), tile_owner, gate_signal, cotangent, conv_input)
     theirs = swapped(send, "ctx", 1)
-    x = conv_input
+    x, w, cot, cot_send, reach = rest(meta, support.T, gate_signal, cotangent, conv_input)
     xs, ws = pack(meta, x, w, theirs, PIECE, lambda j, n: n - PIECE + j, lambda j, n: j)
     x0, w0 = up(xs), down(ws)
     cot_theirs = swapped(cot_send, "ctx", 1)
     half_groups = width // 2 // GROUP // 2
-    one = own_pairs(meta, table, filters, x, w, theirs, lags, 0, half_groups)
-    two = own_pairs(meta, table, filters, x, w, theirs, lags, half_groups, half_groups)
+    one = own_pairs(meta, reach, filters, x, w, theirs, lags, 0, half_groups)
+    two = own_pairs(meta, reach, filters, x, w, theirs, lags, half_groups, half_groups)
     x0, w0, one, two = tie((x0, w0, one, two))
     *one, first_sums = one
     *two, second_sums = two
-    sums = cross_squares(meta, table, first_sums, second_sums, x, w, theirs, x0, w0, lags)
+    sums = cross_squares(meta, reach, first_sums, second_sums, x, w, theirs, x0, w0, lags, norm)
 
     def stage(sums, axis, masks, filler):
         moved = [swapped(sums, axis, mask) for mask in masks]
@@ -600,7 +652,7 @@
         )
 
     def close(meta):
-        return near_pairs(meta, table, one, two, x0, w0, cotangent, cot_theirs, lags)
+        return near_pairs(meta, reach, one, two, x0, w0, cot, cot_theirs, lags)
 
     sums, (xs, ws) = stage(sums, "ctx", (2, 4, 6), relay)
     x2, w2 = up(xs), down(ws)
@@ -608,20 +660,14 @@
 
     def finish(meta):
         return far_pairs(
-            meta, table, conv, adj, one, two, x2, w2, cotangent, cot_theirs, gate, inp, back, lags
+            meta, reach, conv, adj, one, two, x2, w2, cot, cot_theirs, gate, inp, back, lags
         )
 
     sums, (gate, inp, back) = stage(sums, "ctx", (8, 16, 24), finish)
     got = swapped(back, "ctx", 1)
-    sums, (gate, inp) = stage(sums, "ctx", (32,), lambda meta: place_mine(meta, gate, inp))
-    norm = 1.0 / math.sqrt(total * rows * width * lax.axis_size("ch") / filter_count)
-    sums = sums * norm
-    partner = swapped(sums, "ctx", 1)
-    gate, inp = join(tie((sums, meta))[1], got, gate, inp)
-    partner, gate, inp = tie((partner, gate, inp))
-    low = jnp.where(core == 0, sums, partner)
-    high = jnp.where(core == 0, partner, sums)
-    return gate, inp, jnp.concatenate([low, high], axis=0)
+    moved = [swapped(sums, "ctx", mask) for mask in (32, 1, 33)]
+    gate, inp = place_mine(tie((sums, meta))[1], gate, inp)
+    return join(meta, got, gate, inp, sums, moved)
 
 
 def solution(mesh):

time: 112 us -> 107 us (0.955)
  waiting for transfers between devices: 23.6 us -> 17.2 us
  Pallas kernels: 42.1 us -> 46.6 us
  local copies, waits for them, and re-layouts: 4.79 us -> 0.67 us
  starting transfers between devices: 37.7 us -> 41 us
  other arithmetic: 2.89 us -> 0.03 us
    ppermute x14 -> x15, waiting for transfers between devices: 14.7 us -> 7.53 us  [swapped(): return lax.ppermute(value, axis, [(a, a ^ mask) for a in range(count)])]
    pallas_call x9 -> x10, Pallas kernels: 40.2 us -> 44.7 us  [the longest x2 15 us: own_pairs(): pl.pallas_call(functools.partial(own_body, lags, base, steps, groups), in...]
    unnamed x12 -> x8, local copies, waits for them, and re-layouts: 4.79 us -> 0.67 us
    ppermute x14 -> x15, starting transfers between devices: 32.3 us -> 35.5 us  [swapped(): return lax.ppermute(value, axis, [(a, a ^ mask) for a in range(count)])]
    reduce_sum x2 -> x0, other arithmetic: 1.58 us -> none  [the longest x1 0.86 us: per_device(): jnp.sum((tile_owner[None, :] < (me - core + entry)[:, None]).astype(jnp.i...]
  transfers between devices with their start and end apart: 18 -> 19, of which waited for: 7 -> 6; matrix products, arithmetic and copies ran while one was open for 0% -> 0% of each run, Pallas kernels for 32% -> 33%
where the time goes in v4:
time: 107 us; the launch traced here: 106 us
  Pallas kernels  46.6 us (44%)
  starting transfers between devices  41 us (38%)
  waiting for transfers between devices  17.2 us (16%)
    ppermute x15, starting transfers between devices, swapped(): return lax.ppermute(value, axis, [(a, a ^ mask) for a in range(count)])  35.5 us
    pallas_call x2, Pallas kernels, own_pairs(): pl.pallas_call(functools.partial(own_body, lags, base, steps, groups), in...  15 us
    ppermute x4, waiting for transfers between devices, shifted(): return lax.ppermute(value, axis, pairs)  9.64 us
    pallas_call x1, Pallas kernels, near_pairs(): pl.pallas_call(functools.partial(near_body, lags), in_specs=[SMEM, SMEM]...  7.53 us
    ppermute x15, waiting for transfers between devices, swapped(): return lax.ppermute(value, axis, [(a, a ^ mask) for a in range(count)])  7.53 us
    pallas_call x1, Pallas kernels, cross_squares(): pl.pallas_call(functools.partial(cross_body, lags, norm), in_specs=[SMEM,...  6.24 us
    ppermute x4, starting transfers between devices, shifted(): return lax.ppermute(value, axis, pairs)  5.53 us
    pallas_call x1, Pallas kernels, lead(): pl.pallas_call(lead_body, in_specs=[SMEM, SMEM, HBM, HBM, HBM], out_specs...  4.15 us
  transfers between devices with their start and end apart: 19, of which 6 were waited for; matrix products, arithmetic and copies ran while one was open for 0% of the time, Pallas kernels for 33%

profile of v4, /device:TPU:1, one launch (start us, length us, event | category | flops | bytes accessed | tf_op | source)
XLA Modules:
  0.0 106.5 jit_solution(5568551673538034259)
XLA Ops:
  0.6 4.1 %lead.1 = (bf16[2,4,128,1024]{3,2,1,0:T(8,128)(2,1)}, s32[8]{0:T(128)}) custom-call(s32[1]{0:T(128)} %bitcast.me, s32[192]{0:T(256)} %owner.1, bf16[4,128,2048]{2,1,0:T(8,128)(2,1)} %gate.3, bf16[4,128,2048]{2,1,0:T(8,128)(2,1)} %cot.3, bf16[4,128,2048]{2,1,0:T(8,128)(2,1)} %x.3), custom_call_target="tpu_custom_call" | custom-call | flops 1048576 | bytes 6291456 | tf_op jit(solution)/shard_map/lead/pallas_call | solution.py:105
  4.8 3.3 %collective-permute-start = (bf16[2,4,128,1024]{3,2,1,0:T(8,128)(2,1)}, bf16[2,4,128,1024]{3,2,1,0:T(8,128)(2,1)S(1)}, u32[]{:S(2)}, u32[]{:S(2)}) collective-permute-start(bf16[2,4,128,1024]{3,2,1,0:T(8,128)(2,1)} %get-tuple-element.67), channel_id=1, source_target_pairs={{0,4},{4,0},{8,12},{12,8},{16,20},{20,16},{24,28},{28,24},{32,36},... | collective-permute-start | bytes 6291464 | tf_op jit(solution)/shard_map/ppermute | solution.py:33
  8.1 0.7 copy-done
  8.8 3.9 %rest.1 = (bf16[4,128,1024]{2,1,0:T(8,128)(2,1)S(1)}, bf16[4,128,1024]{2,1,0:T(8,128)(2,1)S(1)}, bf16[4,128,1024]{2,1,0:T(8,128)(2,1)S(1)}, bf16[4,128,1024]{2,1,0:T(8,128)(2,1)}, s32[32]{0:T(128)S(1)}) custom-call(s32[8]{0:T(128)S(1)} %copy-done, s32[8,192]{1,0:T(8,128)S(1)} %bitcast.2, bf16[4,128,2048]{2,1,0:T(8,128)(2,1)} %gate.3, ...), custom_call_target="tpu_custom_call" | custom-call | flops 1048576 | bytes 6291456 | tf_op jit(solution)/shard_map/rest/pallas_call | solution.py:160
  12.8 0.9 pack.2
  13.7 1.5 %collective-permute-start.1 = (bf16[4,128,1024]{2,1,0:T(8,128)(2,1)S(1)}, bf16[4,128,1024]{2,1,0:T(8,128)(2,1)S(1)}, u32[]{:S(2)}, u32[]{:S(2)}) collective-permute-start(bf16[4,128,1024]{2,1,0:T(8,128)(2,1)S(1)} %get-tuple-element.68), channel_id=1, source_target_pairs={{0,8},{4,12},{8,16},{12,20},{16,24},{20,28},{24,32},{28,36},{32,40... | collective-permute-start | bytes 3145736 | tf_op jit(solution)/shard_map/ppermute | solution.py:28
  15.2 1.3 %collective-permute-start.2 = (bf16[4,128,1024]{2,1,0:T(8,128)(2,1)S(1)}, bf16[4,128,1024]{2,1,0:T(8,128)(2,1)S(1)}, u32[]{:S(2)}, u32[]{:S(2)}) collective-permute-start(bf16[4,128,1024]{2,1,0:T(8,128)(2,1)S(1)} %get-tuple-element.69), channel_id=1, source_target_pairs={{8,0},{12,4},{16,8},{20,12},{24,16},{28,20},{32,24},{36,28},{40,32... | collective-permute-start | bytes 3145736 | tf_op jit(solution)/shard_map/ppermute | solution.py:28
  16.9 7.5 %own_pairs.3 = (f32[8,128,512]{2,1,0:T(8,128)S(1)}, f32[8,128,512]{2,1,0:T(8,128)S(1)}, bf16[4,128,1024]{2,1,0:T(8,128)(2,1)S(1)}, bf16[4,128,1024]{2,1,0:T(8,128)(2,1)S(1)}, f32[4,1024]{1,0:T(4,128)S(1)}) custom-call(s32[8]{0:T(128)S(1)} %copy-done, s32[32]{0:T(128)S(1)} %get-tuple-element.64.reach, f32[16,1024]{1,0:T(8,128)S(1)} %copy-done.2, ...), custom_call_target="tpu_custom_call" | custom-call | flops 4000000000 | bytes 4194304 | tf_op jit(solution)/shard_map/own_pairs/pallas_call | solution.py:312
  24.4 7.5 %own_pairs.2 = (f32[8,128,512]{2,1,0:T(8,128)S(1)}, f32[8,128,512]{2,1,0:T(8,128)S(1)}, bf16[4,128,1024]{2,1,0:T(8,128)(2,1)S(1)}, bf16[4,128,1024]{2,1,0:T(8,128)(2,1)S(1)}, f32[4,1024]{1,0:T(4,128)S(1)}) custom-call(s32[8]{0:T(128)S(1)} %copy-done, s32[32]{0:T(128)S(1)} %get-tuple-element.64.reach, f32[16,1024]{1,0:T(8,128)S(1)} %copy-done.2, ...), custom_call_target="tpu_custom_call" | custom-call | flops 4000000000 | bytes 4194304 | tf_op jit(solution)/shard_map/own_pairs/pallas_call | solution.py:312
  31.9 5.8 %collective-permute-done.1.xn.rest_0_ = bf16[4,128,1024]{2,1,0:T(8,128)(2,1)S(1)} collective-permute-done((bf16[4,128,1024]{2,1,0:T(8,128)(2,1)S(1)}, bf16[4,128,1024]{2,1,0:T(8,128)(2,1)S(1)}, u32[]{:S(2)}, u32[]{:S(2)}) %collective-permute-start.1) | collective-permute-done | bytes 1048608 | tf_op jit(solution)/shard_map/ppermute | solution.py:28
  37.7 3.9 %collective-permute-done.2.wn.rest_1_ = bf16[4,128,1024]{2,1,0:T(8,128)(2,1)S(1)} collective-permute-done((bf16[4,128,1024]{2,1,0:T(8,128)(2,1)S(1)}, bf16[4,128,1024]{2,1,0:T(8,128)(2,1)S(1)}, u32[]{:S(2)}, u32[]{:S(2)}) %collective-permute-start.2) | collective-permute-done | bytes 1048608 | tf_op jit(solution)/shard_map/ppermute | solution.py:28
  41.5 6.2 %cross_squares.1 = f32[8,1024]{1,0:T(8,128)S(1)} custom-call(s32[8]{0:T(128)S(1)} %copy-done, s32[32]{0:T(128)S(1)} %get-tuple-element.64.reach, f32[4,1024]{1,0:T(4,128)S(1)} %get-tuple-element.80.prior, f32[4,1024]{1,0:T(4,128)S(1)} %get-tuple-element.81.more, bf16[4,128,1024]{2,1,0:T(8,128)(2,1)S(1)} %get-tuple-element.65.x, ...), custom_call_target="tpu_custom_call" | custom-call | flops 3000000000 | bytes 6291456 | tf_op jit(solution)/shard_map/cross_squares/pallas_call | solution.py:394
  47.8 4.8 %collective-permute-start.5 = (f32[8,1024]{1,0:T(8,128)S(1)}, f32[8,1024]{1,0:T(8,128)S(1)}, u32[]{:S(2)}, u32[]{:S(2)}) collective-permute-start(f32[8,1024]{1,0:T(8,128)S(1)} %cross_squares.1), channel_id=1, source_target_pairs={{0,24},{4,28},{8,16},{12,20},{16,8},{20,12},{24,0},{28,4},{32,56},... | collective-permute-start | bytes 98312 | tf_op jit(solution)/shard_map/ppermute | solution.py:33
  52.6 0.7 collective-permute-start.3
  53.3 0.8 pack.3
  54.2 2.7 %collective-permute-done.4 = f32[8,1024]{1,0:T(8,128)S(1)} collective-permute-done((f32[8,1024]{1,0:T(8,128)S(1)}, f32[8,1024]{1,0:T(8,128)S(1)}, u32[]{:S(2)}, u32[]{:S(2)}) %collective-permute-start.4) | collective-permute-done | bytes 32800 | tf_op jit(solution)/shard_map/ppermute | solution.py:33
  56.9 1.4 %collective-permute-start.13 = (bf16[3,128,1024]{2,1,0:T(8,128)(2,1)S(1)}, bf16[3,128,1024]{2,1,0:T(8,128)(2,1)S(1)}, u32[]{:S(2)}, u32[]{:S(2)}) collective-permute-start(bf16[3,128,1024]{2,1,0:T(8,128)(2,1)S(1)} %get-tuple-element.108), channel_id=1, source_target_pairs={{0,8},{4,12},{8,16},{12,20},{16,24},{20,28},{24,32},{28,36},{32,40... | collective-permute-start | bytes 2359304 | tf_op jit(solution)/shard_map/ppermute | solution.py:28
  58.3 1.3 %collective-permute-start.14 = (bf16[3,128,1024]{2,1,0:T(8,128)(2,1)S(1)}, bf16[3,128,1024]{2,1,0:T(8,128)(2,1)S(1)}, u32[]{:S(2)}, u32[]{:S(2)}) collective-permute-start(bf16[3,128,1024]{2,1,0:T(8,128)(2,1)S(1)} %get-tuple-element.109), channel_id=1, source_target_pairs={{8,0},{12,4},{16,8},{20,12},{24,16},{28,20},{32,24},{36,28},{40,32... | collective-permute-start | bytes 2359304 | tf_op jit(solution)/shard_map/ppermute | solution.py:28
  59.6 2.7 %collective-permute-start.8 = (f32[8,1024]{1,0:T(8,128)S(1)}, f32[8,1024]{1,0:T(8,128)S(1)}, u32[]{:S(2)}, u32[]{:S(2)}) collective-permute-start(f32[8,1024]{1,0:T(8,128)S(1)} %add_add_fusion.2), channel_id=1, source_target_pairs={{0,3},{1,2},{2,1},{3,0},{4,7},{5,6},{6,5},{7,4},{8,11},{9,10},{10,... | collective-permute-start | bytes 98312 | tf_op jit(solution)/shard_map/ppermute | solution.py:33
  62.4 0.5 collective-permute-start.7
  63.2 7.5 %near_pairs.1 = (bf16[4,128,1024]{2,1,0:T(8,128)(2,1)S(1)}, bf16[4,128,1024]{2,1,0:T(8,128)(2,1)S(1)}, bf16[2,4,128,1024]{3,2,1,0:T(8,128)(2,1)S(1)}, f32[3,128,1024]{2,1,0:T(8,128)S(1)}, f32[3,128,1024]{2,1,0:T(8,128)S(1)}) custom-call(s32[8]{0:T(128)S(1)} %copy-done, s32[32]{0:T(128)S(1)} %get-tuple-element.64.reach, ...), custom_call_target="tpu_custom_call" | custom-call | flops 3000000000 | bytes 8388608 | tf_op jit(solution)/shard_map/near_pairs/pallas_call | solution.py:473
  70.8 11.5 %collective-permute-start.12 = (f32[8,1024]{1,0:T(8,128)S(1)}, f32[8,1024]{1,0:T(8,128)S(1)}, u32[]{:S(2)}, u32[]{:S(2)}) collective-permute-start(f32[8,1024]{1,0:T(8,128)S(1)} %add_add_fusion.1), channel_id=1, source_target_pairs={{0,96},{4,100},{8,104},{12,108},{16,112},{20,116},{24,120},{28,124... | collective-permute-start | bytes 98312 | tf_op jit(solution)/shard_map/ppermute | solution.py:33
  82.7 3.5 %collective-permute-done.12 = f32[8,1024]{1,0:T(8,128)S(1)} collective-permute-done((f32[8,1024]{1,0:T(8,128)S(1)}, f32[8,1024]{1,0:T(8,128)S(1)}, u32[]{:S(2)}, u32[]{:S(2)}) %collective-permute-start.12) | collective-permute-done | bytes 32800 | tf_op jit(solution)/shard_map/ppermute | solution.py:33
  86.2 0.6 collective-permute-done.11
  86.8 3.6 %far_pairs.1 = (bf16[4,128,1024]{2,1,0:T(8,128)(2,1)S(1)}, bf16[4,128,1024]{2,1,0:T(8,128)(2,1)S(1)}, bf16[2,4,128,1024]{3,2,1,0:T(8,128)(2,1)S(1)}) custom-call(s32[8]{0:T(128)S(1)} %copy-done, s32[32]{0:T(128)S(1)} %get-tuple-element.64.reach, ...), custom_call_target="tpu_custom_call", output_to_operand_aliasing={{0}: (12, {}), {1}: (13, {}), {2}: (14, {})} | custom-call | flops 800000000 | bytes 4194304 | tf_op jit(solution)/shard_map/far_pairs/pallas_call | solution.py:536
  90.4 5.0 %collective-permute-start.15 = (bf16[2,4,128,1024]{3,2,1,0:T(8,128)(2,1)S(1)}, bf16[2,4,128,1024]{3,2,1,0:T(8,128)(2,1)S(1)}, u32[]{:S(2)}, u32[]{:S(2)}) collective-permute-start(bf16[2,4,128,1024]{3,2,1,0:T(8,128)(2,1)S(1)} %get-tuple-element.116), channel_id=1, source_target_pairs={{0,4},{4,0},{8,12},{12,8},{16,20},{20,16},{24,28},{28,24},{32,36},... | collective-permute-start | bytes 6291464 | tf_op jit(solution)/shard_map/ppermute | solution.py:33
  95.4 1.3 %collective-permute-start.18 = (f32[8,1024]{1,0:T(8,128)S(1)}, f32[8,1024]{1,0:T(8,128)S(1)}, u32[]{:S(2)}, u32[]{:S(2)}) collective-permute-start(f32[8,1024]{1,0:T(8,128)S(1)} %add_add_fusion.sums), channel_id=1, source_target_pairs={{0,132},{4,128},{8,140},{12,136},{16,148},{20,144},{24,156},{28,15... | collective-permute-start | bytes 98312 | tf_op jit(solution)/shard_map/ppermute | solution.py:33
  96.7 0.4 collective-permute-start.17
  97.1 4.1 %collective-permute-start.16 = (f32[8,1024]{1,0:T(8,128)S(1)}, f32[8,1024]{1,0:T(8,128)S(1)}, u32[]{:S(2)}, u32[]{:S(2)}) collective-permute-start(f32[8,1024]{1,0:T(8,128)S(1)} %add_add_fusion.sums), channel_id=1, source_target_pairs={{0,128},{4,132},{8,136},{12,140},{16,144},{20,148},{24,152},{28,15... | collective-permute-start | bytes 98312 | tf_op jit(solution)/shard_map/ppermute | solution.py:33
  101.2 1.9 %place_mine.1 = (bf16[4,128,2048]{2,1,0:T(8,128)(2,1)}, bf16[4,128,2048]{2,1,0:T(8,128)(2,1)}) custom-call(s32[8]{0:T(128)S(1)} %copy-done, bf16[4,128,1024]{2,1,0:T(8,128)(2,1)S(1)} %get-tuple-element.119.gate, bf16[4,128,1024]{2,1,0:T(8,128)(2,1)S(1)} %get-tuple-element.120.inp), custom_call_target="tpu_custom_call" | custom-call | tf_op jit(solution)/shard_map/place_mine/pallas_call | solution.py:573
  103.1 0.7 collective-permute-done.16.pair
  103.8 2.5 %join.1 = (bf16[4,128,2048]{2,1,0:T(8,128)(2,1)}, bf16[4,128,2048]{2,1,0:T(8,128)(2,1)}, f32[16,1024]{1,0:T(8,128)}) custom-call(s32[8]{0:T(128)S(1)} %copy-done, bf16[2,4,128,1024]{3,2,1,0:T(8,128)(2,1)S(1)} %collective-permute-done.15.got, bf16[4,128,2048]{2,1,0:T(8,128)(2,1)} %get-tuple-element.121.gate_in, ...), custom_call_target="tpu_custom_call", output_to_operand_aliasing={{0}: (2, {}), {1}: (3, {})} | custom-call | tf_op jit(solution)/shard_map/join/pallas_call | solution.py:595
  (28 shorter events, 1.1 us)
Async XLA Ops:
  0.6 7.5 %copy-start.1 = (s32[192,8]{0,1:T(8,128)S(1)}, s32[192,8]{0,1:T(8,128)}, u32[]{:S(2)}) copy-start(s32[192,8]{0,1:T(8,128)} %param.11) | copy-start | bytes 18436
  4.8 7.9 %collective-permute-start = (bf16[2,4,128,1024]{3,2,1,0:T(8,128)(2,1)}, bf16[2,4,128,1024]{3,2,1,0:T(8,128)(2,1)S(1)}, u32[]{:S(2)}, u32[]{:S(2)}) collective-permute-start(bf16[2,4,128,1024]{3,2,1,0:T(8,128)(2,1)} %get-tuple-element.67), channel_id=1, source_target_pairs={{0,4},{4,0},{8,12},{12,8},{16,20},{20,16},{24,28},{28,24},{32,36},... | collective-permute-start | bytes 6291464 | tf_op jit(solution)/shard_map/ppermute | solution.py:33
  8.1 0.7 copy-start
  12.7 3.8 %copy-start.3 = (bf16[4,128,1024]{2,1,0:T(8,128)(2,1)S(1)}, bf16[4,128,1024]{2,1,0:T(8,128)(2,1)}, u32[]{:S(2)}) copy-start(bf16[4,128,1024]{2,1,0:T(8,128)(2,1)} %get-tuple-element.98) | copy-start | bytes 3145732
  12.7 4.2 %copy-start.2 = (f32[16,1024]{1,0:T(8,128)S(1)}, f32[16,1024]{1,0:T(8,128)}, u32[]{:S(2)}) copy-start(f32[16,1024]{1,0:T(8,128)} %filt.3) | copy-start | bytes 196612
  13.7 24.0 %collective-permute-start.1 = (bf16[4,128,1024]{2,1,0:T(8,128)(2,1)S(1)}, bf16[4,128,1024]{2,1,0:T(8,128)(2,1)S(1)}, u32[]{:S(2)}, u32[]{:S(2)}) collective-permute-start(bf16[4,128,1024]{2,1,0:T(8,128)(2,1)S(1)} %get-tuple-element.68), channel_id=1, source_target_pairs={{0,8},{4,12},{8,16},{12,20},{16,24},{20,28},{24,32},{28,36},{32,40... | collective-permute-start | bytes 3145736 | tf_op jit(solution)/shard_map/ppermute | solution.py:28
  15.2 26.3 %collective-permute-start.2 = (bf16[4,128,1024]{2,1,0:T(8,128)(2,1)S(1)}, bf16[4,128,1024]{2,1,0:T(8,128)(2,1)S(1)}, u32[]{:S(2)}, u32[]{:S(2)}) collective-permute-start(bf16[4,128,1024]{2,1,0:T(8,128)(2,1)S(1)} %get-tuple-element.69), channel_id=1, source_target_pairs={{8,0},{12,4},{16,8},{20,12},{24,16},{28,20},{32,24},{36,28},{40,32... | collective-permute-start | bytes 3145736 | tf_op jit(solution)/shard_map/ppermute | solution.py:28
  16.5 46.4 %collective-permute-start.9 = (bf16[4,128,1024]{2,1,0:T(8,128)(2,1)S(1)}, bf16[4,128,1024]{2,1,0:T(8,128)(2,1)S(1)}, u32[]{:S(2)}, u32[]{:S(2)}) collective-permute-start(bf16[4,128,1024]{2,1,0:T(8,128)(2,1)S(1)} %copy-done.3), channel_id=1, source_target_pairs={{0,4},{4,0},{8,12},{12,8},{16,20},{20,16},{24,28},{28,24},{32,36},... | collective-permute-start | bytes 3145736 | tf_op jit(solution)/shard_map/ppermute | solution.py:33
  47.8 6.4 %collective-permute-start.5 = (f32[8,1024]{1,0:T(8,128)S(1)}, f32[8,1024]{1,0:T(8,128)S(1)}, u32[]{:S(2)}, u32[]{:S(2)}) collective-permute-start(f32[8,1024]{1,0:T(8,128)S(1)} %cross_squares.1), channel_id=1, source_target_pairs={{0,24},{4,28},{8,16},{12,20},{16,8},{20,12},{24,0},{28,4},{32,56},... | collective-permute-start | bytes 98312 | tf_op jit(solution)/shard_map/ppermute | solution.py:33
  52.6 4.3 %collective-permute-start.4 = (f32[8,1024]{1,0:T(8,128)S(1)}, f32[8,1024]{1,0:T(8,128)S(1)}, u32[]{:S(2)}, u32[]{:S(2)}) collective-permute-start(f32[8,1024]{1,0:T(8,128)S(1)} %cross_squares.1), channel_id=1, source_target_pairs={{0,16},{4,20},{8,24},{12,28},{16,0},{20,4},{24,8},{28,12},{32,48},... | collective-permute-start | bytes 98312 | tf_op jit(solution)/shard_map/ppermute | solution.py:33
  52.6 4.3 %collective-permute-start.3 = (f32[8,1024]{1,0:T(8,128)S(1)}, f32[8,1024]{1,0:T(8,128)S(1)}, u32[]{:S(2)}, u32[]{:S(2)}) collective-permute-start(f32[8,1024]{1,0:T(8,128)S(1)} %cross_squares.1), channel_id=1, source_target_pairs={{0,8},{4,12},{8,0},{12,4},{16,24},{20,28},{24,16},{28,20},{32,40},... | collective-permute-start | bytes 98312 | tf_op jit(solution)/shard_map/ppermute | solution.py:33
  56.9 29.9 %collective-permute-start.13 = (bf16[3,128,1024]{2,1,0:T(8,128)(2,1)S(1)}, bf16[3,128,1024]{2,1,0:T(8,128)(2,1)S(1)}, u32[]{:S(2)}, u32[]{:S(2)}) collective-permute-start(bf16[3,128,1024]{2,1,0:T(8,128)(2,1)S(1)} %get-tuple-element.108), channel_id=1, source_target_pairs={{0,8},{4,12},{8,16},{12,20},{16,24},{20,28},{24,32},{28,36},{32,40... | collective-permute-start | bytes 2359304 | tf_op jit(solution)/shard_map/ppermute | solution.py:28
  58.3 28.5 %collective-permute-start.14 = (bf16[3,128,1024]{2,1,0:T(8,128)(2,1)S(1)}, bf16[3,128,1024]{2,1,0:T(8,128)(2,1)S(1)}, u32[]{:S(2)}, u32[]{:S(2)}) collective-permute-start(bf16[3,128,1024]{2,1,0:T(8,128)(2,1)S(1)} %get-tuple-element.109), channel_id=1, source_target_pairs={{8,0},{12,4},{16,8},{20,12},{24,16},{28,20},{32,24},{36,28},{40,32... | collective-permute-start | bytes 2359304 | tf_op jit(solution)/shard_map/ppermute | solution.py:28
  59.6 11.1 %collective-permute-start.8 = (f32[8,1024]{1,0:T(8,128)S(1)}, f32[8,1024]{1,0:T(8,128)S(1)}, u32[]{:S(2)}, u32[]{:S(2)}) collective-permute-start(f32[8,1024]{1,0:T(8,128)S(1)} %add_add_fusion.2), channel_id=1, source_target_pairs={{0,3},{1,2},{2,1},{3,0},{4,7},{5,6},{6,5},{7,4},{8,11},{9,10},{10,... | collective-permute-start | bytes 98312 | tf_op jit(solution)/shard_map/ppermute | solution.py:33
  62.4 8.3 %collective-permute-start.7 = (f32[8,1024]{1,0:T(8,128)S(1)}, f32[8,1024]{1,0:T(8,128)S(1)}, u32[]{:S(2)}, u32[]{:S(2)}) collective-permute-start(f32[8,1024]{1,0:T(8,128)S(1)} %add_add_fusion.2), channel_id=1, source_target_pairs={{0,2},{1,3},{2,0},{3,1},{4,6},{5,7},{6,4},{7,5},{8,10},{9,11},{10,... | collective-permute-start | bytes 98312 | tf_op jit(solution)/shard_map/ppermute | solution.py:33
  62.9 7.8 %collective-permute-start.6 = (f32[8,1024]{1,0:T(8,128)S(1)}, f32[8,1024]{1,0:T(8,128)S(1)}, u32[]{:S(2)}, u32[]{:S(2)}) collective-permute-start(f32[8,1024]{1,0:T(8,128)S(1)} %add_add_fusion.2), channel_id=1, source_target_pairs={{0,1},{1,0},{2,3},{3,2},{4,5},{5,4},{6,7},{7,6},{8,9},{9,8},{10,11... | collective-permute-start | bytes 98312 | tf_op jit(solution)/shard_map/ppermute | solution.py:33
  70.8 15.5 %collective-permute-start.12 = (f32[8,1024]{1,0:T(8,128)S(1)}, f32[8,1024]{1,0:T(8,128)S(1)}, u32[]{:S(2)}, u32[]{:S(2)}) collective-permute-start(f32[8,1024]{1,0:T(8,128)S(1)} %add_add_fusion.1), channel_id=1, source_target_pairs={{0,96},{4,100},{8,104},{12,108},{16,112},{20,116},{24,120},{28,124... | collective-permute-start | bytes 98312 | tf_op jit(solution)/shard_map/ppermute | solution.py:33
  82.3 4.5 %collective-permute-start.11 = (f32[8,1024]{1,0:T(8,128)S(1)}, f32[8,1024]{1,0:T(8,128)S(1)}, u32[]{:S(2)}, u32[]{:S(2)}) collective-permute-start(f32[8,1024]{1,0:T(8,128)S(1)} %add_add_fusion.1), channel_id=1, source_target_pairs={{0,64},{4,68},{8,72},{12,76},{16,80},{20,84},{24,88},{28,92},{32,9... | collective-permute-start | bytes 98312 | tf_op jit(solution)/shard_map/ppermute | solution.py:33
  82.3 4.5 %collective-permute-start.10 = (f32[8,1024]{1,0:T(8,128)S(1)}, f32[8,1024]{1,0:T(8,128)S(1)}, u32[]{:S(2)}, u32[]{:S(2)}) collective-permute-start(f32[8,1024]{1,0:T(8,128)S(1)} %add_add_fusion.1), channel_id=1, source_target_pairs={{0,32},{4,36},{8,40},{12,44},{16,48},{20,52},{24,56},{28,60},{32,0... | collective-permute-start | bytes 98312 | tf_op jit(solution)/shard_map/ppermute | solution.py:33
  90.4 13.4 %collective-permute-start.15 = (bf16[2,4,128,1024]{3,2,1,0:T(8,128)(2,1)S(1)}, bf16[2,4,128,1024]{3,2,1,0:T(8,128)(2,1)S(1)}, u32[]{:S(2)}, u32[]{:S(2)}) collective-permute-start(bf16[2,4,128,1024]{3,2,1,0:T(8,128)(2,1)S(1)} %get-tuple-element.116), channel_id=1, source_target_pairs={{0,4},{4,0},{8,12},{12,8},{16,20},{20,16},{24,28},{28,24},{32,36},... | collective-permute-start | bytes 6291464 | tf_op jit(solution)/shard_map/ppermute | solution.py:33
  95.4 7.7 %collective-permute-start.18 = (f32[8,1024]{1,0:T(8,128)S(1)}, f32[8,1024]{1,0:T(8,128)S(1)}, u32[]{:S(2)}, u32[]{:S(2)}) collective-permute-start(f32[8,1024]{1,0:T(8,128)S(1)} %add_add_fusion.sums), channel_id=1, source_target_pairs={{0,132},{4,128},{8,140},{12,136},{16,148},{20,144},{24,156},{28,15... | collective-permute-start | bytes 98312 | tf_op jit(solution)/shard_map/ppermute | solution.py:33
  96.7 6.4 %collective-permute-start.17 = (f32[8,1024]{1,0:T(8,128)S(1)}, f32[8,1024]{1,0:T(8,128)S(1)}, u32[]{:S(2)}, u32[]{:S(2)}) collective-permute-start(f32[8,1024]{1,0:T(8,128)S(1)} %add_add_fusion.sums), channel_id=1, source_target_pairs={{0,4},{4,0},{8,12},{12,8},{16,20},{20,16},{24,28},{28,24},{32,36},... | collective-permute-start | bytes 98312 | tf_op jit(solution)/shard_map/ppermute | solution.py:33
  97.1 6.7 %collective-permute-start.16 = (f32[8,1024]{1,0:T(8,128)S(1)}, f32[8,1024]{1,0:T(8,128)S(1)}, u32[]{:S(2)}, u32[]{:S(2)}) collective-permute-start(f32[8,1024]{1,0:T(8,128)S(1)} %add_add_fusion.sums), channel_id=1, source_target_pairs={{0,128},{4,132},{8,136},{12,140},{16,144},{20,148},{24,152},{28,15... | collective-permute-start | bytes 98312 | tf_op jit(solution)/shard_map/ppermute | solution.py:33

commit v5 on v4

--- a/solution.py
+++ b/solution.py
@@ -10,7 +10,7 @@
 
 GROUP = 128
 NEAR = 4
-PIECE = 4
+ABOVE = 3
 BF = jnp.bfloat16
 F32 = jnp.float32
 VMEM_LIMIT = 8 * 1024 * 1024
@@ -170,13 +170,13 @@
     )(meta, support, gate, cot, x)
 
 
-def pack_body(tiles, x_at, w_at, halos, meta, x, w, theirs, *rest):
+def pack_body(x_tiles, w_tiles, x_at, w_at, halos, meta, x, w, theirs, *rest):
     x_halos, w_halos = rest[:halos], rest[halos : 2 * halos]
     x_out, w_out, sems = rest[2 * halos :]
     _, _, count, _ = chip_meta(meta)
     for which, (own, out) in enumerate(((x, x_out), (w, w_out))):
-        for j in range(tiles):
-            sem = sems.at[which * tiles + j]
+        for j in range((x_tiles, w_tiles)[which]):
+            sem = sems.at[which * x_tiles + j]
             index = (x_at if which == 0 else w_at)(j, count)
             mine, slot = place(meta, index)
             depth = -1 - index if which == 0 else index - count
@@ -192,30 +192,30 @@
 
             for h in range(halos):
                 halo = (x_halos if which == 0 else w_halos)[h]
-                inside = jnp.clip(depth - h * PIECE, 0, PIECE - 1)
-                row = PIECE - 1 - inside if which == 0 else inside
-
-                @pl.when((depth >= h * PIECE) & (depth < (h + 1) * PIECE))
+                inside = jnp.clip(depth - h * NEAR, 0, NEAR - 1)
+                row = NEAR - 1 - inside if which == 0 else inside
+
+                @pl.when((depth >= h * NEAR) & (depth < (h + 1) * NEAR))
                 def _():
                     pltpu.make_async_copy(halo.at[row], out.at[j], sem).start()
 
     for which, out in enumerate((x_out, w_out)):
-        for j in range(tiles):
-            pltpu.make_async_copy(theirs.at[which, 0], out.at[j], sems.at[which * tiles + j]).wait()
-
-
-def pack(meta, x, w, theirs, tiles, x_at, w_at, x_halos=(), w_halos=()):
+        for j in range((x_tiles, w_tiles)[which]):
+            pltpu.make_async_copy(theirs.at[which, 0], out.at[j], sems.at[which * x_tiles + j]).wait()
+
+
+def pack(meta, x, w, theirs, x_tiles, w_tiles, x_at, w_at, x_halos=(), w_halos=()):
     _, rows, half = x.shape
     halos = len(x_halos)
     loose = pl.BlockSpec(memory_space=pl.ANY)
     return pl.pallas_call(
-        functools.partial(pack_body, tiles, x_at, w_at, halos),
+        functools.partial(pack_body, x_tiles, w_tiles, x_at, w_at, halos),
         in_specs=[SMEM] + [loose] * (3 + 2 * halos),
         out_specs=[loose, loose],
-        scratch_shapes=[pltpu.SemaphoreType.DMA((2 * tiles,))],
-        out_shape=[jax.ShapeDtypeStruct((tiles, rows, half), BF)] * 2,
+        scratch_shapes=[pltpu.SemaphoreType.DMA((x_tiles + w_tiles,))],
+        out_shape=[jax.ShapeDtypeStruct((tiles, rows, half), BF) for tiles in (x_tiles, w_tiles)],
         compiler_params=params(),
-        cost_estimate=pl.CostEstimate(flops=0, bytes_accessed=tiles << 20, transcendentals=0),
+        cost_estimate=pl.CostEstimate(flops=0, bytes_accessed=x_tiles << 20, transcendentals=0),
         name="pack",
     )(meta, x, w, theirs, *x_halos, *w_halos)
 
@@ -360,7 +360,7 @@
             for t in range(blocks):
                 tile = pick(w, theirs.at[1], meta, t, group)
                 if t >= NEAR:
-                    tile = jnp.where(t < count, tile, wn[jnp.clip(t - count, 0, PIECE - 1), :, lanes])
+                    tile = jnp.where(t < count, tile, wn[jnp.clip(t - count, 0, ABOVE - 1), :, lanes])
                 near[t] = tile.T
             for a in range(split):
                 deep[a] = wn[a, :, lanes].T
@@ -424,7 +424,7 @@
             group = part * steps + step
             lanes, local = lanes_of(group), lanes_of(step)
             xs = [xn[p, :, lanes] for p in range(NEAR)]
-            ws = [wn[p, :, lanes] for p in range(NEAR)]
+            ws = [wn[p, :, lanes] for p in range(ABOVE)]
             for i in range(blocks):
                 farthest = min(blocks, i + NEAR)
                 start = (blocks - farthest) * rows
@@ -436,14 +436,14 @@
             for i in range(blocks - NEAR):
                 conv_out[i, :, lanes] = accum[i]
             for c in range(blocks):
-                tiles = min(NEAR, blocks - c)
+                tiles = min(ABOVE, blocks - c)
                 start = (c + 1) * rows
                 right = jnp.concatenate([kept(c + 1 + a < ahead[c], ws[a]) for a in range(tiles)], axis=0)
                 term = dot(bwd[step, :, start : start + tiles * rows], right)
                 accum[cap + blocks + count - 1 - c] = term
             for c in range(blocks, cap):
                 accum[cap + blocks + count - 1 - c] = jnp.zeros((rows, GROUP), F32)
-            for c in range(blocks - NEAR):
+            for c in range(blocks - ABOVE):
                 at = count - 1 - c
                 adj_out[c, :, lanes] = adj[at, :, local] + accum[cap + blocks + at]
             for slot in range(slots):
@@ -482,7 +482,7 @@
             jax.ShapeDtypeStruct((slots, rows, half), BF),
             jax.ShapeDtypeStruct((2, slots, rows, half), BF),
             jax.ShapeDtypeStruct((far, rows, half), F32),
-            jax.ShapeDtypeStruct((far, rows, half), F32),
+            jax.ShapeDtypeStruct((lags - 1 - ABOVE, rows, half), F32),
         ],
         compiler_params=params(),
         cost_estimate=pl.CostEstimate(flops=3_000_000_000, bytes_accessed=8 << 20, transcendentals=0),
@@ -493,9 +493,10 @@
 def far_body(lags, meta, reach, conv, adj, fwd_a, fwd_b, bwd_a, bwd_b, xf, wf, cot, cot_t,
              gate_in, input_in, send_in, gate_out, input_out, send_out):
     far, rows, _ = xf.shape
+    high = wf.shape[0]
     _, _, count, _ = chip_meta(meta)
     behind = [reach[READS + i] for i in range(far)]
-    ahead = [reach[NEAR + count - 1 - c] for c in range(far)]
+    ahead = [reach[NEAR + count - 1 - c] for c in range(high)]
     steps = fwd_a.shape[0]
     for part in range(2):
         fwd, bwd = ((fwd_a, bwd_a), (fwd_b, bwd_b))[part]
@@ -504,16 +505,16 @@
             group = part * steps + step
             lanes = lanes_of(group)
             xs = [xf[p, :, lanes] for p in range(far)]
-            ws = [wf[p, :, lanes] for p in range(far)]
+            ws = [wf[p, :, lanes] for p in range(high)]
             results = []
             for i in range(far):
                 right = [kept(lags - 1 + i - p < behind[i], xs[p]) for p in range(i, far)]
                 term = dot(fwd[step, :, : (far - i) * rows], jnp.concatenate(right, axis=0))
                 value = pick(cot, cot_t, meta, i, group).astype(F32) * (conv[i, :, lanes] + term)
                 results.append((i, gate_out, 0, value.astype(BF)))
-            for c in range(far):
-                right = [kept(c + NEAR + 1 + a < ahead[c], ws[a]) for a in range(far - c)]
-                term = dot(bwd[step, :, (c + NEAR + 1) * rows :], jnp.concatenate(right, axis=0))
+            for c in range(high):
+                right = [kept(c + ABOVE + 1 + a < ahead[c], ws[a]) for a in range(high - c)]
+                term = dot(bwd[step, :, (c + ABOVE + 1) * rows :], jnp.concatenate(right, axis=0))
                 results.append((count - 1 - c, input_out, 1, (adj[c, :, lanes] + term).astype(BF)))
             for index, out, which, value in results:
                 mine, slot = place(meta, index)
@@ -627,7 +628,7 @@
     send, meta = lead(me.reshape(1), tile_owner, gate_signal, cotangent, conv_input)
     theirs = swapped(send, "ctx", 1)
     x, w, cot, cot_send, reach = rest(meta, support.T, gate_signal, cotangent, conv_input)
-    xs, ws = pack(meta, x, w, theirs, PIECE, lambda j, n: n - PIECE + j, lambda j, n: j)
+    xs, ws = pack(meta, x, w, theirs, NEAR, ABOVE, lambda j, n: n - NEAR + j, lambda j, n: j)
     x0, w0 = up(xs), down(ws)
     cot_theirs = swapped(cot_send, "ctx", 1)
     half_groups = width // 2 // GROUP // 2
@@ -636,6 +637,12 @@
     x0, w0, one, two = tie((x0, w0, one, two))
     *one, first_sums = one
     *two, second_sums = two
+    xs, ws = pack(
+        meta, x, w, theirs, lags - 1 - NEAR, lags - 1 - ABOVE,
+        lambda j, n: n - lags + 1 + j, lambda j, n: ABOVE + j, (x0,), (w0,)
+    )
+    xs, ws, first_sums, second_sums = tie((xs, ws, first_sums, second_sums))
+    w2, x2 = down(ws), up(xs)
     sums = cross_squares(meta, reach, first_sums, second_sums, x, w, theirs, x0, w0, lags, norm)
 
     def stage(sums, axis, masks, filler):
@@ -646,16 +653,9 @@
             total_sum = total_sum + (moved[1] + moved[2])
         return tie((total_sum, out))
 
-    def relay(meta):
-        return pack(
-            meta, x, w, theirs, lags - 1 - NEAR, lambda j, n: n - lags + 1 + j, lambda j, n: NEAR + j, (x0,), (w0,)
-        )
-
     def close(meta):
         return near_pairs(meta, reach, one, two, x0, w0, cot, cot_theirs, lags)
 
-    sums, (xs, ws) = stage(sums, "ctx", (2, 4, 6), relay)
-    x2, w2 = up(xs), down(ws)
     sums, (gate, inp, back, conv, adj) = stage(sums, "ch", (1, 2, 3), close)
 
     def finish(meta):
@@ -665,8 +665,15 @@
 
     sums, (gate, inp, back) = stage(sums, "ctx", (8, 16, 24), finish)
     got = swapped(back, "ctx", 1)
-    moved = [swapped(sums, "ctx", mask) for mask in (32, 1, 33)]
-    gate, inp = place_mine(tie((sums, meta))[1], gate, inp)
+    sums, (gate, inp) = stage(sums, "ctx", (2, 4, 6), lambda meta: place_mine(meta, gate, inp))
+    count = lax.axis_size("ctx")
+    low = count // 8 - 1
+    mirrored = [(a, a ^ (count - 1 - low)) for a in range(count)]
+    moved = [
+        lax.ppermute(sums, "ctx", mirrored),
+        swapped(sums, "ctx", 1),
+        lax.ppermute(sums, "ctx", [(a, b ^ 1) for a, b in mirrored]),
+    ]
     return join(meta, got, gate, inp, sums, moved)
 
 

time: 107 us -> 102 us (0.953); the launches traced: 106 us -> 99.8 us
  starting transfers between devices: 41 us -> 36.4 us
  waiting for transfers between devices: 17.2 us -> 15.2 us
    ppermute x15 -> x13, starting transfers between devices: 35.5 us -> 23.1 us  [swapped(): return lax.ppermute(value, axis, [(a, a ^ mask) for a in range(count)])]
    ppermute x0 -> x2, starting transfers between devices: none -> 5 us  [the longest x1 4.77 us: per_device(): lax.ppermute(sums, 'ctx', [(a, b ^ 1) for a, b in mirrored])]
    ppermute x4, waiting for transfers between devices: 9.64 us -> 5.8 us  [shifted(): return lax.ppermute(value, axis, pairs)]
    ppermute x0 -> x2, waiting for transfers between devices: none -> 3.74 us  [the longest x1 2.03 us: per_device(): lax.ppermute(sums, 'ctx', [(a, b ^ 1) for a, b in mirrored])]
    ppermute x4, starting transfers between devices: 5.53 us -> 8.27 us  [shifted(): return lax.ppermute(value, axis, pairs)]
    ppermute x15 -> x13, waiting for transfers between devices: 7.53 us -> 5.66 us  [swapped(): return lax.ppermute(value, axis, [(a, a ^ mask) for a in range(count)])]
  transfers between devices with their start and end apart: 19 -> 19, of which waited for: 6 -> 6; matrix products, arithmetic and copies ran while one was open for 0% -> 0% of each run, Pallas kernels for 33% -> 35%
where the time goes in v5:
time: 102 us; the launch traced here: 99.8 us
  Pallas kernels  46.5 us (46%)
  starting transfers between devices  36.4 us (36%)
  waiting for transfers between devices  15.2 us (15%)
  between operations  1.02 us (1%)
    ppermute x13, starting transfers between devices, swapped(): return lax.ppermute(value, axis, [(a, a ^ mask) for a in range(count)])  23.1 us
    pallas_call x2, Pallas kernels, own_pairs(): pl.pallas_call(functools.partial(own_body, lags, base, steps, groups), in...  15 us
    ppermute x4, starting transfers between devices, shifted(): return lax.ppermute(value, axis, pairs)  8.27 us
    pallas_call x1, Pallas kernels, near_pairs(): pl.pallas_call(functools.partial(near_body, lags), in_specs=[SMEM, SMEM]...  6.93 us
    pallas_call x1, Pallas kernels, cross_squares(): pl.pallas_call(functools.partial(cross_body, lags, norm), in_specs=[SMEM,...  6.23 us
    ppermute x4, waiting for transfers between devices, shifted(): return lax.ppermute(value, axis, pairs)  5.8 us
    ppermute x13, waiting for transfers between devices, swapped(): return lax.ppermute(value, axis, [(a, a ^ mask) for a in range(count)])  5.66 us
    ppermute x1, starting transfers between devices, per_device(): lax.ppermute(sums, 'ctx', [(a, b ^ 1) for a, b in mirrored])  4.77 us
  transfers between devices with their start and end apart: 19, of which 6 were waited for; matrix products, arithmetic and copies ran while one was open for 0% of the time, Pallas kernels for 35%

profile of v5, /device:TPU:1, one launch (start us, length us, event | category | flops | bytes accessed | tf_op | source)
XLA Modules:
  0.0 99.8 jit_solution(7776090580326132175)
XLA Ops:
  0.6 4.1 %lead.1 = (bf16[2,4,128,1024]{3,2,1,0:T(8,128)(2,1)}, s32[8]{0:T(128)}) custom-call(s32[1]{0:T(128)} %bitcast.me, s32[192]{0:T(256)} %owner.1, bf16[4,128,2048]{2,1,0:T(8,128)(2,1)} %gate.3, bf16[4,128,2048]{2,1,0:T(8,128)(2,1)} %cot.3, bf16[4,128,2048]{2,1,0:T(8,128)(2,1)} %x.3), custom_call_target="tpu_custom_call" | custom-call | flops 1048576 | bytes 6291456 | tf_op jit(solution)/shard_map/lead/pallas_call | solution.py:105
  4.8 3.3 %collective-permute-start = (bf16[2,4,128,1024]{3,2,1,0:T(8,128)(2,1)}, bf16[2,4,128,1024]{3,2,1,0:T(8,128)(2,1)S(1)}, u32[]{:S(2)}, u32[]{:S(2)}) collective-permute-start(bf16[2,4,128,1024]{3,2,1,0:T(8,128)(2,1)} %get-tuple-element.70), channel_id=1, source_target_pairs={{0,4},{4,0},{8,12},{12,8},{16,20},{20,16},{24,28},{28,24},{32,36},... | collective-permute-start | bytes 6291464 | tf_op jit(solution)/shard_map/ppermute | solution.py:33
  8.1 0.7 copy-done
  8.8 3.9 %rest.1 = (bf16[4,128,1024]{2,1,0:T(8,128)(2,1)S(1)}, bf16[4,128,1024]{2,1,0:T(8,128)(2,1)S(1)}, bf16[4,128,1024]{2,1,0:T(8,128)(2,1)S(1)}, bf16[4,128,1024]{2,1,0:T(8,128)(2,1)}, s32[32]{0:T(128)S(1)}) custom-call(s32[8]{0:T(128)S(1)} %copy-done, s32[8,192]{1,0:T(8,128)S(1)} %bitcast.2, bf16[4,128,2048]{2,1,0:T(8,128)(2,1)} %gate.3, ...), custom_call_target="tpu_custom_call" | custom-call | flops 1048576 | bytes 6291456 | tf_op jit(solution)/shard_map/rest/pallas_call | solution.py:160
  12.8 0.9 pack.2
  13.6 1.5 %collective-permute-start.1 = (bf16[4,128,1024]{2,1,0:T(8,128)(2,1)S(1)}, bf16[4,128,1024]{2,1,0:T(8,128)(2,1)S(1)}, u32[]{:S(2)}, u32[]{:S(2)}) collective-permute-start(bf16[4,128,1024]{2,1,0:T(8,128)(2,1)S(1)} %get-tuple-element.71), channel_id=1, source_target_pairs={{0,8},{4,12},{8,16},{12,20},{16,24},{20,28},{24,32},{28,36},{32,40... | collective-permute-start | bytes 3145736 | tf_op jit(solution)/shard_map/ppermute | solution.py:28
  15.2 1.3 %collective-permute-start.2 = (bf16[3,128,1024]{2,1,0:T(8,128)(2,1)S(1)}, bf16[3,128,1024]{2,1,0:T(8,128)(2,1)S(1)}, u32[]{:S(2)}, u32[]{:S(2)}) collective-permute-start(bf16[3,128,1024]{2,1,0:T(8,128)(2,1)S(1)} %get-tuple-element.72), channel_id=1, source_target_pairs={{8,0},{12,4},{16,8},{20,12},{24,16},{28,20},{32,24},{36,28},{40,32... | collective-permute-start | bytes 2359304 | tf_op jit(solution)/shard_map/ppermute | solution.py:28
  16.5 0.4 collective-permute-start.6
  16.9 7.5 %own_pairs.3 = (f32[8,128,512]{2,1,0:T(8,128)S(1)}, f32[8,128,512]{2,1,0:T(8,128)S(1)}, bf16[4,128,1024]{2,1,0:T(8,128)(2,1)S(1)}, bf16[4,128,1024]{2,1,0:T(8,128)(2,1)S(1)}, f32[4,1024]{1,0:T(4,128)S(1)}) custom-call(s32[8]{0:T(128)S(1)} %copy-done, s32[32]{0:T(128)S(1)} %get-tuple-element.67.reach, f32[16,1024]{1,0:T(8,128)S(1)} %copy-done.2, ...), custom_call_target="tpu_custom_call" | custom-call | flops 4000000000 | bytes 4194304 | tf_op jit(solution)/shard_map/own_pairs/pallas_call | solution.py:312
  24.4 7.5 %own_pairs.2 = (f32[8,128,512]{2,1,0:T(8,128)S(1)}, f32[8,128,512]{2,1,0:T(8,128)S(1)}, bf16[4,128,1024]{2,1,0:T(8,128)(2,1)S(1)}, bf16[4,128,1024]{2,1,0:T(8,128)(2,1)S(1)}, f32[4,1024]{1,0:T(4,128)S(1)}) custom-call(s32[8]{0:T(128)S(1)} %copy-done, s32[32]{0:T(128)S(1)} %get-tuple-element.67.reach, f32[16,1024]{1,0:T(8,128)S(1)} %copy-done.2, ...), custom_call_target="tpu_custom_call" | custom-call | flops 4000000000 | bytes 4194304 | tf_op jit(solution)/shard_map/own_pairs/pallas_call | solution.py:312
  31.9 4.0 %collective-permute-done.2.rest_1_.wn = bf16[3,128,1024]{2,1,0:T(8,128)(2,1)S(1)} collective-permute-done((bf16[3,128,1024]{2,1,0:T(8,128)(2,1)S(1)}, bf16[3,128,1024]{2,1,0:T(8,128)(2,1)S(1)}, u32[]{:S(2)}, u32[]{:S(2)}) %collective-permute-start.2) | collective-permute-done | bytes 786464 | tf_op jit(solution)/shard_map/ppermute | solution.py:28
  35.9 1.8 %collective-permute-done.1.rest_0_.xn = bf16[4,128,1024]{2,1,0:T(8,128)(2,1)S(1)} collective-permute-done((bf16[4,128,1024]{2,1,0:T(8,128)(2,1)S(1)}, bf16[4,128,1024]{2,1,0:T(8,128)(2,1)S(1)}, u32[]{:S(2)}, u32[]{:S(2)}) %collective-permute-start.1) | collective-permute-done | bytes 1048608 | tf_op jit(solution)/shard_map/ppermute | solution.py:28
  37.7 0.9 pack.3
  38.5 4.2 %collective-permute-start.10 = (bf16[3,128,1024]{2,1,0:T(8,128)(2,1)S(1)}, bf16[3,128,1024]{2,1,0:T(8,128)(2,1)S(1)}, u32[]{:S(2)}, u32[]{:S(2)}) collective-permute-start(bf16[3,128,1024]{2,1,0:T(8,128)(2,1)S(1)} %get-tuple-element.111), channel_id=1, source_target_pairs={{0,8},{4,12},{8,16},{12,20},{16,24},{20,28},{24,32},{28,36},{32,40... | collective-permute-start | bytes 2359304 | tf_op jit(solution)/shard_map/ppermute | solution.py:28
  42.7 1.3 %collective-permute-start.11 = (bf16[4,128,1024]{2,1,0:T(8,128)(2,1)S(1)}, bf16[4,128,1024]{2,1,0:T(8,128)(2,1)S(1)}, u32[]{:S(2)}, u32[]{:S(2)}) collective-permute-start(bf16[4,128,1024]{2,1,0:T(8,128)(2,1)S(1)} %get-tuple-element.112), channel_id=1, source_target_pairs={{8,0},{12,4},{16,8},{20,12},{24,16},{28,20},{32,24},{36,28},{40,32... | collective-permute-start | bytes 3145736 | tf_op jit(solution)/shard_map/ppermute | solution.py:28
  44.0 6.2 %cross_squares.1 = f32[8,1024]{1,0:T(8,128)S(1)} custom-call(s32[8]{0:T(128)S(1)} %copy-done, s32[32]{0:T(128)S(1)} %get-tuple-element.67.reach, f32[4,1024]{1,0:T(4,128)S(1)} %get-tuple-element.89.prior, f32[4,1024]{1,0:T(4,128)S(1)} %get-tuple-element.90.more, bf16[4,128,1024]{2,1,0:T(8,128)(2,1)S(1)} %get-tuple-element.68.x, ...), custom_call_target="tpu_custom_call" | custom-call | flops 3000000000 | bytes 6291456 | tf_op jit(solution)/shard_map/cross_squares/pallas_call | solution.py:394
  50.2 2.5 %collective-permute-start.5 = (f32[8,1024]{1,0:T(8,128)S(1)}, f32[8,1024]{1,0:T(8,128)S(1)}, u32[]{:S(2)}, u32[]{:S(2)}) collective-permute-start(f32[8,1024]{1,0:T(8,128)S(1)} %cross_squares.1), channel_id=1, source_target_pairs={{0,3},{1,2},{2,1},{3,0},{4,7},{5,6},{6,5},{7,4},{8,11},{9,10},{10,... | collective-permute-start | bytes 98312 | tf_op jit(solution)/shard_map/ppermute | solution.py:33
  52.8 0.5 collective-permute-start.4
  53.3 0.3 collective-permute-start.3
  53.6 6.9 %near_pairs.1 = (bf16[4,128,1024]{2,1,0:T(8,128)(2,1)S(1)}, bf16[4,128,1024]{2,1,0:T(8,128)(2,1)S(1)}, bf16[2,4,128,1024]{3,2,1,0:T(8,128)(2,1)S(1)}, f32[3,128,1024]{2,1,0:T(8,128)S(1)}, f32[4,128,1024]{2,1,0:T(8,128)S(1)}) custom-call(s32[8]{0:T(128)S(1)} %copy-done, s32[32]{0:T(128)S(1)} %get-tuple-element.67.reach, ...), custom_call_target="tpu_custom_call" | custom-call | flops 3000000000 | bytes 8388608 | tf_op jit(solution)/shard_map/near_pairs/pallas_call | solution.py:473
  60.6 9.4 %collective-permute-start.9 = (f32[8,1024]{1,0:T(8,128)S(1)}, f32[8,1024]{1,0:T(8,128)S(1)}, u32[]{:S(2)}, u32[]{:S(2)}) collective-permute-start(f32[8,1024]{1,0:T(8,128)S(1)} %add_add_fusion.2), channel_id=1, source_target_pairs={{0,96},{4,100},{8,104},{12,108},{16,112},{20,116},{24,120},{28,124... | collective-permute-start | bytes 98312 | tf_op jit(solution)/shard_map/ppermute | solution.py:33
  69.9 0.4 collective-permute-start.7
  70.3 5.5 %collective-permute-done.9 = f32[8,1024]{1,0:T(8,128)S(1)} collective-permute-done((f32[8,1024]{1,0:T(8,128)S(1)}, f32[8,1024]{1,0:T(8,128)S(1)}, u32[]{:S(2)}, u32[]{:S(2)}) %collective-permute-start.9) | collective-permute-done | bytes 32800 | tf_op jit(solution)/shard_map/ppermute | solution.py:33
  75.8 4.1 %far_pairs.1 = (bf16[4,128,1024]{2,1,0:T(8,128)(2,1)S(1)}, bf16[4,128,1024]{2,1,0:T(8,128)(2,1)S(1)}, bf16[2,4,128,1024]{3,2,1,0:T(8,128)(2,1)S(1)}) custom-call(s32[8]{0:T(128)S(1)} %copy-done, s32[32]{0:T(128)S(1)} %get-tuple-element.67.reach, ...), custom_call_target="tpu_custom_call", output_to_operand_aliasing={{0}: (12, {}), {1}: (13, {}), {2}: (14, {})} | custom-call | flops 800000000 | bytes 4194304 | tf_op jit(solution)/shard_map/far_pairs/pallas_call | solution.py:537
  79.9 3.0 %collective-permute-start.12 = (bf16[2,4,128,1024]{3,2,1,0:T(8,128)(2,1)S(1)}, bf16[2,4,128,1024]{3,2,1,0:T(8,128)(2,1)S(1)}, u32[]{:S(2)}, u32[]{:S(2)}) collective-permute-start(bf16[2,4,128,1024]{3,2,1,0:T(8,128)(2,1)S(1)} %get-tuple-element.119), channel_id=1, source_target_pairs={{0,4},{4,0},{8,12},{12,8},{16,20},{20,16},{24,28},{28,24},{32,36},... | collective-permute-start | bytes 6291464 | tf_op jit(solution)/shard_map/ppermute | solution.py:33
  82.9 1.1 %collective-permute-start.15 = (f32[8,1024]{1,0:T(8,128)S(1)}, f32[8,1024]{1,0:T(8,128)S(1)}, u32[]{:S(2)}, u32[]{:S(2)}) collective-permute-start(f32[8,1024]{1,0:T(8,128)S(1)} %add_add_fusion.1), channel_id=1, source_target_pairs={{0,24},{4,28},{8,16},{12,20},{16,8},{20,12},{24,0},{28,4},{32,56},... | collective-permute-start | bytes 98312 | tf_op jit(solution)/shard_map/ppermute | solution.py:33
  84.0 2.2 %collective-permute-start.13 = (f32[8,1024]{1,0:T(8,128)S(1)}, f32[8,1024]{1,0:T(8,128)S(1)}, u32[]{:S(2)}, u32[]{:S(2)}) collective-permute-start(f32[8,1024]{1,0:T(8,128)S(1)} %add_add_fusion.1), channel_id=1, source_target_pairs={{0,8},{4,12},{8,0},{12,4},{16,24},{20,28},{24,16},{28,20},{32,40},... | collective-permute-start | bytes 98312 | tf_op jit(solution)/shard_map/ppermute | solution.py:33
  86.2 1.9 %place_mine.1 = (bf16[4,128,2048]{2,1,0:T(8,128)(2,1)}, bf16[4,128,2048]{2,1,0:T(8,128)(2,1)}) custom-call(s32[8]{0:T(128)S(1)} %copy-done, bf16[4,128,1024]{2,1,0:T(8,128)(2,1)S(1)} %get-tuple-element.122.gate, bf16[4,128,1024]{2,1,0:T(8,128)(2,1)S(1)} %get-tuple-element.123.inp), custom_call_target="tpu_custom_call" | custom-call | tf_op jit(solution)/shard_map/place_mine/pallas_call | solution.py:574
  88.3 4.8 %collective-permute-start.18 = (f32[8,1024]{1,0:T(8,128)S(1)}, f32[8,1024]{1,0:T(8,128)S(1)}, u32[]{:S(2)}, u32[]{:S(2)}) collective-permute-start(f32[8,1024]{1,0:T(8,128)S(1)} %add_add_fusion.sums), channel_id=1, source_target_pairs={{0,228},{4,224},{8,236},{12,232},{16,244},{20,240},{24,252},{28,24... | collective-permute-start | bytes 98312 | tf_op jit(solution)/shard_map/ppermute | solution.py:675
  93.3 2.0 %collective-permute-done.18.other_pair = f32[8,1024]{1,0:T(8,128)S(1)} collective-permute-done((f32[8,1024]{1,0:T(8,128)S(1)}, f32[8,1024]{1,0:T(8,128)S(1)}, u32[]{:S(2)}, u32[]{:S(2)}) %collective-permute-start.18) | collective-permute-done | bytes 32800 | tf_op jit(solution)/shard_map/ppermute | solution.py:675
  95.3 1.7 %collective-permute-done.16.pair = f32[8,1024]{1,0:T(8,128)S(1)} collective-permute-done((f32[8,1024]{1,0:T(8,128)S(1)}, f32[8,1024]{1,0:T(8,128)S(1)}, u32[]{:S(2)}, u32[]{:S(2)}) %collective-permute-start.16) | collective-permute-done | bytes 32800 | tf_op jit(solution)/shard_map/ppermute | solution.py:673
  97.0 2.5 %join.1 = (bf16[4,128,2048]{2,1,0:T(8,128)(2,1)}, bf16[4,128,2048]{2,1,0:T(8,128)(2,1)}, f32[16,1024]{1,0:T(8,128)}) custom-call(s32[8]{0:T(128)S(1)} %copy-done, bf16[2,4,128,1024]{3,2,1,0:T(8,128)(2,1)S(1)} %collective-permute-done.12.got, bf16[4,128,2048]{2,1,0:T(8,128)(2,1)} %get-tuple-element.126.gate_in, ...), custom_call_target="tpu_custom_call", output_to_operand_aliasing={{0}: (2, {}), {1}: (3, {})} | custom-call | tf_op jit(solution)/shard_map/join/pallas_call | solution.py:596
  (28 shorter events, 0.5 us)
Async XLA Ops:
  0.6 7.5 %copy-start.1 = (s32[192,8]{0,1:T(8,128)S(1)}, s32[192,8]{0,1:T(8,128)}, u32[]{:S(2)}) copy-start(s32[192,8]{0,1:T(8,128)} %param.11) | copy-start | bytes 18436
  4.8 7.9 %collective-permute-start = (bf16[2,4,128,1024]{3,2,1,0:T(8,128)(2,1)}, bf16[2,4,128,1024]{3,2,1,0:T(8,128)(2,1)S(1)}, u32[]{:S(2)}, u32[]{:S(2)}) collective-permute-start(bf16[2,4,128,1024]{3,2,1,0:T(8,128)(2,1)} %get-tuple-element.70), channel_id=1, source_target_pairs={{0,4},{4,0},{8,12},{12,8},{16,20},{20,16},{24,28},{28,24},{32,36},... | collective-permute-start | bytes 6291464 | tf_op jit(solution)/shard_map/ppermute | solution.py:33
  8.1 0.7 copy-start
  12.7 3.7 %copy-start.3 = (bf16[4,128,1024]{2,1,0:T(8,128)(2,1)S(1)}, bf16[4,128,1024]{2,1,0:T(8,128)(2,1)}, u32[]{:S(2)}) copy-start(bf16[4,128,1024]{2,1,0:T(8,128)(2,1)} %get-tuple-element.101) | copy-start | bytes 3145732
  12.7 4.1 %copy-start.2 = (f32[16,1024]{1,0:T(8,128)S(1)}, f32[16,1024]{1,0:T(8,128)}, u32[]{:S(2)}) copy-start(f32[16,1024]{1,0:T(8,128)} %filt.3) | copy-start | bytes 196612
  13.6 24.0 %collective-permute-start.1 = (bf16[4,128,1024]{2,1,0:T(8,128)(2,1)S(1)}, bf16[4,128,1024]{2,1,0:T(8,128)(2,1)S(1)}, u32[]{:S(2)}, u32[]{:S(2)}) collective-permute-start(bf16[4,128,1024]{2,1,0:T(8,128)(2,1)S(1)} %get-tuple-element.71), channel_id=1, source_target_pairs={{0,8},{4,12},{8,16},{12,20},{16,24},{20,28},{24,32},{28,36},{32,40... | collective-permute-start | bytes 3145736 | tf_op jit(solution)/shard_map/ppermute | solution.py:28
  15.2 20.7 %collective-permute-start.2 = (bf16[3,128,1024]{2,1,0:T(8,128)(2,1)S(1)}, bf16[3,128,1024]{2,1,0:T(8,128)(2,1)S(1)}, u32[]{:S(2)}, u32[]{:S(2)}) collective-permute-start(bf16[3,128,1024]{2,1,0:T(8,128)(2,1)S(1)} %get-tuple-element.72), channel_id=1, source_target_pairs={{8,0},{12,4},{16,8},{20,12},{24,16},{28,20},{32,24},{36,28},{40,32... | collective-permute-start | bytes 2359304 | tf_op jit(solution)/shard_map/ppermute | solution.py:28
  16.5 36.8 %collective-permute-start.6 = (bf16[4,128,1024]{2,1,0:T(8,128)(2,1)S(1)}, bf16[4,128,1024]{2,1,0:T(8,128)(2,1)S(1)}, u32[]{:S(2)}, u32[]{:S(2)}) collective-permute-start(bf16[4,128,1024]{2,1,0:T(8,128)(2,1)S(1)} %copy-done.3), channel_id=1, source_target_pairs={{0,4},{4,0},{8,12},{12,8},{16,20},{20,16},{24,28},{28,24},{32,36},... | collective-permute-start | bytes 3145736 | tf_op jit(solution)/shard_map/ppermute | solution.py:33
  38.5 37.3 %collective-permute-start.10 = (bf16[3,128,1024]{2,1,0:T(8,128)(2,1)S(1)}, bf16[3,128,1024]{2,1,0:T(8,128)(2,1)S(1)}, u32[]{:S(2)}, u32[]{:S(2)}) collective-permute-start(bf16[3,128,1024]{2,1,0:T(8,128)(2,1)S(1)} %get-tuple-element.111), channel_id=1, source_target_pairs={{0,8},{4,12},{8,16},{12,20},{16,24},{20,28},{24,32},{28,36},{32,40... | collective-permute-start | bytes 2359304 | tf_op jit(solution)/shard_map/ppermute | solution.py:28
  42.7 33.1 %collective-permute-start.11 = (bf16[4,128,1024]{2,1,0:T(8,128)(2,1)S(1)}, bf16[4,128,1024]{2,1,0:T(8,128)(2,1)S(1)}, u32[]{:S(2)}, u32[]{:S(2)}) collective-permute-start(bf16[4,128,1024]{2,1,0:T(8,128)(2,1)S(1)} %get-tuple-element.112), channel_id=1, source_target_pairs={{8,0},{12,4},{16,8},{20,12},{24,16},{28,20},{32,24},{36,28},{40,32... | collective-permute-start | bytes 3145736 | tf_op jit(solution)/shard_map/ppermute | solution.py:28
  50.2 10.3 %collective-permute-start.5 = (f32[8,1024]{1,0:T(8,128)S(1)}, f32[8,1024]{1,0:T(8,128)S(1)}, u32[]{:S(2)}, u32[]{:S(2)}) collective-permute-start(f32[8,1024]{1,0:T(8,128)S(1)} %cross_squares.1), channel_id=1, source_target_pairs={{0,3},{1,2},{2,1},{3,0},{4,7},{5,6},{6,5},{7,4},{8,11},{9,10},{10,... | collective-permute-start | bytes 98312 | tf_op jit(solution)/shard_map/ppermute | solution.py:33
  52.8 7.7 %collective-permute-start.4 = (f32[8,1024]{1,0:T(8,128)S(1)}, f32[8,1024]{1,0:T(8,128)S(1)}, u32[]{:S(2)}, u32[]{:S(2)}) collective-permute-start(f32[8,1024]{1,0:T(8,128)S(1)} %cross_squares.1), channel_id=1, source_target_pairs={{0,2},{1,3},{2,0},{3,1},{4,6},{5,7},{6,4},{7,5},{8,10},{9,11},{10,... | collective-permute-start | bytes 98312 | tf_op jit(solution)/shard_map/ppermute | solution.py:33
  53.3 7.2 %collective-permute-start.3 = (f32[8,1024]{1,0:T(8,128)S(1)}, f32[8,1024]{1,0:T(8,128)S(1)}, u32[]{:S(2)}, u32[]{:S(2)}) collective-permute-start(f32[8,1024]{1,0:T(8,128)S(1)} %cross_squares.1), channel_id=1, source_target_pairs={{0,1},{1,0},{2,3},{3,2},{4,5},{5,4},{6,7},{7,6},{8,9},{9,8},{10,11... | collective-permute-start | bytes 98312 | tf_op jit(solution)/shard_map/ppermute | solution.py:33
  60.6 15.2 %collective-permute-start.9 = (f32[8,1024]{1,0:T(8,128)S(1)}, f32[8,1024]{1,0:T(8,128)S(1)}, u32[]{:S(2)}, u32[]{:S(2)}) collective-permute-start(f32[8,1024]{1,0:T(8,128)S(1)} %add_add_fusion.2), channel_id=1, source_target_pairs={{0,96},{4,100},{8,104},{12,108},{16,112},{20,116},{24,120},{28,124... | collective-permute-start | bytes 98312 | tf_op jit(solution)/shard_map/ppermute | solution.py:33
  69.9 5.9 %collective-permute-start.8 = (f32[8,1024]{1,0:T(8,128)S(1)}, f32[8,1024]{1,0:T(8,128)S(1)}, u32[]{:S(2)}, u32[]{:S(2)}) collective-permute-start(f32[8,1024]{1,0:T(8,128)S(1)} %add_add_fusion.2), channel_id=1, source_target_pairs={{0,64},{4,68},{8,72},{12,76},{16,80},{20,84},{24,88},{28,92},{32,9... | collective-permute-start | bytes 98312 | tf_op jit(solution)/shard_map/ppermute | solution.py:33
  69.9 5.9 %collective-permute-start.7 = (f32[8,1024]{1,0:T(8,128)S(1)}, f32[8,1024]{1,0:T(8,128)S(1)}, u32[]{:S(2)}, u32[]{:S(2)}) collective-permute-start(f32[8,1024]{1,0:T(8,128)S(1)} %add_add_fusion.2), channel_id=1, source_target_pairs={{0,32},{4,36},{8,40},{12,44},{16,48},{20,52},{24,56},{28,60},{32,0... | collective-permute-start | bytes 98312 | tf_op jit(solution)/shard_map/ppermute | solution.py:33
  79.9 17.1 %collective-permute-start.12 = (bf16[2,4,128,1024]{3,2,1,0:T(8,128)(2,1)S(1)}, bf16[2,4,128,1024]{3,2,1,0:T(8,128)(2,1)S(1)}, u32[]{:S(2)}, u32[]{:S(2)}) collective-permute-start(bf16[2,4,128,1024]{3,2,1,0:T(8,128)(2,1)S(1)} %get-tuple-element.119), channel_id=1, source_target_pairs={{0,4},{4,0},{8,12},{12,8},{16,20},{20,16},{24,28},{28,24},{32,36},... | collective-permute-start | bytes 6291464 | tf_op jit(solution)/shard_map/ppermute | solution.py:33
  82.9 5.2 %collective-permute-start.15 = (f32[8,1024]{1,0:T(8,128)S(1)}, f32[8,1024]{1,0:T(8,128)S(1)}, u32[]{:S(2)}, u32[]{:S(2)}) collective-permute-start(f32[8,1024]{1,0:T(8,128)S(1)} %add_add_fusion.1), channel_id=1, source_target_pairs={{0,24},{4,28},{8,16},{12,20},{16,8},{20,12},{24,0},{28,4},{32,56},... | collective-permute-start | bytes 98312 | tf_op jit(solution)/shard_map/ppermute | solution.py:33
  84.0 4.3 %collective-permute-start.14 = (f32[8,1024]{1,0:T(8,128)S(1)}, f32[8,1024]{1,0:T(8,128)S(1)}, u32[]{:S(2)}, u32[]{:S(2)}) collective-permute-start(f32[8,1024]{1,0:T(8,128)S(1)} %add_add_fusion.1), channel_id=1, source_target_pairs={{0,16},{4,20},{8,24},{12,28},{16,0},{20,4},{24,8},{28,12},{32,48},... | collective-permute-start | bytes 98312 | tf_op jit(solution)/shard_map/ppermute | solution.py:33
  84.0 4.3 %collective-permute-start.13 = (f32[8,1024]{1,0:T(8,128)S(1)}, f32[8,1024]{1,0:T(8,128)S(1)}, u32[]{:S(2)}, u32[]{:S(2)}) collective-permute-start(f32[8,1024]{1,0:T(8,128)S(1)} %add_add_fusion.1), channel_id=1, source_target_pairs={{0,8},{4,12},{8,0},{12,4},{16,24},{20,28},{24,16},{28,20},{32,40},... | collective-permute-start | bytes 98312 | tf_op jit(solution)/shard_map/ppermute | solution.py:33
  88.3 7.0 %collective-permute-start.18 = (f32[8,1024]{1,0:T(8,128)S(1)}, f32[8,1024]{1,0:T(8,128)S(1)}, u32[]{:S(2)}, u32[]{:S(2)}) collective-permute-start(f32[8,1024]{1,0:T(8,128)S(1)} %add_add_fusion.sums), channel_id=1, source_target_pairs={{0,228},{4,224},{8,236},{12,232},{16,244},{20,240},{24,252},{28,24... | collective-permute-start | bytes 98312 | tf_op jit(solution)/shard_map/ppermute | solution.py:675
  93.1 2.3 %collective-permute-start.17 = (f32[8,1024]{1,0:T(8,128)S(1)}, f32[8,1024]{1,0:T(8,128)S(1)}, u32[]{:S(2)}, u32[]{:S(2)}) collective-permute-start(f32[8,1024]{1,0:T(8,128)S(1)} %add_add_fusion.sums), channel_id=1, source_target_pairs={{0,4},{4,0},{8,12},{12,8},{16,20},{20,16},{24,28},{28,24},{32,36},... | collective-permute-start | bytes 98312 | tf_op jit(solution)/shard_map/ppermute | solution.py:33
  93.1 4.0 %collective-permute-start.16 = (f32[8,1024]{1,0:T(8,128)S(1)}, f32[8,1024]{1,0:T(8,128)S(1)}, u32[]{:S(2)}, u32[]{:S(2)}) collective-permute-start(f32[8,1024]{1,0:T(8,128)S(1)} %add_add_fusion.sums), channel_id=1, source_target_pairs={{0,224},{4,228},{8,232},{12,236},{16,240},{20,244},{24,248},{28,25... | collective-permute-start | bytes 98312 | tf_op jit(solution)/shard_map/ppermute | solution.py:673

commit v6 on v5

--- a/solution.py
+++ b/solution.py
@@ -383,7 +383,7 @@
             sums_out[pl.ds(group, 1), :] = (source[pl.ds(step, 1), :] + total_sum) * norm
             return carry
 
-        lax.fori_loop(0, steps, one, 0, unroll=2)
+        lax.fori_loop(0, steps, one, 0, unroll=4)
 
 
 def cross_squares(meta, reach, prior, more, x, w, theirs, x_halo, w_halo, lags, norm):

time: 102 us -> 102 us (level)
  the two profiles are of different devices: /device:TPU:1 before, /device:TPU:34 now
where the time goes in v6:
time: 102 us; the launch traced here: 101 us
  Pallas kernels  45.4 us (45%)
  starting transfers between devices  34.8 us (34%)
  waiting for transfers between devices  19.5 us (19%)
  between operations  1.06 us (1%)
    ppermute x4, starting transfers between devices, shifted(): return lax.ppermute(value, axis, pairs)  15.9 us
    ppermute x13, starting transfers between devices, swapped(): return lax.ppermute(value, axis, [(a, a ^ mask) for a in range(count)])  15.1 us
    pallas_call x2, Pallas kernels, own_pairs(): pl.pallas_call(functools.partial(own_body, lags, base, steps, groups), in...  15 us
    pallas_call x1, Pallas kernels, near_pairs(): pl.pallas_call(functools.partial(near_body, lags), in_specs=[SMEM, SMEM]...  6.94 us
    ppermute x13, waiting for transfers between devices, swapped(): return lax.ppermute(value, axis, [(a, a ^ mask) for a in range(count)])  6.51 us
    ppermute x4, waiting for transfers between devices, shifted(): return lax.ppermute(value, axis, pairs)  6.46 us
    ppermute x1, waiting for transfers between devices, per_device(): lax.ppermute(sums, 'ctx', mirrored)  5.15 us
    pallas_call x1, Pallas kernels, cross_squares(): pl.pallas_call(functools.partial(cross_body, lags, norm), in_specs=[SMEM,...  5.12 us
  transfers between devices with their start and end apart: 19, of which 7 were waited for; matrix products, arithmetic and copies ran while one was open for 0% of the time, Pallas kernels for 33%

profile of v6, /device:TPU:34, one launch (start us, length us, event | category | flops | bytes accessed | tf_op | source)
XLA Modules:
  0.0 101.4 jit_solution(13536927671350052460)
XLA Ops:
  0.6 4.1 %lead.1 = (bf16[2,4,128,1024]{3,2,1,0:T(8,128)(2,1)}, s32[8]{0:T(128)}) custom-call(s32[1]{0:T(128)} %bitcast.me, s32[192]{0:T(256)} %owner.1, bf16[4,128,2048]{2,1,0:T(8,128)(2,1)} %gate.3, bf16[4,128,2048]{2,1,0:T(8,128)(2,1)} %cot.3, bf16[4,128,2048]{2,1,0:T(8,128)(2,1)} %x.3), custom_call_target="tpu_custom_call" | custom-call | flops 1048576 | bytes 6291456 | tf_op jit(solution)/shard_map/lead/pallas_call | solution.py:105
  4.9 0.6 copy-done
  5.6 3.9 %rest.1 = (bf16[4,128,1024]{2,1,0:T(8,128)(2,1)S(1)}, bf16[4,128,1024]{2,1,0:T(8,128)(2,1)S(1)}, bf16[4,128,1024]{2,1,0:T(8,128)(2,1)S(1)}, bf16[4,128,1024]{2,1,0:T(8,128)(2,1)}, s32[32]{0:T(128)S(1)}) custom-call(s32[8]{0:T(128)S(1)} %copy-done, s32[8,192]{1,0:T(8,128)S(1)} %bitcast.2, bf16[4,128,2048]{2,1,0:T(8,128)(2,1)} %gate.3, ...), custom_call_target="tpu_custom_call" | custom-call | flops 1048576 | bytes 6291456 | tf_op jit(solution)/shard_map/rest/pallas_call | solution.py:160
  9.5 0.9 pack.2
  10.4 3.5 %collective-permute-start.1 = (bf16[4,128,1024]{2,1,0:T(8,128)(2,1)S(1)}, bf16[4,128,1024]{2,1,0:T(8,128)(2,1)S(1)}, u32[]{:S(2)}, u32[]{:S(2)}) collective-permute-start(bf16[4,128,1024]{2,1,0:T(8,128)(2,1)S(1)} %get-tuple-element.71), channel_id=1, source_target_pairs={{0,8},{4,12},{8,16},{12,20},{16,24},{20,28},{24,32},{28,36},{32,40... | collective-permute-start | bytes 3145736 | tf_op jit(solution)/shard_map/ppermute | solution.py:28
  13.9 4.5 %collective-permute-start.2 = (bf16[3,128,1024]{2,1,0:T(8,128)(2,1)S(1)}, bf16[3,128,1024]{2,1,0:T(8,128)(2,1)S(1)}, u32[]{:S(2)}, u32[]{:S(2)}) collective-permute-start(bf16[3,128,1024]{2,1,0:T(8,128)(2,1)S(1)} %get-tuple-element.72), channel_id=1, source_target_pairs={{8,0},{12,4},{16,8},{20,12},{24,16},{28,20},{32,24},{36,28},{40,32... | collective-permute-start | bytes 2359304 | tf_op jit(solution)/shard_map/ppermute | solution.py:28
  18.5 7.5 %own_pairs.3 = (f32[8,128,512]{2,1,0:T(8,128)S(1)}, f32[8,128,512]{2,1,0:T(8,128)S(1)}, bf16[4,128,1024]{2,1,0:T(8,128)(2,1)S(1)}, bf16[4,128,1024]{2,1,0:T(8,128)(2,1)S(1)}, f32[4,1024]{1,0:T(4,128)S(1)}) custom-call(s32[8]{0:T(128)S(1)} %copy-done, s32[32]{0:T(128)S(1)} %get-tuple-element.67.reach, f32[16,1024]{1,0:T(8,128)S(1)} %copy-done.2, ...), custom_call_target="tpu_custom_call" | custom-call | flops 4000000000 | bytes 4194304 | tf_op jit(solution)/shard_map/own_pairs/pallas_call | solution.py:312
  26.0 7.5 %own_pairs.2 = (f32[8,128,512]{2,1,0:T(8,128)S(1)}, f32[8,128,512]{2,1,0:T(8,128)S(1)}, bf16[4,128,1024]{2,1,0:T(8,128)(2,1)S(1)}, bf16[4,128,1024]{2,1,0:T(8,128)(2,1)S(1)}, f32[4,1024]{1,0:T(4,128)S(1)}) custom-call(s32[8]{0:T(128)S(1)} %copy-done, s32[32]{0:T(128)S(1)} %get-tuple-element.67.reach, f32[16,1024]{1,0:T(8,128)S(1)} %copy-done.2, ...), custom_call_target="tpu_custom_call" | custom-call | flops 4000000000 | bytes 4194304 | tf_op jit(solution)/shard_map/own_pairs/pallas_call | solution.py:312
  33.5 2.0 %collective-permute-done.2.rest_1_.wn = bf16[3,128,1024]{2,1,0:T(8,128)(2,1)S(1)} collective-permute-done((bf16[3,128,1024]{2,1,0:T(8,128)(2,1)S(1)}, bf16[3,128,1024]{2,1,0:T(8,128)(2,1)S(1)}, u32[]{:S(2)}, u32[]{:S(2)}) %collective-permute-start.2) | collective-permute-done | bytes 786464 | tf_op jit(solution)/shard_map/ppermute | solution.py:28
  35.5 4.4 %collective-permute-done.1.rest_0_.xn = bf16[4,128,1024]{2,1,0:T(8,128)(2,1)S(1)} collective-permute-done((bf16[4,128,1024]{2,1,0:T(8,128)(2,1)S(1)}, bf16[4,128,1024]{2,1,0:T(8,128)(2,1)S(1)}, u32[]{:S(2)}, u32[]{:S(2)}) %collective-permute-start.1) | collective-permute-done | bytes 1048608 | tf_op jit(solution)/shard_map/ppermute | solution.py:28
  40.0 0.9 pack.3
  40.9 1.9 %collective-permute-start.10 = (bf16[3,128,1024]{2,1,0:T(8,128)(2,1)S(1)}, bf16[3,128,1024]{2,1,0:T(8,128)(2,1)S(1)}, u32[]{:S(2)}, u32[]{:S(2)}) collective-permute-start(bf16[3,128,1024]{2,1,0:T(8,128)(2,1)S(1)} %get-tuple-element.111), channel_id=1, source_target_pairs={{0,8},{4,12},{8,16},{12,20},{16,24},{20,28},{24,32},{28,36},{32,40... | collective-permute-start | bytes 2359304 | tf_op jit(solution)/shard_map/ppermute | solution.py:28
  42.8 6.0 %collective-permute-start.11 = (bf16[4,128,1024]{2,1,0:T(8,128)(2,1)S(1)}, bf16[4,128,1024]{2,1,0:T(8,128)(2,1)S(1)}, u32[]{:S(2)}, u32[]{:S(2)}) collective-permute-start(bf16[4,128,1024]{2,1,0:T(8,128)(2,1)S(1)} %get-tuple-element.112), channel_id=1, source_target_pairs={{8,0},{12,4},{16,8},{20,12},{24,16},{28,20},{32,24},{36,28},{40,32... | collective-permute-start | bytes 3145736 | tf_op jit(solution)/shard_map/ppermute | solution.py:28
  48.8 5.1 %cross_squares.1 = f32[8,1024]{1,0:T(8,128)S(1)} custom-call(s32[8]{0:T(128)S(1)} %copy-done, s32[32]{0:T(128)S(1)} %get-tuple-element.67.reach, f32[4,1024]{1,0:T(4,128)S(1)} %get-tuple-element.89.prior, f32[4,1024]{1,0:T(4,128)S(1)} %get-tuple-element.90.more, bf16[4,128,1024]{2,1,0:T(8,128)(2,1)S(1)} %get-tuple-element.68.x, ...), custom_call_target="tpu_custom_call" | custom-call | flops 3000000000 | bytes 6291456 | tf_op jit(solution)/shard_map/cross_squares/pallas_call | solution.py:394
  53.9 1.7 %collective-permute-start.5 = (f32[8,1024]{1,0:T(8,128)S(1)}, f32[8,1024]{1,0:T(8,128)S(1)}, u32[]{:S(2)}, u32[]{:S(2)}) collective-permute-start(f32[8,1024]{1,0:T(8,128)S(1)} %cross_squares.1), channel_id=1, source_target_pairs={{0,3},{1,2},{2,1},{3,0},{4,7},{5,6},{6,5},{7,4},{8,11},{9,10},{10,... | collective-permute-start | bytes 98312 | tf_op jit(solution)/shard_map/ppermute | solution.py:33
  55.7 1.1 %collective-permute-start.4 = (f32[8,1024]{1,0:T(8,128)S(1)}, f32[8,1024]{1,0:T(8,128)S(1)}, u32[]{:S(2)}, u32[]{:S(2)}) collective-permute-start(f32[8,1024]{1,0:T(8,128)S(1)} %cross_squares.1), channel_id=1, source_target_pairs={{0,2},{1,3},{2,0},{3,1},{4,6},{5,7},{6,4},{7,5},{8,10},{9,11},{10,... | collective-permute-start | bytes 98312 | tf_op jit(solution)/shard_map/ppermute | solution.py:33
  56.8 1.5 %collective-permute-start.3 = (f32[8,1024]{1,0:T(8,128)S(1)}, f32[8,1024]{1,0:T(8,128)S(1)}, u32[]{:S(2)}, u32[]{:S(2)}) collective-permute-start(f32[8,1024]{1,0:T(8,128)S(1)} %cross_squares.1), channel_id=1, source_target_pairs={{0,1},{1,0},{2,3},{3,2},{4,5},{5,4},{6,7},{7,6},{8,9},{9,8},{10,11... | collective-permute-start | bytes 98312 | tf_op jit(solution)/shard_map/ppermute | solution.py:33
  58.3 6.9 %near_pairs.1 = (bf16[4,128,1024]{2,1,0:T(8,128)(2,1)S(1)}, bf16[4,128,1024]{2,1,0:T(8,128)(2,1)S(1)}, bf16[2,4,128,1024]{3,2,1,0:T(8,128)(2,1)S(1)}, f32[3,128,1024]{2,1,0:T(8,128)S(1)}, f32[4,128,1024]{2,1,0:T(8,128)S(1)}) custom-call(s32[8]{0:T(128)S(1)} %copy-done, s32[32]{0:T(128)S(1)} %get-tuple-element.67.reach, ...), custom_call_target="tpu_custom_call" | custom-call | flops 3000000000 | bytes 8388608 | tf_op jit(solution)/shard_map/near_pairs/pallas_call | solution.py:473
  65.3 2.0 %collective-permute-start.9 = (f32[8,1024]{1,0:T(8,128)S(1)}, f32[8,1024]{1,0:T(8,128)S(1)}, u32[]{:S(2)}, u32[]{:S(2)}) collective-permute-start(f32[8,1024]{1,0:T(8,128)S(1)} %add_add_fusion.2), channel_id=1, source_target_pairs={{0,96},{4,100},{8,104},{12,108},{16,112},{20,116},{24,120},{28,124... | collective-permute-start | bytes 98312 | tf_op jit(solution)/shard_map/ppermute | solution.py:33
  67.3 1.4 %collective-permute-start.8 = (f32[8,1024]{1,0:T(8,128)S(1)}, f32[8,1024]{1,0:T(8,128)S(1)}, u32[]{:S(2)}, u32[]{:S(2)}) collective-permute-start(f32[8,1024]{1,0:T(8,128)S(1)} %add_add_fusion.2), channel_id=1, source_target_pairs={{0,64},{4,68},{8,72},{12,76},{16,80},{20,84},{24,88},{28,92},{32,9... | collective-permute-start | bytes 98312 | tf_op jit(solution)/shard_map/ppermute | solution.py:33
  68.7 1.4 %collective-permute-start.7 = (f32[8,1024]{1,0:T(8,128)S(1)}, f32[8,1024]{1,0:T(8,128)S(1)}, u32[]{:S(2)}, u32[]{:S(2)}) collective-permute-start(f32[8,1024]{1,0:T(8,128)S(1)} %add_add_fusion.2), channel_id=1, source_target_pairs={{0,32},{4,36},{8,40},{12,44},{16,48},{20,52},{24,56},{28,60},{32,0... | collective-permute-start | bytes 98312 | tf_op jit(solution)/shard_map/ppermute | solution.py:33
  70.1 4.8 %collective-permute-done.9 = f32[8,1024]{1,0:T(8,128)S(1)} collective-permute-done((f32[8,1024]{1,0:T(8,128)S(1)}, f32[8,1024]{1,0:T(8,128)S(1)}, u32[]{:S(2)}, u32[]{:S(2)}) %collective-permute-start.9) | collective-permute-done | bytes 32800 | tf_op jit(solution)/shard_map/ppermute | solution.py:33
  74.9 1.3 %collective-permute-done.8 = f32[8,1024]{1,0:T(8,128)S(1)} collective-permute-done((f32[8,1024]{1,0:T(8,128)S(1)}, f32[8,1024]{1,0:T(8,128)S(1)}, u32[]{:S(2)}, u32[]{:S(2)}) %collective-permute-start.8) | collective-permute-done | bytes 32800 | tf_op jit(solution)/shard_map/ppermute | solution.py:33
  76.3 4.0 %far_pairs.1 = (bf16[4,128,1024]{2,1,0:T(8,128)(2,1)S(1)}, bf16[4,128,1024]{2,1,0:T(8,128)(2,1)S(1)}, bf16[2,4,128,1024]{3,2,1,0:T(8,128)(2,1)S(1)}) custom-call(s32[8]{0:T(128)S(1)} %copy-done, s32[32]{0:T(128)S(1)} %get-tuple-element.67.reach, ...), custom_call_target="tpu_custom_call", output_to_operand_aliasing={{0}: (12, {}), {1}: (13, {}), {2}: (14, {})} | custom-call | flops 800000000 | bytes 4194304 | tf_op jit(solution)/shard_map/far_pairs/pallas_call | solution.py:537
  80.5 1.0 collective-permute-start.15
  81.4 3.2 %collective-permute-start.13 = (f32[8,1024]{1,0:T(8,128)S(1)}, f32[8,1024]{1,0:T(8,128)S(1)}, u32[]{:S(2)}, u32[]{:S(2)}) collective-permute-start(f32[8,1024]{1,0:T(8,128)S(1)} %add_add_fusion.1), channel_id=1, source_target_pairs={{0,8},{4,12},{8,0},{12,4},{16,24},{20,28},{24,16},{28,20},{32,40},... | collective-permute-start | bytes 98312 | tf_op jit(solution)/shard_map/ppermute | solution.py:33
  84.6 1.9 %place_mine.1 = (bf16[4,128,2048]{2,1,0:T(8,128)(2,1)}, bf16[4,128,2048]{2,1,0:T(8,128)(2,1)}) custom-call(s32[8]{0:T(128)S(1)} %copy-done, bf16[4,128,1024]{2,1,0:T(8,128)(2,1)S(1)} %get-tuple-element.122.gate, bf16[4,128,1024]{2,1,0:T(8,128)(2,1)S(1)} %get-tuple-element.123.inp), custom_call_target="tpu_custom_call" | custom-call | tf_op jit(solution)/shard_map/place_mine/pallas_call | solution.py:574
  86.9 3.3 %collective-permute-start.18 = (f32[8,1024]{1,0:T(8,128)S(1)}, f32[8,1024]{1,0:T(8,128)S(1)}, u32[]{:S(2)}, u32[]{:S(2)}) collective-permute-start(f32[8,1024]{1,0:T(8,128)S(1)} %add_add_fusion.sums), channel_id=1, source_target_pairs={{0,228},{4,224},{8,236},{12,232},{16,244},{20,240},{24,252},{28,24... | collective-permute-start | bytes 98312 | tf_op jit(solution)/shard_map/ppermute | solution.py:675
  90.2 1.5 %collective-permute-start.17 = (f32[8,1024]{1,0:T(8,128)S(1)}, f32[8,1024]{1,0:T(8,128)S(1)}, u32[]{:S(2)}, u32[]{:S(2)}) collective-permute-start(f32[8,1024]{1,0:T(8,128)S(1)} %add_add_fusion.sums), channel_id=1, source_target_pairs={{0,4},{4,0},{8,12},{12,8},{16,20},{20,16},{24,28},{28,24},{32,36},... | collective-permute-start | bytes 98312 | tf_op jit(solution)/shard_map/ppermute | solution.py:33
  92.1 1.4 %collective-permute-done.18.other_pair = f32[8,1024]{1,0:T(8,128)S(1)} collective-permute-done((f32[8,1024]{1,0:T(8,128)S(1)}, f32[8,1024]{1,0:T(8,128)S(1)}, u32[]{:S(2)}, u32[]{:S(2)}) %collective-permute-start.18) | collective-permute-done | bytes 32800 | tf_op jit(solution)/shard_map/ppermute | solution.py:675
  93.5 5.1 %collective-permute-done.16.pair = f32[8,1024]{1,0:T(8,128)S(1)} collective-permute-done((f32[8,1024]{1,0:T(8,128)S(1)}, f32[8,1024]{1,0:T(8,128)S(1)}, u32[]{:S(2)}, u32[]{:S(2)}) %collective-permute-start.16) | collective-permute-done | bytes 32800 | tf_op jit(solution)/shard_map/ppermute | solution.py:673
  98.7 2.5 %join.1 = (bf16[4,128,2048]{2,1,0:T(8,128)(2,1)}, bf16[4,128,2048]{2,1,0:T(8,128)(2,1)}, f32[16,1024]{1,0:T(8,128)}) custom-call(s32[8]{0:T(128)S(1)} %copy-done, bf16[2,4,128,1024]{3,2,1,0:T(8,128)(2,1)S(1)} %collective-permute-done.12.got, bf16[4,128,2048]{2,1,0:T(8,128)(2,1)} %get-tuple-element.126.gate_in, ...), custom_call_target="tpu_custom_call", output_to_operand_aliasing={{0}: (2, {}), {1}: (3, {})} | custom-call | tf_op jit(solution)/shard_map/join/pallas_call | solution.py:596
  (28 shorter events, 1.1 us)
Async XLA Ops:
  0.6 4.3 %copy-start.1 = (s32[192,8]{0,1:T(8,128)S(1)}, s32[192,8]{0,1:T(8,128)}, u32[]{:S(2)}) copy-start(s32[192,8]{0,1:T(8,128)} %param.11) | copy-start | bytes 18436
  4.8 4.7 %collective-permute-start = (bf16[2,4,128,1024]{3,2,1,0:T(8,128)(2,1)}, bf16[2,4,128,1024]{3,2,1,0:T(8,128)(2,1)S(1)}, u32[]{:S(2)}, u32[]{:S(2)}) collective-permute-start(bf16[2,4,128,1024]{3,2,1,0:T(8,128)(2,1)} %get-tuple-element.70), channel_id=1, source_target_pairs={{0,4},{4,0},{8,12},{12,8},{16,20},{20,16},{24,28},{28,24},{32,36},... | collective-permute-start | bytes 6291464 | tf_op jit(solution)/shard_map/ppermute | solution.py:33
  4.9 0.7 copy-start
  9.5 8.9 %copy-start.3 = (bf16[4,128,1024]{2,1,0:T(8,128)(2,1)S(1)}, bf16[4,128,1024]{2,1,0:T(8,128)(2,1)}, u32[]{:S(2)}) copy-start(bf16[4,128,1024]{2,1,0:T(8,128)(2,1)} %get-tuple-element.101) | copy-start | bytes 3145732
  9.5 9.0 %copy-start.2 = (f32[16,1024]{1,0:T(8,128)S(1)}, f32[16,1024]{1,0:T(8,128)}, u32[]{:S(2)}) copy-start(f32[16,1024]{1,0:T(8,128)} %filt.3) | copy-start | bytes 196612
  10.4 29.6 %collective-permute-start.1 = (bf16[4,128,1024]{2,1,0:T(8,128)(2,1)S(1)}, bf16[4,128,1024]{2,1,0:T(8,128)(2,1)S(1)}, u32[]{:S(2)}, u32[]{:S(2)}) collective-permute-start(bf16[4,128,1024]{2,1,0:T(8,128)(2,1)S(1)} %get-tuple-element.71), channel_id=1, source_target_pairs={{0,8},{4,12},{8,16},{12,20},{16,24},{20,28},{24,32},{28,36},{32,40... | collective-permute-start | bytes 3145736 | tf_op jit(solution)/shard_map/ppermute | solution.py:28
  13.9 21.6 %collective-permute-start.2 = (bf16[3,128,1024]{2,1,0:T(8,128)(2,1)S(1)}, bf16[3,128,1024]{2,1,0:T(8,128)(2,1)S(1)}, u32[]{:S(2)}, u32[]{:S(2)}) collective-permute-start(bf16[3,128,1024]{2,1,0:T(8,128)(2,1)S(1)} %get-tuple-element.72), channel_id=1, source_target_pairs={{8,0},{12,4},{16,8},{20,12},{24,16},{28,20},{32,24},{36,28},{40,32... | collective-permute-start | bytes 2359304 | tf_op jit(solution)/shard_map/ppermute | solution.py:28
  18.4 38.4 %collective-permute-start.6 = (bf16[4,128,1024]{2,1,0:T(8,128)(2,1)S(1)}, bf16[4,128,1024]{2,1,0:T(8,128)(2,1)S(1)}, u32[]{:S(2)}, u32[]{:S(2)}) collective-permute-start(bf16[4,128,1024]{2,1,0:T(8,128)(2,1)S(1)} %copy-done.3), channel_id=1, source_target_pairs={{0,4},{4,0},{8,12},{12,8},{16,20},{20,16},{24,28},{28,24},{32,36},... | collective-permute-start | bytes 3145736 | tf_op jit(solution)/shard_map/ppermute | solution.py:33
  40.9 35.4 %collective-permute-start.10 = (bf16[3,128,1024]{2,1,0:T(8,128)(2,1)S(1)}, bf16[3,128,1024]{2,1,0:T(8,128)(2,1)S(1)}, u32[]{:S(2)}, u32[]{:S(2)}) collective-permute-start(bf16[3,128,1024]{2,1,0:T(8,128)(2,1)S(1)} %get-tuple-element.111), channel_id=1, source_target_pairs={{0,8},{4,12},{8,16},{12,20},{16,24},{20,28},{24,32},{28,36},{32,40... | collective-permute-start | bytes 2359304 | tf_op jit(solution)/shard_map/ppermute | solution.py:28
  42.8 33.5 %collective-permute-start.11 = (bf16[4,128,1024]{2,1,0:T(8,128)(2,1)S(1)}, bf16[4,128,1024]{2,1,0:T(8,128)(2,1)S(1)}, u32[]{:S(2)}, u32[]{:S(2)}) collective-permute-start(bf16[4,128,1024]{2,1,0:T(8,128)(2,1)S(1)} %get-tuple-element.112), channel_id=1, source_target_pairs={{8,0},{12,4},{16,8},{20,12},{24,16},{28,20},{32,24},{36,28},{40,32... | collective-permute-start | bytes 3145736 | tf_op jit(solution)/shard_map/ppermute | solution.py:28
  53.9 11.3 %collective-permute-start.5 = (f32[8,1024]{1,0:T(8,128)S(1)}, f32[8,1024]{1,0:T(8,128)S(1)}, u32[]{:S(2)}, u32[]{:S(2)}) collective-permute-start(f32[8,1024]{1,0:T(8,128)S(1)} %cross_squares.1), channel_id=1, source_target_pairs={{0,3},{1,2},{2,1},{3,0},{4,7},{5,6},{6,5},{7,4},{8,11},{9,10},{10,... | collective-permute-start | bytes 98312 | tf_op jit(solution)/shard_map/ppermute | solution.py:33
  55.7 9.6 %collective-permute-start.4 = (f32[8,1024]{1,0:T(8,128)S(1)}, f32[8,1024]{1,0:T(8,128)S(1)}, u32[]{:S(2)}, u32[]{:S(2)}) collective-permute-start(f32[8,1024]{1,0:T(8,128)S(1)} %cross_squares.1), channel_id=1, source_target_pairs={{0,2},{1,3},{2,0},{3,1},{4,6},{5,7},{6,4},{7,5},{8,10},{9,11},{10,... | collective-permute-start | bytes 98312 | tf_op jit(solution)/shard_map/ppermute | solution.py:33
  56.8 8.5 %collective-permute-start.3 = (f32[8,1024]{1,0:T(8,128)S(1)}, f32[8,1024]{1,0:T(8,128)S(1)}, u32[]{:S(2)}, u32[]{:S(2)}) collective-permute-start(f32[8,1024]{1,0:T(8,128)S(1)} %cross_squares.1), channel_id=1, source_target_pairs={{0,1},{1,0},{2,3},{3,2},{4,5},{5,4},{6,7},{7,6},{8,9},{9,8},{10,11... | collective-permute-start | bytes 98312 | tf_op jit(solution)/shard_map/ppermute | solution.py:33
  65.3 9.7 %collective-permute-start.9 = (f32[8,1024]{1,0:T(8,128)S(1)}, f32[8,1024]{1,0:T(8,128)S(1)}, u32[]{:S(2)}, u32[]{:S(2)}) collective-permute-start(f32[8,1024]{1,0:T(8,128)S(1)} %add_add_fusion.2), channel_id=1, source_target_pairs={{0,96},{4,100},{8,104},{12,108},{16,112},{20,116},{24,120},{28,124... | collective-permute-start | bytes 98312 | tf_op jit(solution)/shard_map/ppermute | solution.py:33
  67.3 9.0 %collective-permute-start.8 = (f32[8,1024]{1,0:T(8,128)S(1)}, f32[8,1024]{1,0:T(8,128)S(1)}, u32[]{:S(2)}, u32[]{:S(2)}) collective-permute-start(f32[8,1024]{1,0:T(8,128)S(1)} %add_add_fusion.2), channel_id=1, source_target_pairs={{0,64},{4,68},{8,72},{12,76},{16,80},{20,84},{24,88},{28,92},{32,9... | collective-permute-start | bytes 98312 | tf_op jit(solution)/shard_map/ppermute | solution.py:33
  68.7 7.6 %collective-permute-start.7 = (f32[8,1024]{1,0:T(8,128)S(1)}, f32[8,1024]{1,0:T(8,128)S(1)}, u32[]{:S(2)}, u32[]{:S(2)}) collective-permute-start(f32[8,1024]{1,0:T(8,128)S(1)} %add_add_fusion.2), channel_id=1, source_target_pairs={{0,32},{4,36},{8,40},{12,44},{16,48},{20,52},{24,56},{28,60},{32,0... | collective-permute-start | bytes 98312 | tf_op jit(solution)/shard_map/ppermute | solution.py:33
  80.4 18.3 %collective-permute-start.12 = (bf16[2,4,128,1024]{3,2,1,0:T(8,128)(2,1)S(1)}, bf16[2,4,128,1024]{3,2,1,0:T(8,128)(2,1)S(1)}, u32[]{:S(2)}, u32[]{:S(2)}) collective-permute-start(bf16[2,4,128,1024]{3,2,1,0:T(8,128)(2,1)S(1)} %get-tuple-element.119), channel_id=1, source_target_pairs={{0,4},{4,0},{8,12},{12,8},{16,20},{20,16},{24,28},{28,24},{32,36},... | collective-permute-start | bytes 6291464 | tf_op jit(solution)/shard_map/ppermute | solution.py:33
  80.5 6.1 %collective-permute-start.15 = (f32[8,1024]{1,0:T(8,128)S(1)}, f32[8,1024]{1,0:T(8,128)S(1)}, u32[]{:S(2)}, u32[]{:S(2)}) collective-permute-start(f32[8,1024]{1,0:T(8,128)S(1)} %add_add_fusion.1), channel_id=1, source_target_pairs={{0,24},{4,28},{8,16},{12,20},{16,8},{20,12},{24,0},{28,4},{32,56},... | collective-permute-start | bytes 98312 | tf_op jit(solution)/shard_map/ppermute | solution.py:33
  81.4 5.4 %collective-permute-start.14 = (f32[8,1024]{1,0:T(8,128)S(1)}, f32[8,1024]{1,0:T(8,128)S(1)}, u32[]{:S(2)}, u32[]{:S(2)}) collective-permute-start(f32[8,1024]{1,0:T(8,128)S(1)} %add_add_fusion.1), channel_id=1, source_target_pairs={{0,16},{4,20},{8,24},{12,28},{16,0},{20,4},{24,8},{28,12},{32,48},... | collective-permute-start | bytes 98312 | tf_op jit(solution)/shard_map/ppermute | solution.py:33
  81.4 5.4 %collective-permute-start.13 = (f32[8,1024]{1,0:T(8,128)S(1)}, f32[8,1024]{1,0:T(8,128)S(1)}, u32[]{:S(2)}, u32[]{:S(2)}) collective-permute-start(f32[8,1024]{1,0:T(8,128)S(1)} %add_add_fusion.1), channel_id=1, source_target_pairs={{0,8},{4,12},{8,0},{12,4},{16,24},{20,28},{24,16},{28,20},{32,40},... | collective-permute-start | bytes 98312 | tf_op jit(solution)/shard_map/ppermute | solution.py:33
  86.9 6.6 %collective-permute-start.18 = (f32[8,1024]{1,0:T(8,128)S(1)}, f32[8,1024]{1,0:T(8,128)S(1)}, u32[]{:S(2)}, u32[]{:S(2)}) collective-permute-start(f32[8,1024]{1,0:T(8,128)S(1)} %add_add_fusion.sums), channel_id=1, source_target_pairs={{0,228},{4,224},{8,236},{12,232},{16,244},{20,240},{24,252},{28,24... | collective-permute-start | bytes 98312 | tf_op jit(solution)/shard_map/ppermute | solution.py:675
  90.2 3.3 %collective-permute-start.17 = (f32[8,1024]{1,0:T(8,128)S(1)}, f32[8,1024]{1,0:T(8,128)S(1)}, u32[]{:S(2)}, u32[]{:S(2)}) collective-permute-start(f32[8,1024]{1,0:T(8,128)S(1)} %add_add_fusion.sums), channel_id=1, source_target_pairs={{0,4},{4,0},{8,12},{12,8},{16,20},{20,16},{24,28},{28,24},{32,36},... | collective-permute-start | bytes 98312 | tf_op jit(solution)/shard_map/ppermute | solution.py:33
  91.7 6.9 %collective-permute-start.16 = (f32[8,1024]{1,0:T(8,128)S(1)}, f32[8,1024]{1,0:T(8,128)S(1)}, u32[]{:S(2)}, u32[]{:S(2)}) collective-permute-start(f32[8,1024]{1,0:T(8,128)S(1)} %add_add_fusion.sums), channel_id=1, source_target_pairs={{0,224},{4,228},{8,232},{12,236},{16,240},{20,244},{24,248},{28,25... | collective-permute-start | bytes 98312 | tf_op jit(solution)/shard_map/ppermute | solution.py:673
